TPU v7x, 32 devices: a whole 2x2x4 slice. The times are simulated.
32 devices in a mesh: groups: 2 (over x), row: 16 (over z, y, core).
Axes of the slice: x: 2, y: 2, z: 4, core: 2. Of those that a mesh axis runs over, the one named last changes fastest.
Arguments:
- queries: bfloat16 [32, 5, 64, 768], P(('groups', 'row')), parts along dimension 0, may hold values from -20 to 20
- keys: bfloat16 [32, 5, 64, 768], P(('groups', 'row')), parts along dimension 0, may hold values from -20 to 20
- values: bfloat16 [32, 5, 64, 768], P(('groups', 'row')), parts along dimension 0, may hold values from -6 to 6
- outputs: bfloat16 [32, 5, 64, 768], P(('groups', 'row')), parts along dimension 0, may hold values from -6 to 6
- grad_out: bfloat16 [32, 5, 64, 1536], P(('groups', 'row')), parts along dimension 0, may hold values from -6 to 6
- w_out: bfloat16 [768, 1536], replicated, may hold values from -0.21875 to 0.21875
- bounds: int32 [32, 2], P('groups'), parts along dimension 0, may hold values from 0 to 15, as said below
Outputs:
- grad_queries: bfloat16 [32, 5, 64, 768], P(('groups', 'row')), parts along dimension 0
- grad_keys: bfloat16 [32, 5, 64, 768], P(('groups', 'row')), parts along dimension 0
- grad_values: bfloat16 [32, 5, 64, 768], P(('groups', 'row')), parts along dimension 0
- grad_w_out: float32 [1536, 1536], P(('groups', 'row')), parts along dimension 0
There are 2 independent parts, one for each index of `groups`. A program takes and returns all parts, laid end to end along the dimension named above; an argument that names none is the same for every part. Nothing has to cross between parts.
Inputs may be any that keep to these rules, and one draw needn't show every extreme that they name: Images are packed one below another on the canvas, each covering whole tile rows; bounds[r, 0] <= r <= bounds[r, 1], and all tile rows of one image carry the same pair.
All inputs are finite; a program needn't handle non-finite values.
Results may differ from a plain program's by a relative error of at most 0.0058.
Values may be sent and summed in bfloat16 or wider, within the bound.
No kernel may reach another device: no remote copies, remote signals or barrier semaphores. Data moves between devices by JAX's collectives and lax.ppermute only.
A program may use at most 192 MiB of HBM per device.

v0:
```python
import math

import jax
import jax.numpy as jnp
from jax import lax
from jax.sharding import PartitionSpec as P

HEAD = 64
REACH = 3


SCALE = 0.125
NEGATIVE = -1e30


def from_behind(value, axis, steps):
    count = lax.axis_size(axis)
    initial, last = (max(0, -steps), min(count, count - steps))
    return lax.ppermute(value, axis, [(source, source + steps) for source in range(initial, last)])


def window_mask(centre, bounds, col_count, tile_len):
    window_rows = 2 * REACH + 1
    window_idx = jnp.arange(window_rows * col_count * tile_len, dtype=jnp.int32)
    other_row = centre - REACH + window_idx // (col_count * tile_len)
    other_col = window_idx // tile_len % col_count
    own_col = jnp.arange(col_count * tile_len, dtype=jnp.int32) // tile_len
    limits = lax.dynamic_index_in_dim(bounds, centre, 0, keepdims=False)
    row_ok = (other_row >= limits[0]) & (other_row <= limits[1])
    col_ok = jnp.abs(own_col[:, None] - other_col[None, :]) <= REACH
    return row_ok[None, :] & col_ok


def widen_rows(stacked, row_axis, hop_count, sender):
    pieces = []
    for distance in range(hop_count, 0, -1):
        pieces.append(sender(stacked, distance))
    pieces.append(stacked)
    for distance in range(1, hop_count + 1):
        pieces.append(sender(stacked, -distance))
    joined = jnp.concatenate(pieces, axis=row_axis)
    return joined


def query_row(query_here, grad_here, dot_here, key_win, value_win, allowed):
    count_here = query_here.shape[0]
    query_heads = query_here.reshape(count_here, -1, HEAD)
    grad_heads = grad_here.reshape(count_here, -1, HEAD)
    key_heads = key_win.reshape(key_win.shape[0], -1, HEAD)
    value_heads = value_win.reshape(value_win.shape[0], -1, HEAD)
    scores = SCALE * jnp.einsum(
        "qhe,khe->hqk", query_heads, key_heads, preferred_element_type=jnp.float32
    )
    scores = jnp.where(allowed[None], scores, NEGATIVE)
    row_peak = jnp.max(scores, axis=2, keepdims=True)
    log_total = row_peak + jnp.log(jnp.sum(jnp.exp(scores - row_peak), axis=2, keepdims=True))
    softmax_out = jnp.exp(scores - log_total)
    grad_probs = jnp.einsum(
        "qhe,khe->hqk", grad_heads, value_heads, preferred_element_type=jnp.float32
    )
    grad_scores = (softmax_out * (grad_probs - jnp.transpose(dot_here)[:, :, None])).astype(
        jnp.bfloat16
    )
    grad_q = SCALE * jnp.einsum(
        "hqk,khe->qhe", grad_scores, key_heads, preferred_element_type=jnp.float32
    )
    grad_q = grad_q.reshape(count_here, -1).astype(jnp.bfloat16)
    return (
        grad_q,
        softmax_out.astype(jnp.bfloat16),
        grad_scores,
        jnp.transpose(log_total[:, :, 0]),
    )


def body(queries, keys, values, outputs, grad_out, w_out, bounds):
    own_rows, own_cols, tile_len, feature_count = queries.shape
    token_count = own_rows * own_cols * tile_len
    window_rows = 2 * REACH + 1
    hop_count = -(-REACH // own_rows)
    lead_rows = hop_count * own_rows
    head_total = feature_count // HEAD
    group_heads = math.gcd(head_total, 4)
    group_count = head_total // group_heads
    group_width = group_heads * HEAD
    row_start = lax.axis_index("row") * own_rows
    row_order = jnp.arange(own_rows, dtype=jnp.int32)
    flat_grad = grad_out.reshape(token_count, grad_out.shape[3])
    grad_attn = lax.dot_general(
        flat_grad, w_out, (((1,), (1,)), ((), ())), preferred_element_type=jnp.float32
    ).astype(jnp.bfloat16)
    grad_attn = grad_attn.reshape(own_rows, own_cols, tile_len, feature_count)
    widened = lax.optimization_barrier(grad_attn).astype(jnp.float32)
    grad_dot = jnp.sum(
        (widened * outputs.astype(jnp.float32)).reshape(
            own_rows, own_cols, tile_len, head_total, HEAD
        ),
        axis=4,
    )

    def send_keys(part, distance):
        return from_behind(part, "row", distance)

    key_rims = widen_rows(jnp.stack([keys, values]), 1, hop_count, send_keys)

    def feature_part(array, head_group):
        return array[..., head_group * group_width : (head_group + 1) * group_width]

    def head_part(array, head_group):
        return array[..., head_group * group_heads : (head_group + 1) * group_heads]

    def query_pass(head_group):
        rims_group = feature_part(key_rims, head_group)
        query_group = feature_part(queries, head_group)
        grad_group = feature_part(grad_attn, head_group)
        dot_group = head_part(grad_dot, head_group)

        def one_row(offset):
            allowed = window_mask(row_start + offset, bounds, own_cols, tile_len)
            query_here = lax.dynamic_index_in_dim(query_group, offset, 0, keepdims=False).reshape(
                -1, group_width
            )
            grad_here = lax.dynamic_index_in_dim(grad_group, offset, 0, keepdims=False).reshape(
                -1, group_width
            )
            dot_here = lax.dynamic_index_in_dim(dot_group, offset, 0, keepdims=False).reshape(
                -1, group_heads
            )
            results = query_row(
                query_here,
                grad_here,
                dot_here,
                rims_group[0].reshape(-1, group_width),
                rims_group[1].reshape(-1, group_width),
                allowed,
            )
            return (query_here, grad_here, results)

        return one_row

    grad_pieces = []
    total_pieces = []
    for head_group in range(group_count):
        one_row = query_pass(head_group)

        def add_row(offset):
            query_here, grad_here, results = one_row(offset)
            grad_q, weights, grad_scores, log_total = results
            query_heads = query_here.reshape(query_here.shape[0], -1, HEAD)
            grad_heads = grad_here.reshape(grad_here.shape[0], -1, HEAD)
            part_k = jnp.einsum(
                "hqk,qhe->khe", grad_scores, query_heads, preferred_element_type=jnp.float32
            )
            part_v = jnp.einsum(
                "hqk,qhe->khe", weights, grad_heads, preferred_element_type=jnp.float32
            )
            update = jnp.stack([part_k, part_v]).reshape(
                2, window_rows, own_cols, tile_len, group_width
            )
            return (grad_q, update)

        grad_q_rows, updates = lax.map(add_row, row_order)
        grad_pieces.append(grad_q_rows)
        group_totals = jnp.zeros(
            (2, (2 * hop_count + 1) * own_rows, own_cols, tile_len, group_width), jnp.float32
        )
        offset = 0
        first_row = lead_rows - REACH + offset
        group_totals = group_totals.at[:, first_row : first_row + window_rows].add(updates[offset])
        total_pieces.append(group_totals)
    totals = jnp.concatenate(total_pieces, axis=4)
    own_part = totals[:, lead_rows : lead_rows + own_rows]
    for distance in range(-hop_count, hop_count + 1):
        if distance != 0:
            first_row = lead_rows + distance * own_rows
            own_part = own_part + from_behind(
                totals[:, first_row : first_row + own_rows], "row", distance
            )
    grad_keys = (SCALE * own_part[0]).astype(jnp.bfloat16)
    grad_values = own_part[1].astype(jnp.bfloat16)
    grad_queries = jnp.concatenate(grad_pieces, axis=2).reshape(
        own_rows, own_cols, tile_len, feature_count
    )
    flat_outputs = outputs.reshape(token_count, feature_count)
    grad_w_out = lax.psum_scatter(
        lax.dot_general(
            flat_outputs, flat_grad, (((0,), (0,)), ((), ())), preferred_element_type=jnp.float32
        ),
        "row",
        scatter_dimension=0,
        tiled=True,
    )
    return (grad_queries, grad_keys, grad_values, grad_w_out)


def solution(mesh):
    placed = (
        P(("groups", "row"), None, None, None),
        P(("groups", "row"), None, None, None),
        P(("groups", "row"), None, None, None),
        P(("groups", "row"), None, None, None),
        P(("groups", "row"), None, None, None),
        P(),
        P("groups", None),
    )
    return jax.shard_map(
        body,
        mesh=mesh,
        in_specs=placed,
        out_specs=(
            P(("groups", "row"), None, None, None),
            P(("groups", "row"), None, None, None),
            P(("groups", "row"), None, None, None),
            P(("groups", "row"), None),
        ),
        check_vma=False,
    )
```

profile of v0, /device:TPU:0, one launch (start us, length us, event | category | flops | bytes accessed | tf_op | source)
XLA Modules:
  0.0 510.0 jit_solution(10956698632313746986)
XLA Ops:
  16.2 5.5 %collective-permute-start.1 = (bf16[2,1,5,64,768]{4,3,2,1,0:T(8,128)(2,1)}, bf16[2,1,5,64,768]{4,3,2,1,0:T(8,128)(2,1)}, u32[]{:S(2)}, u32[]{:S(2)}) collective-permute-start(bf16[2,1,5,64,768]{4,3,2,1,0:T(8,128)(2,1)} %pad_maximum_fusion.1), channel_id=1, source_target_pairs={{0,2},{1,3},{2,4},{3,5},{4,6},{5,7},{6,8},{7,9},{8,10},{9,11},{10,... | collective-permute-start | bytes 2949128 | tf_op jit(solution)/shard_map/ppermute | solution.py:19
  21.7 5.1 collective-permute-start
  26.7 4.9 convolution_bitcast_fusion.3
  48.9 63.6 %collective-permute-done = bf16[2,1,5,64,768]{4,3,2,1,0:T(8,128)(2,1)} collective-permute-done((bf16[2,1,5,64,768]{4,3,2,1,0:T(8,128)(2,1)}, bf16[2,1,5,64,768]{4,3,2,1,0:T(8,128)(2,1)}, u32[]{:S(2)}, u32[]{:S(2)}) %collective-permute-start) | collective-permute-done | bytes 983072 | tf_op jit(solution)/shard_map/ppermute | solution.py:19
  123.3 5.9 %collective-permute-done.5 = bf16[2,1,5,64,768]{4,3,2,1,0:T(8,128)(2,1)S(1)} collective-permute-done((bf16[2,1,5,64,768]{4,3,2,1,0:T(8,128)(2,1)}, bf16[2,1,5,64,768]{4,3,2,1,0:T(8,128)(2,1)S(1)}, u32[]{:S(2)}, u32[]{:S(2)}) %collective-permute-start.5) | collective-permute-done | bytes 983072 | tf_op jit(solution)/shard_map/ppermute | solution.py:19
  132.0 4.9 squeeze.82
  176.0 6.7 %multiply_convert_fusion.2 = bf16[4,320,2240]{2,1,0:T(8,128)(2,1)} fusion(f32[4,320,2240]{2,1,0:T(8,128)S(1)} %get-tuple-element.173, bf16[320,4,64]{0,2,1:T(8,128)(2,1)} %copy.64, f32[4,320]{1,0:T(4,128)S(1)} %bitcast.121, f32[4,320]{1,0:T(4,128)S(1)} %log_add_fusion.2, bf16[2240,4,64]{2,1,0:T(4,128)(2,1)S(1)} %copy-done.5), kind=kOutput, calls=%fused_computation.10 | convolution fusion | flops 378470400 | bytes 18524160 | tf_op jit(solution)/shard_map/while/body/eval_jaxpr/qhe,khe->hqk/dot_general | solution.py:58
  182.8 5.4 %convolution_bitcast_fusion.2 = f32[2240,4,64]{0,2,1:T(8,128)} fusion(bf16[320,4,64]{0,2,1:T(8,128)(2,1)} %copy.63, bf16[4,320,2240]{2,1,0:T(8,128)(2,1)} %multiply_convert_fusion.2), kind=kOutput, calls=%fused_computation.30 | convolution fusion | flops 367001600 | bytes 8192000 | tf_op jit(solution)/shard_map/while/body/eval_jaxpr/hqk,qhe->khe/dot_general | solution.py:151
  188.2 5.6 %copy.84 = f32[2240,4,64]{2,1,0:T(4,128)} copy(f32[2240,4,64]{0,2,1:T(8,128)} %convolution_bitcast_fusion.2) | data formatting | bytes 4587520 | tf_op jit(solution)/shard_map/while/body/eval_jaxpr/hqk,qhe->khe/transpose | solution.py:151
  193.7 5.4 %stack.48 = f32[1,1,7,5,64,256]{5,4,3,2,1,0:T(8,128)} reshape(f32[2240,4,64]{2,1,0:T(4,128)} %copy.84) | data formatting | bytes 4587520 | tf_op jit(solution)/shard_map/while/body/eval_jaxpr/stack | solution.py:157
  199.1 5.4 %copy.86 = f32[2240,4,64]{2,1,0:T(4,128)} copy(f32[2240,4,64]{0,2,1:T(8,128)} %fusion.12) | data formatting | bytes 4587520 | tf_op jit(solution)/shard_map/while/body/eval_jaxpr/hqk,qhe->khe/transpose | solution.py:154
  204.5 5.4 %stack.49 = f32[1,1,7,5,64,256]{5,4,3,2,1,0:T(8,128)} reshape(f32[2240,4,64]{2,1,0:T(4,128)} %copy.86) | data formatting | bytes 4587520 | tf_op jit(solution)/shard_map/while/body/eval_jaxpr/stack | solution.py:157
  218.3 5.3 %multiply_convert_fusion.1 = bf16[4,320,2240]{2,1,0:T(8,128)(2,1)} fusion(f32[4,320,2240]{2,1,0:T(8,128)S(1)} %get-tuple-element.171, bf16[320,4,64]{0,2,1:T(8,128)(2,1)S(1)} %copy.71, f32[4,320]{1,0:T(4,128)S(1)} %bitcast.120, f32[4,320]{1,0:T(4,128)S(1)} %log_add_fusion.1, bf16[2240,4,64]{2,1,0:T(4,128)(2,1)S(1)} %copy-done.4), kind=kOutput, calls=%fused_computation.7 | convolution fusion | flops 378470400 | bytes 18524160 | tf_op jit(solution)/shard_map/while/body/eval_jaxpr/qhe,khe->hqk/dot_general | solution.py:58
  223.7 5.5 %convolution_bitcast_fusion.1 = f32[2240,4,64]{0,2,1:T(8,128)} fusion(bf16[320,4,64]{0,2,1:T(8,128)(2,1)} %copy.70, bf16[4,320,2240]{2,1,0:T(8,128)(2,1)} %multiply_convert_fusion.1), kind=kOutput, calls=%fused_computation.29 | convolution fusion | flops 367001600 | bytes 8192000 | tf_op jit(solution)/shard_map/while/body/eval_jaxpr/hqk,qhe->khe/dot_general | solution.py:151
  229.1 5.4 %copy.88 = f32[2240,4,64]{2,1,0:T(4,128)} copy(f32[2240,4,64]{0,2,1:T(8,128)} %convolution_bitcast_fusion.1) | data formatting | bytes 4587520 | tf_op jit(solution)/shard_map/while/body/eval_jaxpr/hqk,qhe->khe/transpose | solution.py:151
  234.6 5.3 %stack.51 = f32[1,1,7,5,64,256]{5,4,3,2,1,0:T(8,128)} reshape(f32[2240,4,64]{2,1,0:T(4,128)} %copy.88) | data formatting | bytes 4587520 | tf_op jit(solution)/shard_map/while/body/eval_jaxpr/stack | solution.py:157
  239.9 5.4 %copy.90 = f32[2240,4,64]{2,1,0:T(4,128)} copy(f32[2240,4,64]{0,2,1:T(8,128)} %fusion.15) | data formatting | bytes 4587520 | tf_op jit(solution)/shard_map/while/body/eval_jaxpr/hqk,qhe->khe/transpose | solution.py:154
  245.3 5.6 %stack.52 = f32[1,1,7,5,64,256]{5,4,3,2,1,0:T(8,128)} reshape(f32[2240,4,64]{2,1,0:T(4,128)} %copy.90) | data formatting | bytes 4587520 | tf_op jit(solution)/shard_map/while/body/eval_jaxpr/stack | solution.py:157
  258.5 5.3 %multiply_convert_fusion = bf16[4,320,2240]{2,1,0:T(8,128)(2,1)} fusion(f32[4,320,2240]{2,1,0:T(8,128)S(1)} %get-tuple-element.169, bf16[320,4,64]{0,2,1:T(8,128)(2,1)S(1)} %copy.78, f32[4,320]{1,0:T(4,128)S(1)} %bitcast.119, f32[4,320]{1,0:T(4,128)S(1)} %log_add_fusion, bf16[2240,4,64]{2,1,0:T(4,128)(2,1)S(1)} %copy-done.3), kind=kOutput, calls=%fused_computation.4 | convolution fusion | flops 378470400 | bytes 18524160 | tf_op jit(solution)/shard_map/while/body/eval_jaxpr/qhe,khe->hqk/dot_general | solution.py:58
  263.8 5.4 %convolution_bitcast_fusion = f32[2240,4,64]{0,2,1:T(8,128)} fusion(bf16[320,4,64]{0,2,1:T(8,128)(2,1)S(1)} %copy-done.10, bf16[4,320,2240]{2,1,0:T(8,128)(2,1)} %multiply_convert_fusion), kind=kOutput, calls=%fused_computation.28 | convolution fusion | flops 367001600 | bytes 8192000 | tf_op jit(solution)/shard_map/while/body/eval_jaxpr/hqk,qhe->khe/dot_general | solution.py:151
  269.2 5.4 %copy.92 = f32[2240,4,64]{2,1,0:T(4,128)} copy(f32[2240,4,64]{0,2,1:T(8,128)} %convolution_bitcast_fusion) | data formatting | bytes 4587520 | tf_op jit(solution)/shard_map/while/body/eval_jaxpr/hqk,qhe->khe/transpose | solution.py:151
  274.6 5.4 %stack.54 = f32[1,1,7,5,64,256]{5,4,3,2,1,0:T(8,128)} reshape(f32[2240,4,64]{2,1,0:T(4,128)} %copy.92) | data formatting | bytes 4587520 | tf_op jit(solution)/shard_map/while/body/eval_jaxpr/stack | solution.py:157
  280.1 5.4 %copy.94 = f32[2240,4,64]{2,1,0:T(4,128)} copy(f32[2240,4,64]{0,2,1:T(8,128)} %fusion.18) | data formatting | bytes 4587520 | tf_op jit(solution)/shard_map/while/body/eval_jaxpr/hqk,qhe->khe/transpose | solution.py:154
  285.5 5.6 %stack.55 = f32[1,1,7,5,64,256]{5,4,3,2,1,0:T(8,128)} reshape(f32[2240,4,64]{2,1,0:T(4,128)} %copy.94) | data formatting | bytes 4587520 | tf_op jit(solution)/shard_map/while/body/eval_jaxpr/stack | solution.py:157
  291.1 5.1 %maximum_bitcast_fusion.2 = f32[2,7,5,64,256]{4,3,2,1,0:T(8,128)} fusion(f32[1,1,7,5,64,256]{5,4,3,2,1,0:T(8,128)} %stack.55, f32[1,1,7,5,64,256]{5,4,3,2,1,0:T(8,128)} %stack.54), kind=kLoop, calls=%fused_computation.24 | loop fusion | flops 1146880 | bytes 9175040 | tf_op jit(solution)/shard_map/add | solution.py:169
  300.5 7.9 %pad_maximum_fusion = f32[2,7,5,64,768]{4,3,2,1,0:T(8,128)} fusion(f32[2,7,5,64,256]{4,3,2,1,0:T(8,128)} %maximum_bitcast_fusion.2, f32[2,7,5,64,256]{4,3,2,1,0:T(8,128)S(1)} %get-tuple-element.175, f32[2,7,5,64,256]{4,3,2,1,0:T(8,128)S(1)} %get-tuple-element.174), kind=kLoop, calls=%fused_computation | loop fusion | flops 6881280 | bytes 27525120 | tf_op jit(solution)/shard_map/concatenate | solution.py:171
  308.4 8.9 %fusion.54 = (f32[2,1,5,64,768]{4,3,2,1,0:T(8,128)}, f32[2,1,5,64,768]{4,3,2,1,0:T(8,128)}, f32[2,1,5,64,768]{4,3,2,1,0:T(8,128)}, f32[2,1,5,64,768]{4,3,2,1,0:T...) fusion(f32[2,7,5,64,768]{4,3,2,1,0:T(8,128)} %pad_maximum_fusion), kind=kLoop, calls=%fused_computation.100 | loop fusion | bytes 23592960 | tf_op jit(solution)/shard_map/slice | solution.py:177
  318.6 11.1 %collective-permute-start.11 = (f32[2,1,5,64,768]{4,3,2,1,0:T(8,128)}, f32[2,1,5,64,768]{4,3,2,1,0:T(8,128)}, u32[]{:S(2)}, u32[]{:S(2)}) collective-permute-start(f32[2,1,5,64,768]{4,3,2,1,0:T(8,128)} %get-tuple-element.146), channel_id=1, source_target_pairs={{0,3},{1,4},{2,5},{3,6},{4,7},{5,8},{6,9},{7,10},{8,11},{9,12},{10... | collective-permute-start | bytes 5898248 | tf_op jit(solution)/shard_map/ppermute | solution.py:19
  338.2 18.9 %collective-permute-done.6 = f32[2,1,5,64,768]{4,3,2,1,0:T(8,128)} collective-permute-done((f32[2,1,5,64,768]{4,3,2,1,0:T(8,128)}, f32[2,1,5,64,768]{4,3,2,1,0:T(8,128)}, u32[]{:S(2)}, u32[]{:S(2)}) %collective-permute-start.6) | collective-permute-done | bytes 1966112 | tf_op jit(solution)/shard_map/ppermute | solution.py:19
  371.1 60.6 %collective-permute-done.11 = f32[2,1,5,64,768]{4,3,2,1,0:T(8,128)} collective-permute-done((f32[2,1,5,64,768]{4,3,2,1,0:T(8,128)}, f32[2,1,5,64,768]{4,3,2,1,0:T(8,128)}, u32[]{:S(2)}, u32[]{:S(2)}) %collective-permute-start.11) | collective-permute-done | bytes 1966112 | tf_op jit(solution)/shard_map/ppermute | solution.py:19
  431.7 63.2 %collective-permute-done.10 = f32[2,1,5,64,768]{4,3,2,1,0:T(8,128)} collective-permute-done((f32[2,1,5,64,768]{4,3,2,1,0:T(8,128)}, f32[2,1,5,64,768]{4,3,2,1,0:T(8,128)}, u32[]{:S(2)}, u32[]{:S(2)}) %collective-permute-start.10) | collective-permute-done | bytes 1966112 | tf_op jit(solution)/shard_map/ppermute | solution.py:19
  494.9 6.1 %fusion.29 = f32[2,1,5,64,768]{4,3,2,1,0:T(8,128)S(1)} fusion(f32[2,1,5,64,768]{4,3,2,1,0:T(8,128)} %collective-permute-done.11, f32[2,1,5,64,768]{4,3,2,1,0:T(8,128)} %collective-permute-done.10, f32[2,1,5,64,768]{4,3,2,1,0:T(8,128)} %collective-permute-done.9, f32[2,1,5,64,768]{4,3,2,1,0:T(8,128)} %collective-permute-done.8, ...), kind=kLoop, calls=%fused_computation.42 | loop fusion | flops 2949120 | bytes 15728640 | tf_op jit(solution)/shard_map/add | solution.py:176
  (120 shorter events, 124.3 us)
Async XLA Ops:
  7.2 28.0 %copy-start = (bf16[768,1536]{1,0:T(8,128)(2,1)S(1)}, bf16[768,1536]{1,0:T(8,128)(2,1)}, u32[]{:S(2)}) copy-start(bf16[768,1536]{1,0:T(8,128)(2,1)} %param.24) | copy-start | bytes 7077892
  7.2 495.5 %reduce-scatter.2.cloned.1.call-start = ((), (), s32[]{:S(2)}) async-start(), calls=%async_computation.1 | async-start | bytes 5013504 | tf_op jit(solution)/shard_map/reduce_scatter | solution.py:185
  9.6 112.4 %collective-permute-start.4 = (bf16[2,1,5,64,768]{4,3,2,1,0:T(8,128)(2,1)}, bf16[2,1,5,64,768]{4,3,2,1,0:T(8,128)(2,1)}, u32[]{:S(2)}, u32[]{:S(2)}) collective-permute-start(bf16[2,1,5,64,768]{4,3,2,1,0:T(8,128)(2,1)} %pad_maximum_fusion.1), channel_id=1, source_target_pairs={{2,0},{3,1},{4,2},{5,3},{6,4},{7,5},{8,6},{9,7},{10,8},{11,9},{12,... | collective-permute-start | bytes 2949128 | tf_op jit(solution)/shard_map/ppermute | solution.py:19
  10.9 109.9 %collective-permute-start.3 = (bf16[2,1,5,64,768]{4,3,2,1,0:T(8,128)(2,1)}, bf16[2,1,5,64,768]{4,3,2,1,0:T(8,128)(2,1)}, u32[]{:S(2)}, u32[]{:S(2)}) collective-permute-start(bf16[2,1,5,64,768]{4,3,2,1,0:T(8,128)(2,1)} %pad_maximum_fusion.1), channel_id=1, source_target_pairs={{1,0},{2,1},{3,2},{4,3},{5,4},{6,5},{7,6},{8,7},{9,8},{10,9},{11,1... | collective-permute-start | bytes 2949128 | tf_op jit(solution)/shard_map/ppermute | solution.py:19
  12.2 107.2 %collective-permute-start.2 = (bf16[2,1,5,64,768]{4,3,2,1,0:T(8,128)(2,1)}, bf16[2,1,5,64,768]{4,3,2,1,0:T(8,128)(2,1)}, u32[]{:S(2)}, u32[]{:S(2)}) collective-permute-start(bf16[2,1,5,64,768]{4,3,2,1,0:T(8,128)(2,1)} %pad_maximum_fusion.1), channel_id=1, source_target_pairs={{0,1},{1,2},{2,3},{3,4},{4,5},{5,6},{6,7},{7,8},{8,9},{9,10},{10,1... | collective-permute-start | bytes 2949128 | tf_op jit(solution)/shard_map/ppermute | solution.py:19
  16.2 101.9 %collective-permute-start.1 = (bf16[2,1,5,64,768]{4,3,2,1,0:T(8,128)(2,1)}, bf16[2,1,5,64,768]{4,3,2,1,0:T(8,128)(2,1)}, u32[]{:S(2)}, u32[]{:S(2)}) collective-permute-start(bf16[2,1,5,64,768]{4,3,2,1,0:T(8,128)(2,1)} %pad_maximum_fusion.1), channel_id=1, source_target_pairs={{0,2},{1,3},{2,4},{3,5},{4,6},{5,7},{6,8},{7,9},{8,10},{9,11},{10,... | collective-permute-start | bytes 2949128 | tf_op jit(solution)/shard_map/ppermute | solution.py:19
  21.7 90.8 %collective-permute-start = (bf16[2,1,5,64,768]{4,3,2,1,0:T(8,128)(2,1)}, bf16[2,1,5,64,768]{4,3,2,1,0:T(8,128)(2,1)}, u32[]{:S(2)}, u32[]{:S(2)}) collective-permute-start(bf16[2,1,5,64,768]{4,3,2,1,0:T(8,128)(2,1)} %pad_maximum_fusion.1), channel_id=1, source_target_pairs={{0,3},{1,4},{2,5},{3,6},{4,7},{5,8},{6,9},{7,10},{8,11},{9,12},{10... | collective-permute-start | bytes 2949128 | tf_op jit(solution)/shard_map/ppermute | solution.py:19
  31.7 0.7 copy-start.12
  35.2 3.6 copy-start.11
  46.2 74.4 %copy-start.7 = (bf16[1,5,64,768]{3,2,1,0:T(8,128)(2,1)S(1)}, bf16[1,5,64,768]{3,2,1,0:T(8,128)(2,1)}, u32[]{:S(2)}) copy-start(bf16[1,5,64,768]{3,2,1,0:T(8,128)(2,1)} %param.21) | copy-start | bytes 1474564
  46.2 74.5 %copy-start.8 = (bf16[1,5,64,768]{3,2,1,0:T(8,128)(2,1)S(1)}, bf16[1,5,64,768]{3,2,1,0:T(8,128)(2,1)}, u32[]{:S(2)}) copy-start(bf16[1,5,64,768]{3,2,1,0:T(8,128)(2,1)} %param.20) | copy-start | bytes 1474564
  112.5 16.7 %collective-permute-start.5 = (bf16[2,1,5,64,768]{4,3,2,1,0:T(8,128)(2,1)}, bf16[2,1,5,64,768]{4,3,2,1,0:T(8,128)(2,1)S(1)}, u32[]{:S(2)}, u32[]{:S(2)}) collective-permute-start(bf16[2,1,5,64,768]{4,3,2,1,0:T(8,128)(2,1)} %pad_maximum_fusion.1), channel_id=1, source_target_pairs={{3,0},{4,1},{5,2},{6,3},{7,4},{8,5},{9,6},{10,7},{11,8},{12,9},{13... | collective-permute-start | bytes 2949128 | tf_op jit(solution)/shard_map/ppermute | solution.py:19
  170.9 1.7 copy-start.9
  172.7 3.4 copy-start.5
  215.0 3.4 copy-start.4
  245.3 5.6 %copy-start.10 = (bf16[320,4,64]{0,2,1:T(8,128)(2,1)S(1)}, bf16[320,4,64]{0,2,1:T(8,128)(2,1)}, u32[]{:S(2)}) copy-start(bf16[320,4,64]{0,2,1:T(8,128)(2,1)} %copy.77) | copy-start | bytes 491524
  255.1 3.4 copy-start.3
  291.1 5.1 %copy-start.6 = (f32[1,1,7,5,64,256]{5,4,3,2,1,0:T(8,128)S(1)}, f32[1,1,7,5,64,256]{5,4,3,2,1,0:T(8,128)}, u32[]{:S(2)}) copy-start(f32[1,1,7,5,64,256]{5,4,3,2,1,0:T(8,128)} %stack.48) | copy-start | bytes 6881284
  296.2 62.2 %slice-start = ((s8[5898240]{0:T(1024)(128)(4,1)}), s8[4194304]{0:T(1024)(128)(4,1)S(1)}, s32[]{:S(2)}) async-start(s8[5898240]{0:T(1024)(128)(4,1)} %bitcast.107), calls=%async_computation.2 | async-start | bytes 8388608
  300.5 57.9 %slice-start.1 = ((s8[5898240]{0:T(1024)(128)(4,1)}), s8[1703936]{0:T(1024)(128)(4,1)S(1)}, s32[]{:S(2)}) async-start(s8[5898240]{0:T(1024)(128)(4,1)} %bitcast.107), calls=%async_computation.3 | async-start | bytes 3407872
  308.4 50.1 %copy-start.2 = (bf16[2240,4,64]{0,2,1:T(8,128)(2,1)S(1)}, bf16[2240,4,64]{0,2,1:T(8,128)(2,1)}, u32[]{:S(2)}) copy-start(bf16[2240,4,64]{0,2,1:T(8,128)(2,1)} %copy.67) | copy-start | bytes 3440644
  317.3 39.8 %collective-permute-start.6 = (f32[2,1,5,64,768]{4,3,2,1,0:T(8,128)}, f32[2,1,5,64,768]{4,3,2,1,0:T(8,128)}, u32[]{:S(2)}, u32[]{:S(2)}) collective-permute-start(f32[2,1,5,64,768]{4,3,2,1,0:T(8,128)} %get-tuple-element.145), channel_id=1, source_target_pairs={{3,0},{4,1},{5,2},{6,3},{7,4},{8,5},{9,6},{10,7},{11,8},{12,9},{13... | collective-permute-start | bytes 5898248 | tf_op jit(solution)/shard_map/ppermute | solution.py:19
  318.6 113.1 %collective-permute-start.11 = (f32[2,1,5,64,768]{4,3,2,1,0:T(8,128)}, f32[2,1,5,64,768]{4,3,2,1,0:T(8,128)}, u32[]{:S(2)}, u32[]{:S(2)}) collective-permute-start(f32[2,1,5,64,768]{4,3,2,1,0:T(8,128)} %get-tuple-element.146), channel_id=1, source_target_pairs={{0,3},{1,4},{2,5},{3,6},{4,7},{5,8},{6,9},{7,10},{8,11},{9,12},{10... | collective-permute-start | bytes 5898248 | tf_op jit(solution)/shard_map/ppermute | solution.py:19
  329.7 165.2 %collective-permute-start.10 = (f32[2,1,5,64,768]{4,3,2,1,0:T(8,128)}, f32[2,1,5,64,768]{4,3,2,1,0:T(8,128)}, u32[]{:S(2)}, u32[]{:S(2)}) collective-permute-start(f32[2,1,5,64,768]{4,3,2,1,0:T(8,128)} %get-tuple-element.147), channel_id=1, source_target_pairs={{0,2},{1,3},{2,4},{3,5},{4,6},{5,7},{6,8},{7,9},{8,10},{9,11},{10,... | collective-permute-start | bytes 5898248 | tf_op jit(solution)/shard_map/ppermute | solution.py:19
  334.3 160.6 %collective-permute-start.9 = (f32[2,1,5,64,768]{4,3,2,1,0:T(8,128)}, f32[2,1,5,64,768]{4,3,2,1,0:T(8,128)}, u32[]{:S(2)}, u32[]{:S(2)}) collective-permute-start(f32[2,1,5,64,768]{4,3,2,1,0:T(8,128)} %get-tuple-element.148), channel_id=1, source_target_pairs={{0,1},{1,2},{2,3},{3,4},{4,5},{5,6},{6,7},{7,8},{8,9},{9,10},{10,1... | collective-permute-start | bytes 5898248 | tf_op jit(solution)/shard_map/ppermute | solution.py:19
  336.9 158.0 %collective-permute-start.8 = (f32[2,1,5,64,768]{4,3,2,1,0:T(8,128)}, f32[2,1,5,64,768]{4,3,2,1,0:T(8,128)}, u32[]{:S(2)}, u32[]{:S(2)}) collective-permute-start(f32[2,1,5,64,768]{4,3,2,1,0:T(8,128)} %get-tuple-element.149), channel_id=1, source_target_pairs={{1,0},{2,1},{3,2},{4,3},{5,4},{6,5},{7,6},{8,7},{9,8},{10,9},{11,1... | collective-permute-start | bytes 5898248 | tf_op jit(solution)/shard_map/ppermute | solution.py:19
  357.1 137.8 %collective-permute-start.7 = (f32[2,1,5,64,768]{4,3,2,1,0:T(8,128)}, f32[2,1,5,64,768]{4,3,2,1,0:T(8,128)}, u32[]{:S(2)}, u32[]{:S(2)}) collective-permute-start(f32[2,1,5,64,768]{4,3,2,1,0:T(8,128)} %get-tuple-element.150), channel_id=1, source_target_pairs={{2,0},{3,1},{4,2},{5,3},{6,4},{7,5},{8,6},{9,7},{10,8},{11,9},{12,... | collective-permute-start | bytes 5898248 | tf_op jit(solution)/shard_map/ppermute | solution.py:19
  494.9 7.8 %copy-start.1 = (bf16[768,1536]{1,0:T(8,128)(2,1)S(1)}, bf16[768,1536]{1,0:T(8,128)(2,1)}, u32[]{:S(2)}) copy-start(bf16[768,1536]{1,0:T(8,128)(2,1)} %param.24) | copy-start | bytes 7077892
Sparse Core Ops, SparseCore 0:
  31.8 97.7 reduce-scatter.1
where the time goes:
time: 520 us; the launch traced here: 510 us
  waiting for transfers between devices  212 us (41%)
  local copies, waits for them, and re-layouts  132 us (25%)
  matrix products  71.2 us (14%)
  starting transfers between devices  40.6 us (8%)
  other arithmetic  38.7 us (7%)
  between operations  15 us (3%)
    ppermute x12, waiting for transfers between devices, from_behind(): lax.ppermute(value, axis, [(source, source + steps) for source in range(i...  212 us
    ppermute x12, starting transfers between devices, from_behind(): lax.ppermute(value, axis, [(source, source + steps) for source in range(i...  40.6 us
    another operation x6, local copies, waits for them, and re-layouts, add_row(): jnp.stack([part_k, part_v])  32.7 us
    squeeze x6, local copies, waits for them, and re-layouts, query_row(): key_heads = key_win.reshape(key_win.shape[0], -1, HEAD)  20.9 us
    dot_general x3, matrix products, query_row(): jnp.einsum('qhe,khe->hqk', grad_heads, value_heads, preferred_element_typ...  17.4 us
    transpose x3, local copies, waits for them, and re-layouts, add_row(): jnp.einsum('hqk,qhe->khe', grad_scores, query_heads, preferred_element_ty...  16.4 us
    dot_general x3, matrix products, add_row(): jnp.einsum('hqk,qhe->khe', grad_scores, query_heads, preferred_element_ty...  16.3 us
    transpose x3, local copies, waits for them, and re-layouts, add_row(): jnp.einsum('hqk,qhe->khe', weights, grad_heads, preferred_element_type=jn...  16.2 us
  transfers between devices with their start and end apart: 13, of which 5 were waited for; matrix products, arithmetic and copies ran while one was open for 47% of the time, Pallas kernels for 0%

commit v1 on v0

v1 whole, which is shorter than its diff:
```python
import functools
import math

import jax
import jax.numpy as jnp
from jax import lax
from jax.experimental import pallas as pl
from jax.experimental.pallas import tpu as pltpu
from jax.sharding import PartitionSpec as P

HEAD = 64
REACH = 3
SCALE = 0.125
NEGATIVE = -1e30
GROUP = 4
LANES = 128
CHUNK = 256
WINDOW = 8

VMEM_SPEC = pl.BlockSpec(memory_space=pltpu.VMEM)
SMEM_SPEC = pl.BlockSpec(memory_space=pltpu.SMEM)
ANY_SPEC = pl.BlockSpec(memory_space=pl.ANY)
PARAMS = pltpu.CompilerParams(vmem_limit_bytes=56 * 1024 * 1024)


def lanes_below(shape):
    return lax.broadcasted_iota(jnp.int32, shape, len(shape) - 1) < HEAD


def pair_slab(left, right, head):
    columns = slice(head // 2 * LANES, (head // 2 + 1) * LANES)
    a, b = left[:, columns], right[:, columns]
    if head % 2:
        a = pltpu.roll(a, HEAD, 1)
    else:
        b = pltpu.roll(b, HEAD, 1)
    return jnp.where(lanes_below(a.shape), a, b)


def send_pieces(pieces, outs, sem, me):
    copies = []
    for target in range(GROUP):
        for slot in range(GROUP):
            copy = pltpu.make_async_copy(pieces.at[target], outs[slot], sem.at[target])
            copies.append((jnp.bitwise_xor(me, slot) == target, copy))
    for cond, copy in copies:
        pl.when(cond)(copy.start)
    for cond, copy in copies:
        pl.when(cond)(copy.wait)


def pack_kv_kernel(heads, me_ref, k_ref, v_ref, *rest):
    outs, (pieces, sem) = rest[:GROUP], rest[GROUP:]
    per = heads // GROUP
    for target in range(GROUP):
        for head in range(per):
            pieces[target, head] = pair_slab(k_ref, v_ref, target * per + head)
    send_pieces(pieces, outs, sem, me_ref[0])


def pack_qd_kernel(heads, me_ref, q_ref, grad_ref, w_ref, o_ref, *rest):
    outs, (pieces, sem, attn) = rest[:GROUP], rest[GROUP:]
    per = heads // GROUP
    tokens = q_ref.shape[0]
    lanes_up = -(-tokens // LANES) * LANES
    grad_attn = lax.dot_general(
        grad_ref[...], w_ref[...], (((1,), (1,)), ((), ())), preferred_element_type=jnp.float32
    ).astype(jnp.bfloat16)
    attn[...] = grad_attn
    product = grad_attn.astype(jnp.float32) * o_ref[...].astype(jnp.float32)
    lane = lax.broadcasted_iota(jnp.int32, (tokens, LANES), 1)
    for target in range(GROUP):
        columns = jnp.zeros((tokens, LANES), jnp.float32)
        for head in range(per):
            full = target * per + head
            pieces[target, head * tokens : (head + 1) * tokens] = pair_slab(q_ref, attn, full)
            dot = jnp.sum(product[:, full * HEAD : (full + 1) * HEAD], axis=1, keepdims=True)
            high = dot.astype(jnp.bfloat16).astype(jnp.float32)
            columns = jnp.where(lane == 2 * head, high, columns)
            columns = jnp.where(lane == 2 * head + 1, dot - high, columns)
        rows = jnp.transpose(columns)[:16]
        rows = jnp.concatenate([rows, jnp.zeros((16, lanes_up - tokens), jnp.float32)], axis=1)
        rows = rows.astype(jnp.bfloat16)
        for block in range(lanes_up // LANES):
            start = per * tokens + 16 * block
            pieces[target, start : start + 16] = rows[:, block * LANES : (block + 1) * LANES]
    send_pieces(pieces, outs, sem, me_ref[0])


def halo_kernel(me_ref, *refs):
    received, (up_ref, down_ref) = refs[:GROUP], refs[GROUP:]
    for slot in range(GROUP):
        row = jnp.bitwise_xor(me_ref[0], slot)

        @pl.when(row >= GROUP - REACH)
        def _():
            up_ref[row - GROUP + REACH] = received[slot][...]

        @pl.when(row < REACH)
        def _():
            down_ref[row] = received[slot][...]


def attention_kernel(per, cols, scalars, *refs):
    kv_refs = refs[:GROUP]
    above_ref, below_ref = refs[GROUP : GROUP + 2]
    qd_refs = refs[GROUP + 2 : 2 * GROUP + 2]
    outs = refs[2 * GROUP + 2 :]
    to_above, to_below, own_ref, dq_ref = outs[:4]
    k_buf, v_buf, q_buf, d_buf, qz_buf, dz_buf, delta_buf, s_all, dp_all, wds_all, zq_buf, acc, dq_buf, dqn_buf = outs[4:]
    head = pl.program_id(0)
    me, first_row = scalars[0], scalars[1]
    tokens = above_ref.shape[2]
    half = tokens // 2
    tile = tokens // cols
    rows_all = GROUP + 2 * REACH
    factor = SCALE * math.log2(math.e)
    bf16 = jnp.bfloat16
    zero = jnp.zeros((), bf16)

    lane = lax.broadcasted_iota(jnp.int32, (tokens, LANES), 1)
    low_half = lane < HEAD
    col_of = lax.broadcasted_iota(jnp.int32, (tokens, LANES), 0) // tile
    col_hot = lane == HEAD + 16 + col_of
    q_col_bias = (lane >= HEAD + 16) & (lane < HEAD + 16 + cols) & (jnp.abs(lane - (HEAD + 16) - col_of) > REACH)

    lows, highs = [], []
    for row in range(GROUP):
        here = first_row + row
        base = first_row - REACH
        lows.append(jnp.maximum(scalars[2 + 2 * row], here - REACH) - base)
        highs.append(jnp.minimum(scalars[3 + 2 * row], here + REACH) - base + 1)

    @pl.when(head == 0)
    def _():
        for slot in range(GROUP):
            row = jnp.bitwise_xor(me, slot)
            blocks = -(-tokens // LANES)
            lines = jnp.concatenate([qd_refs[slot][per * tokens + 16 * b : per * tokens + 16 * (b + 1)] for b in range(blocks)], axis=1)
            lines = jnp.concatenate([lines.astype(jnp.float32), jnp.zeros((LANES - 16, blocks * LANES), jnp.float32)], axis=0)
            delta_buf[row] = jnp.transpose(lines)[:tokens].astype(bf16)

    v_const = jnp.where((lane == 2 * head) | (lane == 2 * head + 1), -1.0, 0.0).astype(bf16)

    def put_kv(j, slab):
        where_j = pl.ds(pl.multiple_of(j * tokens, tokens), tokens)
        k_buf[where_j] = jnp.where(low_half, slab, jnp.where(col_hot | (lane == HEAD + j), 1.0, 0.0).astype(bf16))
        v_buf[where_j] = jnp.where(low_half, v_const, slab)

    for slot in range(GROUP):
        row = jnp.bitwise_xor(me, slot)
        put_kv(row + REACH, kv_refs[slot][head])
        qd = qd_refs[slot][pl.ds(pl.multiple_of(head * tokens, tokens), tokens)]
        low, high = lows[0], highs[0]
        for other in range(1, GROUP):
            low = jnp.where(row == other, lows[other], low)
            high = jnp.where(row == other, highs[other], high)
        at = lane - HEAD
        bias = q_col_bias | ((at >= 0) & (at < rows_all) & ((at < low) | (at >= high)))
        place = pl.ds(pl.multiple_of(row * tokens, tokens), tokens)
        q_buf[place] = jnp.where(low_half, qd, jnp.where(bias, NEGATIVE, 0.0).astype(bf16))
        d_buf[place] = jnp.where(low_half, delta_buf[row], qd)
        qz_buf[place] = jnp.where(low_half, qd, zero)
        dz_buf[place] = jnp.where(low_half, zero, qd)
    for row in range(REACH):
        put_kv(row, above_ref[row, head])
        put_kv(GROUP + REACH + row, below_ref[row, head])
    for c in range(GROUP * tokens // CHUNK):
        zq_buf[c, :CHUNK] = dz_buf[c * CHUNK:(c + 1) * CHUNK]
        zq_buf[c, CHUNK:] = qz_buf[c * CHUNK:(c + 1) * CHUNK]
    acc[...] = jnp.zeros_like(acc)
    nt = (((1,), (1,)), ((), ()))

    wide = WINDOW * tokens
    chunks = GROUP * tokens // CHUNK
    block = tokens

    for chunk in range(chunks):
        slot = chunk % 2
        s_buf, dp_buf, wds_buf = s_all.at[slot], dp_all.at[slot], wds_all.at[slot]
        first = min(chunk * CHUNK // tokens, rows_all - WINDOW)
        place = slice(chunk * CHUNK, (chunk + 1) * CHUNK)
        span = slice(first * tokens, first * tokens + wide)
        query = q_buf[place]
        grad = d_buf[place]
        s_buf[...] = lax.dot_general(k_buf[span], query, nt, preferred_element_type=jnp.float32)
        peak = jnp.full((8, CHUNK), NEGATIVE, jnp.float32)
        for at in range(0, wide, block):
            peak = jnp.maximum(peak, jnp.max(s_buf[at:at+block].reshape(block // 8, 8, CHUNK), axis=0))
        peak = jnp.max(peak, axis=0, keepdims=True)
        dp_buf[...] = lax.dot_general(v_buf[span], grad, nt, preferred_element_type=jnp.float32)
        total = jnp.zeros((8, CHUNK), jnp.float32)
        for at in range(0, wide, block):
            p = jnp.exp2((s_buf[at:at+block] - peak) * factor)
            s_buf[at:at+block] = p
            total = total + jnp.sum(p.reshape(block // 8, 8, CHUNK), axis=0)
        inverse = 1.0 / jnp.sum(total, axis=0, keepdims=True)
        for at in range(0, wide, block):
            p = s_buf[at:at+block] * inverse
            wds_buf[at:at+block, :CHUNK] = p.astype(bf16)
            wds_buf[at:at+block, CHUNK:] = (p * dp_buf[at:at+block]).astype(bf16)
        acc[span] += jnp.dot(wds_buf[...], zq_buf[chunk], preferred_element_type=jnp.float32)
        dq_buf[chunk] = lax.dot_general(k_buf[span], wds_buf[:, CHUNK:], (((0,), (0,)), ((), ())), preferred_element_type=jnp.float32)
    for chunk in range(chunks):
        dqn_buf[chunk * CHUNK:(chunk + 1) * CHUNK] = jnp.transpose(dq_buf[chunk])

    for row in range(REACH):
        to_above[row, head] = acc[row * tokens:(row + 1) * tokens].astype(bf16)
        to_below[row, head] = acc[(GROUP + REACH + row) * tokens:(GROUP + REACH + row + 1) * tokens].astype(bf16)
    for row in range(GROUP):
        own_ref[row, head] = acc[(REACH + row) * tokens:(REACH + row + 1) * tokens]
        dq = (SCALE * dqn_buf[row * tokens : (row + 1) * tokens]).astype(bf16)
        dq_ref[row, head] = jnp.where(low_half[:half], dq[:half], pltpu.roll(dq[half:], HEAD, 1))


def sum_kernel(per, me_ref, own_ref, above_ref, below_ref, *rest):
    outs, (pieces, sem) = rest[:GROUP], rest[GROUP:]
    for row in range(GROUP):
        for slab in range(per):
            value = own_ref[row, slab]
            if row < REACH:
                value = value + above_ref[row, slab].astype(jnp.float32)
            if row >= GROUP - REACH:
                value = value + below_ref[row - GROUP + REACH, slab].astype(jnp.float32)
            value = jnp.where(lanes_below(value.shape), value * SCALE, value)
            pieces[row, slab] = value.astype(jnp.bfloat16)
    send_pieces(pieces, outs, sem, me_ref[0])


def unpack_kernel(per, me_ref, *refs):
    dq_refs, kv_refs = refs[:GROUP], refs[GROUP : 2 * GROUP]
    q_out, k_out, v_out, dq_all, kv_all, sem = refs[2 * GROUP :]
    me = me_ref[0]
    half = dq_refs[0].shape[1]
    copies = []
    for slot in range(GROUP):
        source = jnp.bitwise_xor(me, slot)
        copies.append(pltpu.make_async_copy(dq_refs[slot], dq_all.at[source], sem.at[0, slot]))
        copies.append(pltpu.make_async_copy(kv_refs[slot], kv_all.at[source], sem.at[1, slot]))
    for copy in copies:
        copy.start()
    for copy in copies:
        copy.wait()
    for pair in range(GROUP * per // 2):
        (ga, ha), (gb, hb) = [divmod(2 * pair + step, per) for step in range(2)]
        columns = slice(pair * LANES, (pair + 1) * LANES)
        a, b = dq_all[ga, ha], dq_all[gb, hb]
        below = lanes_below(a.shape)
        q_out[:half, columns] = jnp.where(below, a, pltpu.roll(b, HEAD, 1))
        q_out[half:, columns] = jnp.where(below, pltpu.roll(a, HEAD, 1), b)
        a, b = kv_all[ga, ha], kv_all[gb, hb]
        below = lanes_below(a.shape)
        k_out[:, columns] = jnp.where(below, a, pltpu.roll(b, HEAD, 1))
        v_out[:, columns] = jnp.where(below, pltpu.roll(a, HEAD, 1), b)


def body(queries, keys, values, outputs, grad_out, w_out, bounds):
    own_rows, cols, tile, features = queries.shape
    tokens = own_rows * cols * tile
    half = tokens // 2
    heads = features // HEAD
    per = heads // GROUP
    count = lax.axis_size("row")
    assert own_rows == 1 and count % GROUP == 0 and heads % GROUP == 0
    bf16 = jnp.bfloat16
    position = lax.axis_index("row")
    me = (position % GROUP).astype(jnp.int32)
    first_row = position - me
    me_arr = me.reshape(1)
    q2, k2, v2, o2 = [x.reshape(tokens, features) for x in (queries, keys, values, outputs)]
    g2 = grad_out.reshape(tokens, -1)

    def exchange(pieces):
        result = [pieces[0]]
        for slot in range(1, GROUP):
            result.append(
                lax.ppermute(pieces[slot], "row", [(i, i ^ slot) for i in range(count)])
            )
        return result

    def shift(value, step):
        pairs = [(i, i + step) for i in range(count) if 0 <= i + step < count]
        return lax.ppermute(value, "row", pairs)

    def spread(rows):
        return [
            lax.dynamic_index_in_dim(rows, jnp.bitwise_xor(me, slot), 0, keepdims=False)
            for slot in range(GROUP)
        ]

    piece = (per, tokens, LANES)
    kv = pl.pallas_call(
        functools.partial(pack_kv_kernel, heads),
        out_shape=[jax.ShapeDtypeStruct(piece, bf16)] * GROUP,
        in_specs=[SMEM_SPEC, VMEM_SPEC, VMEM_SPEC],
        out_specs=[ANY_SPEC] * GROUP,
        scratch_shapes=[pltpu.VMEM((GROUP,) + piece, bf16), pltpu.SemaphoreType.DMA((GROUP,))],
        compiler_params=PARAMS,
        name="pack_kv",
    )(me_arr, k2, v2)
    kv = exchange(kv)

    qd_rows = per * tokens + 16 * (-(-tokens // LANES))
    qd = pl.pallas_call(
        functools.partial(pack_qd_kernel, heads),
        out_shape=[jax.ShapeDtypeStruct((qd_rows, LANES), bf16)] * GROUP,
        in_specs=[SMEM_SPEC] + [VMEM_SPEC] * 4,
        out_specs=[ANY_SPEC] * GROUP,
        scratch_shapes=[
            pltpu.VMEM((GROUP, qd_rows, LANES), bf16),
            pltpu.SemaphoreType.DMA((GROUP,)),
            pltpu.VMEM((tokens, features), bf16),
        ],
        compiler_params=PARAMS,
        name="pack_qd",
    )(me_arr, q2, g2, w_out, o2)
    qd = exchange(qd)

    window = (REACH,) + piece
    up, down = pl.pallas_call(
        halo_kernel,
        out_shape=[jax.ShapeDtypeStruct(window, bf16)] * 2,
        in_specs=[SMEM_SPEC] + [VMEM_SPEC] * GROUP,
        out_specs=[VMEM_SPEC] * 2,
        compiler_params=PARAMS,
        name="halo",
    )(me_arr, *kv)
    above = shift(up, GROUP)
    below = shift(down, -GROUP)

    limits = lax.dynamic_slice_in_dim(bounds, first_row, GROUP, 0).reshape(-1)
    scalars = jnp.concatenate([me_arr, first_row.reshape(1), limits])
    rows_all = GROUP + 2 * REACH
    chunks = GROUP * tokens // CHUNK
    results = pl.pallas_call(
        functools.partial(attention_kernel, per, cols),
        grid=(per,),
        out_shape=[
            jax.ShapeDtypeStruct(window, bf16),
            jax.ShapeDtypeStruct(window, bf16),
            jax.ShapeDtypeStruct((GROUP,) + piece, jnp.float32),
            jax.ShapeDtypeStruct((GROUP, per, half, LANES), bf16),
        ],
        in_specs=[SMEM_SPEC] + [VMEM_SPEC] * (2 * GROUP + 2),
        out_specs=[VMEM_SPEC] * 4,
        scratch_shapes=[pltpu.VMEM((rows_all * tokens, LANES), bf16)] * 2
        + [pltpu.VMEM((GROUP * tokens, LANES), bf16)] * 4
        + [
            pltpu.VMEM((GROUP, tokens, LANES), bf16),
            pltpu.VMEM((2, WINDOW * tokens, CHUNK), jnp.float32),
            pltpu.VMEM((2, WINDOW * tokens, CHUNK), jnp.float32),
            pltpu.VMEM((2, WINDOW * tokens, 2 * CHUNK), bf16),
            pltpu.VMEM((chunks, 2 * CHUNK, LANES), bf16),
            pltpu.VMEM((rows_all * tokens, LANES), jnp.float32),
            pltpu.VMEM((chunks, LANES, CHUNK), jnp.float32),
            pltpu.VMEM((GROUP * tokens, LANES), jnp.float32),
        ],
        compiler_params=PARAMS,
        name="attention",
    )(scalars, *kv, above, below, *qd)
    to_above, to_below, own, dq = results
    dq = exchange(spread(dq))
    from_above = shift(to_below, GROUP)
    from_below = shift(to_above, -GROUP)

    dkv = pl.pallas_call(
        functools.partial(sum_kernel, per),
        out_shape=[jax.ShapeDtypeStruct(piece, bf16)] * GROUP,
        in_specs=[SMEM_SPEC] + [VMEM_SPEC] * 3,
        out_specs=[ANY_SPEC] * GROUP,
        scratch_shapes=[pltpu.VMEM((GROUP,) + piece, bf16), pltpu.SemaphoreType.DMA((GROUP,))],
        compiler_params=PARAMS,
        name="sum",
    )(me_arr, own, from_above, from_below)
    dkv = exchange(dkv)

    grads = pl.pallas_call(
        functools.partial(unpack_kernel, per),
        out_shape=[jax.ShapeDtypeStruct((tokens, features), bf16)] * 3,
        in_specs=[SMEM_SPEC] + [ANY_SPEC] * (2 * GROUP),
        out_specs=[VMEM_SPEC] * 3,
        scratch_shapes=[
            pltpu.VMEM((GROUP, per, half, LANES), bf16),
            pltpu.VMEM((GROUP,) + piece, bf16),
            pltpu.SemaphoreType.DMA((2, GROUP)),
        ],
        compiler_params=PARAMS,
        name="unpack",
    )(me_arr, *dq, *dkv)
    grads = [x.reshape(queries.shape) for x in grads]

    grad_w_out = lax.psum_scatter(
        lax.dot_general(o2, g2, (((0,), (0,)), ((), ())), preferred_element_type=jnp.float32),
        "row",
        scatter_dimension=0,
        tiled=True,
    )
    return (*grads, grad_w_out)


def solution(mesh):
    placed = P(("groups", "row"), None, None, None)
    return jax.shard_map(
        body,
        mesh=mesh,
        in_specs=(placed, placed, placed, placed, placed, P(), P("groups", None)),
        out_specs=(placed, placed, placed, P(("groups", "row"), None)),
        check_vma=False,
    )
```

time: 520 us -> 166 us (0.32); the launches traced: 510 us -> 166 us
  waiting for transfers between devices: 212 us -> 64.8 us
  local copies, waits for them, and re-layouts: 132 us -> 5.77 us
  matrix products: 71.2 us -> 4.91 us
  Pallas kernels: 0 us -> 56.9 us
  other arithmetic: 38.7 us -> 0.62 us
  starting transfers between devices: 40.6 us -> 18.4 us
    ppermute x12 -> x16, waiting for transfers between devices: 212 us -> 64.8 us  [the longest x12 47.6 us: exchange(): lax.ppermute(pieces[slot], 'row', [(i, i ^ slot) for i in range(count)])]
    dot_general x17 -> x1, matrix products: 71.2 us -> 4.91 us  [body(): lax.dot_general(o2, g2, (((0,), (0,)), ((), ())), preferred_element_type=...]
    pallas_call x0 -> x6, Pallas kernels: none -> 56.9 us  [the longest x1 38.6 us: body(): pl.pallas_call(functools.partial(attention_kernel, per, cols), grid=(per,...]
    squeeze x9 -> x1, local copies, waits for them, and re-layouts: 34.9 us -> 1.76 us  [spread(): lax.dynamic_index_in_dim(rows, jnp.bitwise_xor(me, slot), 0, keepdims=False)]
    another operation x6 -> x0, local copies, waits for them, and re-layouts: 32.7 us -> none  [add_row(): jnp.stack([part_k, part_v])]
    transpose x6 -> x0, local copies, waits for them, and re-layouts: 32.6 us -> none  [the longest x3 16.4 us: add_row(): jnp.einsum('hqk,qhe->khe', grad_scores, query_heads, preferred_element_ty...]
    ppermute x12 -> x16, starting transfers between devices: 40.6 us -> 18.4 us  [the longest x4 10.4 us: shift(): return lax.ppermute(value, 'row', pairs)]
    add x6 -> x0, other arithmetic: 15.5 us -> none  [the longest x2 9.34 us: body(): group_totals.at[:, first_row:first_row + window_rows].add(updates[offset])]
  transfers between devices with their start and end apart: 13 -> 17, of which waited for: 5 -> 8; matrix products, arithmetic and copies ran while one was open for 47% -> 2% of each run, Pallas kernels for 0% -> 34%
where the time goes in v1:
time: 166 us
  waiting for transfers between devices  64.8 us (39%)
  Pallas kernels  56.9 us (34%)
  starting transfers between devices  18.4 us (11%)
  between operations  14.3 us (9%)
  local copies, waits for them, and re-layouts  5.77 us (3%)
  matrix products  4.91 us (3%)
    ppermute x12, waiting for transfers between devices, exchange(): lax.ppermute(pieces[slot], 'row', [(i, i ^ slot) for i in range(count)])  47.6 us
    pallas_call x1, Pallas kernels, body(): pl.pallas_call(functools.partial(attention_kernel, per, cols), grid=(per,...  38.6 us
    ppermute x4, waiting for transfers between devices, shift(): return lax.ppermute(value, 'row', pairs)  17.2 us
    ppermute x4, starting transfers between devices, shift(): return lax.ppermute(value, 'row', pairs)  10.4 us
    ppermute x12, starting transfers between devices, exchange(): lax.ppermute(pieces[slot], 'row', [(i, i ^ slot) for i in range(count)])  7.95 us
    pallas_call x1, Pallas kernels, body(): pl.pallas_call(functools.partial(pack_qd_kernel, heads), out_shape=[jax.S...  6.8 us
    dot_general x1, matrix products, body(): lax.dot_general(o2, g2, (((0,), (0,)), ((), ())), preferred_element_type=...  4.91 us
    unnamed x34, local copies, waits for them, and re-layouts  3.75 us
  transfers between devices with their start and end apart: 17, of which 8 were waited for; matrix products, arithmetic and copies ran while one was open for 2% of the time, Pallas kernels for 34%

profile of v1, /device:TPU:0, one launch (start us, length us, event | category | flops | bytes accessed | tf_op | source)
XLA Modules:
  0.0 165.6 jit_solution(1661169743835087429)
XLA Ops:
  7.2 4.9 %convolution_bitcast_fusion = f32[768,1536]{1,0:T(8,128)} fusion(bf16[1,5,64,1536]{3,2,1,0:T(8,128)(2,1)} %param.11, bf16[1,5,64,768]{3,2,1,0:T(8,128)(2,1)} %param.10), kind=kOutput, calls=%fused_computation | convolution fusion | flops 754974720 | bytes 6193152 | tf_op jit(solution)/shard_map/dot_general | solution.py:393
  12.2 2.5 %pack_kv.1 = (bf16[3,320,128]{2,1,0:T(8,128)(2,1)}, bf16[3,320,128]{2,1,0:T(8,128)(2,1)}, bf16[3,320,128]{2,1,0:T(8,128)(2,1)}, bf16[3,320,128]{2,1,0:T(8,128)(2,1)}) custom-call(s32[1]{0:T(128)} %bitcast.me_ref, bf16[320,768]{1,0:T(8,128)(2,1)} %bitcast.27, bf16[320,768]{1,0:T(8,128)(2,1)} %bitcast.28), custom_call_target="tpu_custom_call" | custom-call | tf_op jit(solution)/shard_map/pack_kv/pallas_call | solution.py:292
  14.7 0.5 collective-permute-start
  15.2 2.6 %collective-permute-start.1 = (bf16[3,320,128]{2,1,0:T(8,128)(2,1)}, bf16[3,320,128]{2,1,0:T(8,128)(2,1)S(1)}, u32[]{:S(2)}, u32[]{:S(2)}) collective-permute-start(bf16[3,320,128]{2,1,0:T(8,128)(2,1)} %get-tuple-element.27), channel_id=1, source_target_pairs={{0,2},{1,3},{2,0},{3,1},{4,6},{5,7},{6,4},{7,5},{8,10},{9,11},{10,... | collective-permute-start | bytes 737288 | tf_op jit(solution)/shard_map/ppermute | solution.py:277
  17.8 6.9 %collective-permute-done.1.refs_2_ = bf16[3,320,128]{2,1,0:T(8,128)(2,1)S(1)} collective-permute-done((bf16[3,320,128]{2,1,0:T(8,128)(2,1)}, bf16[3,320,128]{2,1,0:T(8,128)(2,1)S(1)}, u32[]{:S(2)}, u32[]{:S(2)}) %collective-permute-start.1) | collective-permute-done | bytes 245792 | tf_op jit(solution)/shard_map/ppermute | solution.py:277
  24.8 4.7 %collective-permute-done.2.refs_3_ = bf16[3,320,128]{2,1,0:T(8,128)(2,1)S(1)} collective-permute-done((bf16[3,320,128]{2,1,0:T(8,128)(2,1)}, bf16[3,320,128]{2,1,0:T(8,128)(2,1)S(1)}, u32[]{:S(2)}, u32[]{:S(2)}) %collective-permute-start.2) | collective-permute-done | bytes 245792 | tf_op jit(solution)/shard_map/ppermute | solution.py:277
  29.5 0.7 copy-done.3
  30.2 2.7 %halo.1 = (bf16[3,3,320,128]{3,2,1,0:T(8,128)(2,1)}, bf16[3,3,320,128]{3,2,1,0:T(8,128)(2,1)}) custom-call(s32[1]{0:T(128)} %bitcast.me_ref, bf16[3,320,128]{2,1,0:T(8,128)(2,1)} %get-tuple-element.25.refs_0_, bf16[3,320,128]{2,1,0:T(8,128)(2,1)} %copy-done.1, bf16[3,320,128]{2,1,0:T(8,128)(2,1)} %copy-done.2, bf16[3,320,128]{2,1,0:T(8,128)(2,1)} %copy-done.3), custom_call_target="tpu_custom_call" | custom-call | tf_op jit(solution)/shard_map/halo/pallas_call | solution.py:320
  32.9 3.6 %collective-permute-start.3 = (bf16[3,3,320,128]{3,2,1,0:T(8,128)(2,1)}, bf16[3,3,320,128]{3,2,1,0:T(8,128)(2,1)S(1)}, u32[]{:S(2)}, u32[]{:S(2)}) collective-permute-start(bf16[3,3,320,128]{3,2,1,0:T(8,128)(2,1)} %get-tuple-element.29), channel_id=1, source_target_pairs={{0,4},{1,5},{2,6},{3,7},{4,8},{5,9},{6,10},{7,11},{8,12},{9,13},{1... | collective-permute-start | bytes 2211848 | tf_op jit(solution)/shard_map/ppermute | solution.py:283
  36.5 1.3 collective-permute-start.4
  37.8 6.8 %pack_qd.1 = (bf16[1008,128]{1,0:T(8,128)(2,1)}, bf16[1008,128]{1,0:T(8,128)(2,1)}, bf16[1008,128]{1,0:T(8,128)(2,1)}, bf16[1008,128]{1,0:T(8,128)(2,1)}) custom-call(s32[1]{0:T(128)} %bitcast.me_ref, bf16[320,768]{1,0:T(8,128)(2,1)} %bitcast.29, bf16[320,1536]{1,0:T(8,128)(2,1)} %bitcast.26, bf16[768,1536]{1,0:T(8,128)(2,1)} %w_ref.1, bf16[320,768]{1,0:T(8,128)(2,1)} %bitcast.30), custom_call_target="tpu_custom_call" | custom-call | tf_op jit(solution)/shard_map/pack_qd/pallas_call | solution.py:304
  44.6 1.6 collective-permute-start.6
  46.8 0.6 pad_add_fusion.scalars
  47.4 11.9 %collective-permute-done.6.refs_8_ = bf16[1008,128]{1,0:T(8,128)(2,1)S(1)} collective-permute-done((bf16[1008,128]{1,0:T(8,128)(2,1)}, bf16[1008,128]{1,0:T(8,128)(2,1)S(1)}, u32[]{:S(2)}, u32[]{:S(2)}) %collective-permute-start.6) | collective-permute-done | bytes 258080 | tf_op jit(solution)/shard_map/ppermute | solution.py:277
  59.3 10.3 %collective-permute-done.7.refs_9_ = bf16[1008,128]{1,0:T(8,128)(2,1)S(1)} collective-permute-done((bf16[1008,128]{1,0:T(8,128)(2,1)}, bf16[1008,128]{1,0:T(8,128)(2,1)S(1)}, u32[]{:S(2)}, u32[]{:S(2)}) %collective-permute-start.7) | collective-permute-done | bytes 258080 | tf_op jit(solution)/shard_map/ppermute | solution.py:277
  69.6 0.7 copy-done.10
  70.3 0.4 copy-done.4
  70.9 38.6 %attention.1 = (bf16[3,3,320,128]{3,2,1,0:T(8,128)(2,1)}, bf16[3,3,320,128]{3,2,1,0:T(8,128)(2,1)}, f32[4,3,320,128]{3,2,1,0:T(8,128)}, bf16[4,3,160,128]{3,2,1,0:T(8,128)(2,1)}) custom-call(s32[10]{0:T(128)} %pad_add_fusion.scalars, bf16[3,320,128]{2,1,0:T(8,128)(2,1)} %get-tuple-element.25.refs_0_, bf16[3,320,128]{2,1,0:T(8,128)(2,1)} %copy-done.1, ...), custom_call_target="tpu_custom_call" | custom-call | tf_op jit(solution)/shard_map/attention/pallas_call | solution.py:335
  109.6 4.3 %collective-permute-start.11 = (bf16[3,3,320,128]{3,2,1,0:T(8,128)(2,1)}, bf16[3,3,320,128]{3,2,1,0:T(8,128)(2,1)S(1)}, u32[]{:S(2)}, u32[]{:S(2)}) collective-permute-start(bf16[3,3,320,128]{3,2,1,0:T(8,128)(2,1)} %get-tuple-element.37), channel_id=1, source_target_pairs={{0,4},{1,5},{2,6},{3,7},{4,8},{5,9},{6,10},{7,11},{8,12},{9,13},{1... | collective-permute-start | bytes 2211848 | tf_op jit(solution)/shard_map/ppermute | solution.py:283
  113.8 1.3 collective-permute-start.12
  115.2 1.8 %dynamic-slice_bitcast_fusion = (bf16[3,160,128]{2,1,0:T(8,128)(2,1)S(1)}, bf16[3,160,128]{2,1,0:T(8,128)(2,1)S(1)}, bf16[3,160,128]{2,1,0:T(8,128)(2,1)S(1)}, bf16[3,160,128]{2,1,0:T(8,128)(2,1)}) fusion(bf16[4,3,160,128]{3,2,1,0:T(8,128)(2,1)} %get-tuple-element.35, s32[]{:T(128)S(6)} %select_n.28, s32[]{:T(128)S(6)} %select_n.27, s32[]{:T(128)S(6)} %select_n.26, ...), kind=kLoop, calls=%fused_computation.3 | loop fusion | bytes 983056 | tf_op jit(solution)/shard_map/jit(dynamic_index_in_dim)/squeeze | solution.py:287
  116.9 13.1 %collective-permute-done.11.above_ref = bf16[3,3,320,128]{3,2,1,0:T(8,128)(2,1)S(1)} collective-permute-done((bf16[3,3,320,128]{3,2,1,0:T(8,128)(2,1)}, bf16[3,3,320,128]{3,2,1,0:T(8,128)(2,1)S(1)}, u32[]{:S(2)}, u32[]{:S(2)}) %collective-permute-start.11) | collective-permute-done | bytes 737312 | tf_op jit(solution)/shard_map/ppermute | solution.py:283
  130.0 4.1 %collective-permute-done.12.below_ref = bf16[3,3,320,128]{3,2,1,0:T(8,128)(2,1)S(1)} collective-permute-done((bf16[3,3,320,128]{3,2,1,0:T(8,128)(2,1)}, bf16[3,3,320,128]{3,2,1,0:T(8,128)(2,1)S(1)}, u32[]{:S(2)}, u32[]{:S(2)}) %collective-permute-start.12) | collective-permute-done | bytes 737312 | tf_op jit(solution)/shard_map/ppermute | solution.py:283
  134.1 0.8 copy-done.7
  134.9 3.2 %sum.1 = (bf16[3,320,128]{2,1,0:T(8,128)(2,1)}, bf16[3,320,128]{2,1,0:T(8,128)(2,1)}, bf16[3,320,128]{2,1,0:T(8,128)(2,1)}, bf16[3,320,128]{2,1,0:T(8,128)(2,1)}) custom-call(s32[1]{0:T(128)} %bitcast.me_ref, f32[4,3,320,128]{3,2,1,0:T(8,128)} %get-tuple-element.36.own_ref, bf16[3,3,320,128]{3,2,1,0:T(8,128)(2,1)} %copy-done.6, ...), custom_call_target="tpu_custom_call" | custom-call | tf_op jit(solution)/shard_map/sum/pallas_call | solution.py:366
  138.3 0.6 collective-permute-start.14
  138.9 1.2 collective-permute-start.15
  140.5 0.6 collective-permute-start.9
  141.0 0.4 collective-permute-done.8.refs_1_
  141.5 13.3 %collective-permute-done.9.refs_2_ = bf16[3,160,128]{2,1,0:T(8,128)(2,1)S(1)} collective-permute-done((bf16[3,160,128]{2,1,0:T(8,128)(2,1)S(1)}, bf16[3,160,128]{2,1,0:T(8,128)(2,1)S(1)}, u32[]{:S(2)}, u32[]{:S(2)}) %collective-permute-start.9) | collective-permute-done | bytes 122912 | tf_op jit(solution)/shard_map/ppermute | solution.py:277
  154.8 0.6 copy-done.16
  155.7 3.0 %unpack.1 = (bf16[320,768]{1,0:T(8,128)(2,1)}, bf16[320,768]{1,0:T(8,128)(2,1)}, bf16[320,768]{1,0:T(8,128)(2,1)}) custom-call(s32[1]{0:T(128)} %bitcast.me_ref, bf16[3,160,128]{2,1,0:T(8,128)(2,1)} %get-tuple-element.49.refs_0_, bf16[3,160,128]{2,1,0:T(8,128)(2,1)} %copy-done.15, bf16[3,160,128]{2,1,0:T(8,128)(2,1)} %copy-done.16, ...), custom_call_target="tpu_custom_call" | custom-call | tf_op jit(solution)/shard_map/unpack/pallas_call | solution.py:377
  (49 shorter events, 1.8 us)
Async XLA Ops:
  7.2 39.4 %copy-start = (s32[16,2]{0,1:T(2,128)S(1)}, s32[16,2]{0,1:T(2,128)}, u32[]{:S(2)}) copy-start(s32[16,2]{0,1:T(2,128)} %param.13) | copy-start | bytes 388
  7.2 151.6 %reduce-scatter.2.cloned.1.call-start = ((), (), s32[]{:S(2)}) async-start(), calls=%async_computation.1 | async-start | bytes 5013504 | tf_op jit(solution)/shard_map/reduce_scatter | solution.py:392
  14.7 3.2 %collective-permute-start = (bf16[3,320,128]{2,1,0:T(8,128)(2,1)}, bf16[3,320,128]{2,1,0:T(8,128)(2,1)S(1)}, u32[]{:S(2)}, u32[]{:S(2)}) collective-permute-start(bf16[3,320,128]{2,1,0:T(8,128)(2,1)} %get-tuple-element.26), channel_id=1, source_target_pairs={{0,1},{1,0},{2,3},{3,2},{4,5},{5,4},{6,7},{7,6},{8,9},{9,8},{10,11... | collective-permute-start | bytes 737288 | tf_op jit(solution)/shard_map/ppermute | solution.py:277
  15.2 9.6 %collective-permute-start.1 = (bf16[3,320,128]{2,1,0:T(8,128)(2,1)}, bf16[3,320,128]{2,1,0:T(8,128)(2,1)S(1)}, u32[]{:S(2)}, u32[]{:S(2)}) collective-permute-start(bf16[3,320,128]{2,1,0:T(8,128)(2,1)} %get-tuple-element.27), channel_id=1, source_target_pairs={{0,2},{1,3},{2,0},{3,1},{4,6},{5,7},{6,4},{7,5},{8,10},{9,11},{10,... | collective-permute-start | bytes 737288 | tf_op jit(solution)/shard_map/ppermute | solution.py:277
  17.8 11.8 %collective-permute-start.2 = (bf16[3,320,128]{2,1,0:T(8,128)(2,1)}, bf16[3,320,128]{2,1,0:T(8,128)(2,1)S(1)}, u32[]{:S(2)}, u32[]{:S(2)}) collective-permute-start(bf16[3,320,128]{2,1,0:T(8,128)(2,1)} %get-tuple-element.28), channel_id=1, source_target_pairs={{0,3},{1,2},{2,1},{3,0},{4,7},{5,6},{6,5},{7,4},{8,11},{9,10},{10,... | collective-permute-start | bytes 737288 | tf_op jit(solution)/shard_map/ppermute | solution.py:277
  17.8 11.7 %copy-start.1 = (bf16[3,320,128]{2,1,0:T(8,128)(2,1)}, bf16[3,320,128]{2,1,0:T(8,128)(2,1)S(1)}, u32[]{:S(2)}) copy-start(bf16[3,320,128]{2,1,0:T(8,128)(2,1)S(1)} %collective-permute-done.refs_1_) | copy-start | bytes 737284
  24.8 4.8 %copy-start.2 = (bf16[3,320,128]{2,1,0:T(8,128)(2,1)}, bf16[3,320,128]{2,1,0:T(8,128)(2,1)S(1)}, u32[]{:S(2)}) copy-start(bf16[3,320,128]{2,1,0:T(8,128)(2,1)S(1)} %collective-permute-done.1.refs_2_) | copy-start | bytes 737284
  32.9 36.7 %collective-permute-start.3 = (bf16[3,3,320,128]{3,2,1,0:T(8,128)(2,1)}, bf16[3,3,320,128]{3,2,1,0:T(8,128)(2,1)S(1)}, u32[]{:S(2)}, u32[]{:S(2)}) collective-permute-start(bf16[3,3,320,128]{3,2,1,0:T(8,128)(2,1)} %get-tuple-element.29), channel_id=1, source_target_pairs={{0,4},{1,5},{2,6},{3,7},{4,8},{5,9},{6,10},{7,11},{8,12},{9,13},{1... | collective-permute-start | bytes 2211848 | tf_op jit(solution)/shard_map/ppermute | solution.py:283
  36.5 33.1 %collective-permute-start.4 = (bf16[3,3,320,128]{3,2,1,0:T(8,128)(2,1)}, bf16[3,3,320,128]{3,2,1,0:T(8,128)(2,1)S(1)}, u32[]{:S(2)}, u32[]{:S(2)}) collective-permute-start(bf16[3,3,320,128]{3,2,1,0:T(8,128)(2,1)} %get-tuple-element.30), channel_id=1, source_target_pairs={{4,0},{5,1},{6,2},{7,3},{8,4},{9,5},{10,6},{11,7},{12,8},{13,9},{1... | collective-permute-start | bytes 2211848 | tf_op jit(solution)/shard_map/ppermute | solution.py:283
  44.6 2.8 %collective-permute-start.5 = (bf16[1008,128]{1,0:T(8,128)(2,1)}, bf16[1008,128]{1,0:T(8,128)(2,1)S(1)}, u32[]{:S(2)}, u32[]{:S(2)}) collective-permute-start(bf16[1008,128]{1,0:T(8,128)(2,1)} %get-tuple-element.32), channel_id=1, source_target_pairs={{0,1},{1,0},{2,3},{3,2},{4,5},{5,4},{6,7},{7,6},{8,9},{9,8},{10,11... | collective-permute-start | bytes 774152 | tf_op jit(solution)/shard_map/ppermute | solution.py:277
  44.6 14.7 %collective-permute-start.6 = (bf16[1008,128]{1,0:T(8,128)(2,1)}, bf16[1008,128]{1,0:T(8,128)(2,1)S(1)}, u32[]{:S(2)}, u32[]{:S(2)}) collective-permute-start(bf16[1008,128]{1,0:T(8,128)(2,1)} %get-tuple-element.33), channel_id=1, source_target_pairs={{0,2},{1,3},{2,0},{3,1},{4,6},{5,7},{6,4},{7,5},{8,10},{9,11},{10,... | collective-permute-start | bytes 774152 | tf_op jit(solution)/shard_map/ppermute | solution.py:277
  46.2 23.4 %collective-permute-start.7 = (bf16[1008,128]{1,0:T(8,128)(2,1)}, bf16[1008,128]{1,0:T(8,128)(2,1)S(1)}, u32[]{:S(2)}, u32[]{:S(2)}) collective-permute-start(bf16[1008,128]{1,0:T(8,128)(2,1)} %get-tuple-element.34), channel_id=1, source_target_pairs={{0,3},{1,2},{2,1},{3,0},{4,7},{5,6},{6,5},{7,4},{8,11},{9,10},{10,... | collective-permute-start | bytes 774152 | tf_op jit(solution)/shard_map/ppermute | solution.py:277
  47.4 22.2 %copy-start.8 = (bf16[1008,128]{1,0:T(8,128)(2,1)}, bf16[1008,128]{1,0:T(8,128)(2,1)S(1)}, u32[]{:S(2)}) copy-start(bf16[1008,128]{1,0:T(8,128)(2,1)S(1)} %collective-permute-done.5.refs_7_) | copy-start | bytes 774148
  59.3 10.3 %copy-start.9 = (bf16[1008,128]{1,0:T(8,128)(2,1)}, bf16[1008,128]{1,0:T(8,128)(2,1)S(1)}, u32[]{:S(2)}) copy-start(bf16[1008,128]{1,0:T(8,128)(2,1)S(1)} %collective-permute-done.6.refs_8_) | copy-start | bytes 774148
  69.6 0.7 copy-start.10
  69.6 1.1 copy-start.4
  69.6 1.3 copy-start.5
  109.6 20.5 %collective-permute-start.11 = (bf16[3,3,320,128]{3,2,1,0:T(8,128)(2,1)}, bf16[3,3,320,128]{3,2,1,0:T(8,128)(2,1)S(1)}, u32[]{:S(2)}, u32[]{:S(2)}) collective-permute-start(bf16[3,3,320,128]{3,2,1,0:T(8,128)(2,1)} %get-tuple-element.37), channel_id=1, source_target_pairs={{0,4},{1,5},{2,6},{3,7},{4,8},{5,9},{6,10},{7,11},{8,12},{9,13},{1... | collective-permute-start | bytes 2211848 | tf_op jit(solution)/shard_map/ppermute | solution.py:283
  113.8 20.2 %collective-permute-start.12 = (bf16[3,3,320,128]{3,2,1,0:T(8,128)(2,1)}, bf16[3,3,320,128]{3,2,1,0:T(8,128)(2,1)S(1)}, u32[]{:S(2)}, u32[]{:S(2)}) collective-permute-start(bf16[3,3,320,128]{3,2,1,0:T(8,128)(2,1)} %get-tuple-element.38), channel_id=1, source_target_pairs={{4,0},{5,1},{6,2},{7,3},{8,4},{9,5},{10,6},{11,7},{12,8},{13,9},{1... | collective-permute-start | bytes 2211848 | tf_op jit(solution)/shard_map/ppermute | solution.py:283
  116.9 23.6 %collective-permute-start.10 = (bf16[3,160,128]{2,1,0:T(8,128)(2,1)S(1)}, bf16[3,160,128]{2,1,0:T(8,128)(2,1)S(1)}, u32[]{:S(2)}, u32[]{:S(2)}) collective-permute-start(bf16[3,160,128]{2,1,0:T(8,128)(2,1)S(1)} %get-tuple-element.46), channel_id=1, source_target_pairs={{0,3},{1,2},{2,1},{3,0},{4,7},{5,6},{6,5},{7,4},{8,11},{9,10},{10,... | collective-permute-start | bytes 368648 | tf_op jit(solution)/shard_map/ppermute | solution.py:277
  130.0 4.1 %copy-start.6 = (bf16[3,3,320,128]{3,2,1,0:T(8,128)(2,1)}, bf16[3,3,320,128]{3,2,1,0:T(8,128)(2,1)S(1)}, u32[]{:S(2)}) copy-start(bf16[3,3,320,128]{3,2,1,0:T(8,128)(2,1)S(1)} %collective-permute-done.11.above_ref) | copy-start | bytes 2211844
  134.1 0.9 copy-start.7
  138.2 16.6 %collective-permute-start.13 = (bf16[3,320,128]{2,1,0:T(8,128)(2,1)}, bf16[3,320,128]{2,1,0:T(8,128)(2,1)S(1)}, u32[]{:S(2)}, u32[]{:S(2)}) collective-permute-start(bf16[3,320,128]{2,1,0:T(8,128)(2,1)} %get-tuple-element.40), channel_id=1, source_target_pairs={{0,1},{1,0},{2,3},{3,2},{4,5},{5,4},{6,7},{7,6},{8,9},{9,8},{10,11... | collective-permute-start | bytes 737288 | tf_op jit(solution)/shard_map/ppermute | solution.py:277
  138.3 16.5 %collective-permute-start.14 = (bf16[3,320,128]{2,1,0:T(8,128)(2,1)}, bf16[3,320,128]{2,1,0:T(8,128)(2,1)S(1)}, u32[]{:S(2)}, u32[]{:S(2)}) collective-permute-start(bf16[3,320,128]{2,1,0:T(8,128)(2,1)} %get-tuple-element.41), channel_id=1, source_target_pairs={{0,2},{1,3},{2,0},{3,1},{4,6},{5,7},{6,4},{7,5},{8,10},{9,11},{10,... | collective-permute-start | bytes 737288 | tf_op jit(solution)/shard_map/ppermute | solution.py:277
  138.9 15.9 %collective-permute-start.15 = (bf16[3,320,128]{2,1,0:T(8,128)(2,1)}, bf16[3,320,128]{2,1,0:T(8,128)(2,1)S(1)}, u32[]{:S(2)}, u32[]{:S(2)}) collective-permute-start(bf16[3,320,128]{2,1,0:T(8,128)(2,1)} %get-tuple-element.42), channel_id=1, source_target_pairs={{0,3},{1,2},{2,1},{3,0},{4,7},{5,6},{6,5},{7,4},{8,11},{9,10},{10,... | collective-permute-start | bytes 737288 | tf_op jit(solution)/shard_map/ppermute | solution.py:277
  140.1 1.3 collective-permute-start.8
  140.5 14.3 %copy-start.14 = (bf16[3,160,128]{2,1,0:T(8,128)(2,1)}, bf16[3,160,128]{2,1,0:T(8,128)(2,1)S(1)}, u32[]{:S(2)}) copy-start(bf16[3,160,128]{2,1,0:T(8,128)(2,1)S(1)} %collective-permute-done.10.refs_3_) | copy-start | bytes 368644
  140.5 14.3 %collective-permute-start.9 = (bf16[3,160,128]{2,1,0:T(8,128)(2,1)S(1)}, bf16[3,160,128]{2,1,0:T(8,128)(2,1)S(1)}, u32[]{:S(2)}, u32[]{:S(2)}) collective-permute-start(bf16[3,160,128]{2,1,0:T(8,128)(2,1)S(1)} %get-tuple-element.47), channel_id=1, source_target_pairs={{0,2},{1,3},{2,0},{3,1},{4,6},{5,7},{6,4},{7,5},{8,10},{9,11},{10,... | collective-permute-start | bytes 368648 | tf_op jit(solution)/shard_map/ppermute | solution.py:277
  141.5 13.3 %copy-start.15 = (bf16[3,160,128]{2,1,0:T(8,128)(2,1)}, bf16[3,160,128]{2,1,0:T(8,128)(2,1)S(1)}, u32[]{:S(2)}) copy-start(bf16[3,160,128]{2,1,0:T(8,128)(2,1)S(1)} %collective-permute-done.8.refs_1_) | copy-start | bytes 368644
  154.8 0.8 copy-start.11
  154.8 0.8 copy-start.12
  154.8 0.9 copy-start.13
  (2 other events, 1.3 us)
Sparse Core Ops, SparseCore 0:
  12.4 88.1 reduce-scatter.1

commit v2 on v1

v2 whole, which is shorter than its diff:
```python
import functools
import math

import jax
import jax.numpy as jnp
from jax import lax
from jax.experimental import pallas as pl
from jax.experimental.pallas import tpu as pltpu
from jax.sharding import PartitionSpec as P

HEAD = 64
REACH = 3
SCALE = 0.125
NEGATIVE = -1e30
GROUP = 4
LANES = 128
CHUNK = 256
WINDOW = 8

VMEM_SPEC = pl.BlockSpec(memory_space=pltpu.VMEM)
SMEM_SPEC = pl.BlockSpec(memory_space=pltpu.SMEM)
ANY_SPEC = pl.BlockSpec(memory_space=pl.ANY)
PARAMS = pltpu.CompilerParams(vmem_limit_bytes=56 * 1024 * 1024)


MICROS = {
    "pack_kv": 2.5,
    "pack_qd": 11,
    "last": 2,
    "fold": 2,
    "halo": 2.5,
    "attention": 14,
    "sum": 2.5,
    "unpack": 3,
}


def kernel_call(*args, micros, **options):
    cost = pl.CostEstimate(flops=int(micros * 1.1e9), bytes_accessed=0, transcendentals=0)
    return pl.pallas_call(*args, cost_estimate=cost, **options)


def lanes_below(shape):
    return lax.broadcasted_iota(jnp.int32, shape, len(shape) - 1) < HEAD


def pair_slab(left, right, head):
    columns = slice(head // 2 * LANES, (head // 2 + 1) * LANES)
    a, b = left[:, columns], right[:, columns]
    if head % 2:
        a = pltpu.roll(a, HEAD, 1)
    else:
        b = pltpu.roll(b, HEAD, 1)
    return jnp.where(lanes_below(a.shape), a, b)


def send_pieces(pieces, outs, sem, me):
    copies = []
    for target in range(GROUP):
        for slot in range(GROUP):
            copy = pltpu.make_async_copy(pieces.at[target], outs[slot], sem.at[target])
            copies.append((jnp.bitwise_xor(me, slot) == target, copy))
    for cond, copy in copies:
        pl.when(cond)(copy.start)
    for cond, copy in copies:
        pl.when(cond)(copy.wait)


def pack_kv_kernel(heads, me_ref, k_ref, v_ref, *rest):
    outs, (pieces, sem) = rest[:GROUP], rest[GROUP:]
    per = heads // GROUP
    for target in range(GROUP):
        for head in range(per):
            pieces[target, head] = pair_slab(k_ref, v_ref, target * per + head)
    send_pieces(pieces, outs, sem, me_ref[0])


def pack_qd_kernel(heads, count, me_ref, q_ref, grad_ref, w_ref, o_ref, *rest):
    outs, rest = rest[:GROUP], rest[GROUP:]
    if count:
        weight_part(count, me_ref[1], o_ref, grad_ref, *rest[:2], rest[-1])
        rest = rest[2:-1]
    pieces, sem, attn = rest
    per = heads // GROUP
    tokens = q_ref.shape[0]
    lanes_up = -(-tokens // LANES) * LANES
    grad_attn = lax.dot_general(
        grad_ref[...], w_ref[...], (((1,), (1,)), ((), ())), preferred_element_type=jnp.float32
    ).astype(jnp.bfloat16)
    attn[...] = grad_attn
    product = grad_attn.astype(jnp.float32) * o_ref[...].astype(jnp.float32)
    lane = lax.broadcasted_iota(jnp.int32, (tokens, LANES), 1)
    for target in range(GROUP):
        columns = jnp.zeros((tokens, LANES), jnp.float32)
        for head in range(per):
            full = target * per + head
            pieces[target, head * tokens : (head + 1) * tokens] = pair_slab(q_ref, attn, full)
            dot = jnp.sum(product[:, full * HEAD : (full + 1) * HEAD], axis=1, keepdims=True)
            high = dot.astype(jnp.bfloat16).astype(jnp.float32)
            columns = jnp.where(lane == 2 * head, high, columns)
            columns = jnp.where(lane == 2 * head + 1, dot - high, columns)
        rows = jnp.transpose(columns)[:16]
        rows = jnp.concatenate([rows, jnp.zeros((16, lanes_up - tokens), jnp.float32)], axis=1)
        rows = rows.astype(jnp.bfloat16)
        for block in range(lanes_up // LANES):
            start = per * tokens + 16 * block
            pieces[target, start : start + 16] = rows[:, block * LANES : (block + 1) * LANES]
    send_pieces(pieces, outs, sem, me_ref[0])


def halo_kernel(me_ref, *refs):
    received, (up_ref, down_ref) = refs[:GROUP], refs[GROUP:]
    for slot in range(GROUP):
        row = jnp.bitwise_xor(me_ref[0], slot)

        @pl.when(row >= GROUP - REACH)
        def _():
            up_ref[:, row - GROUP + REACH] = received[slot][...]

        @pl.when(row < REACH)
        def _():
            down_ref[:, row] = received[slot][...]


def attention_kernel(per, cols, first_head, scalars, *refs):
    kv_refs = refs[:GROUP]
    above_ref, below_ref = refs[GROUP : GROUP + 2]
    qd_refs = refs[GROUP + 2 : 2 * GROUP + 2]
    delta_refs = refs[2 * GROUP + 2 : 3 * GROUP + 2]
    to_above, to_below, own_ref, dq_ref = refs[3 * GROUP + 2 : 3 * GROUP + 6]
    k_buf, v_buf, q_buf, d_buf, s_buf, dp_buf, wds_buf, zq_buf, acc, dq_buf = refs[3 * GROUP + 6 :]
    me, first_row = scalars[0], scalars[1]
    head = first_head + pl.program_id(0)
    tokens = above_ref.shape[2]
    half = tokens // 2
    tile = tokens // cols
    rows_all = GROUP + 2 * REACH
    chunks = GROUP * tokens // CHUNK
    wide = WINDOW * tokens
    factor = SCALE * math.log2(math.e)
    bf16, f32 = jnp.bfloat16, jnp.float32
    zero = jnp.zeros((), bf16)

    lane = lax.broadcasted_iota(jnp.int32, (tokens, LANES), 1)
    low_half = lane < HEAD
    at = lane - HEAD
    col_of = lax.broadcasted_iota(jnp.int32, (tokens, LANES), 0) // tile
    col_hot = at == 16 + col_of
    col_bias = (at >= 16) & (at < 16 + cols) & (jnp.abs(at - 16 - col_of) > REACH)
    v_const = jnp.where((lane == 2 * head) | (lane == 2 * head + 1), -1.0, 0.0).astype(bf16)

    def put_kv(j, slab):
        place = pl.ds(pl.multiple_of(j * tokens, tokens), tokens)
        hot = jnp.where(col_hot | (at == j), 1.0, 0.0).astype(bf16)
        k_buf[place] = jnp.where(low_half, slab, hot)
        v_buf[place] = jnp.where(low_half, v_const, slab)

    for slot in range(GROUP):
        row = jnp.bitwise_xor(me, slot)
        put_kv(row + REACH, kv_refs[slot][0])
        here = first_row + row
        base = first_row - REACH
        low = jnp.maximum(scalars[2 + 2 * row], here - REACH) - base
        high = jnp.minimum(scalars[3 + 2 * row], here + REACH) - base
        bias = col_bias | ((at >= 0) & (at < rows_all) & ((at < low) | (at > high)))
        qd = qd_refs[slot][...]
        place = pl.ds(pl.multiple_of(row * tokens, tokens), tokens)
        q_buf[place] = jnp.where(low_half, qd, jnp.where(bias, NEGATIVE, 0.0).astype(bf16))
        blocks = -(-tokens // LANES)
        lines = [delta_refs[slot][16 * b : 16 * (b + 1)] for b in range(blocks)]
        lines = jnp.concatenate(lines, axis=1).astype(f32)
        lines = jnp.concatenate(
            [lines, jnp.zeros((LANES - 16, blocks * LANES), f32)], axis=0
        )
        d_buf[place] = jnp.where(low_half, jnp.transpose(lines)[:tokens].astype(bf16), qd)
    for row in range(REACH):
        put_kv(row, above_ref[0, row])
        put_kv(GROUP + REACH + row, below_ref[0, row])
    chunk_low = lax.broadcasted_iota(jnp.int32, (CHUNK, LANES), 1) < HEAD
    for chunk in range(chunks):
        place = slice(chunk * CHUNK, (chunk + 1) * CHUNK)
        zq_buf[chunk, :CHUNK] = jnp.where(chunk_low, zero, d_buf[place])
        zq_buf[chunk, CHUNK:] = jnp.where(chunk_low, q_buf[place], zero)
    acc[...] = jnp.zeros_like(acc)

    nt = (((1,), (1,)), ((), ()))
    tn = (((0,), (0,)), ((), ()))
    starts = [min(c * CHUNK // tokens, rows_all - WINDOW) for c in range(chunks)]
    spans = [slice(f * tokens, f * tokens + wide) for f in starts]
    places = [slice(c * CHUNK, (c + 1) * CHUNK) for c in range(chunks)]

    def products(c):
        s_buf[c % 2] = lax.dot_general(
            k_buf[spans[c]], q_buf[places[c]], nt, preferred_element_type=f32
        )
        dp_buf[c % 2] = lax.dot_general(
            v_buf[spans[c]], d_buf[places[c]], nt, preferred_element_type=f32
        )

    products(0)
    for c in range(chunks):
        if c + 1 < chunks:
            products(c + 1)
        s_ref, dp_ref, wds_ref = s_buf.at[c % 2], dp_buf.at[c % 2], wds_buf.at[c % 2]
        peak = jnp.full((8, CHUNK), NEGATIVE, f32)
        for first in range(0, wide, tokens):
            part = s_ref[first : first + tokens].reshape(tokens // 8, 8, CHUNK)
            peak = jnp.maximum(peak, jnp.max(part, axis=0))
        peak = jnp.max(peak, axis=0, keepdims=True)
        total = jnp.zeros((8, CHUNK), f32)
        for first in range(0, wide, tokens):
            p = jnp.exp2((s_ref[first : first + tokens] - peak) * factor)
            s_ref[first : first + tokens] = p
            total = total + jnp.sum(p.reshape(tokens // 8, 8, CHUNK), axis=0)
        inverse = 1.0 / jnp.sum(total, axis=0, keepdims=True)
        for first in range(0, wide, tokens):
            p = s_ref[first : first + tokens] * inverse
            wds_ref[first : first + tokens, :CHUNK] = p.astype(bf16)
            wds_ref[first : first + tokens, CHUNK:] = (
                p * dp_ref[first : first + tokens]
            ).astype(bf16)
        acc[spans[c]] += jnp.dot(wds_ref[...], zq_buf[c], preferred_element_type=f32)
        dq_buf[c] = lax.dot_general(
            k_buf[spans[c]], wds_ref[:, CHUNK:], tn, preferred_element_type=f32
        )

    grad_q = jnp.concatenate([jnp.transpose(dq_buf[c]) for c in range(chunks)], axis=0)
    grad_q = (SCALE * grad_q).astype(bf16)
    for row in range(REACH):
        last = GROUP + REACH + row
        to_above[0, row] = acc[row * tokens : (row + 1) * tokens].astype(bf16)
        to_below[0, row] = acc[last * tokens : (last + 1) * tokens].astype(bf16)
    for row in range(GROUP):
        own_ref[0, row] = acc[(REACH + row) * tokens : (REACH + row + 1) * tokens]
        dq = grad_q[row * tokens : (row + 1) * tokens]
        dq_ref[0, row] = jnp.where(low_half[:half], dq[:half], pltpu.roll(dq[half:], HEAD, 1))


def sum_kernel(me_ref, own_ref, above_ref, below_ref, dq_ref, *rest):
    outs, (pieces, sem) = rest[:GROUP], rest[GROUP:]
    tokens, half = own_ref.shape[2], dq_ref.shape[2]
    for head in range(own_ref.shape[0]):
        for row in range(GROUP):
            value = own_ref[head, row]
            if row < REACH:
                value = value + above_ref[head, row].astype(jnp.float32)
            if row >= GROUP - REACH:
                value = value + below_ref[head, row - GROUP + REACH].astype(jnp.float32)
            value = jnp.where(lanes_below(value.shape), value * SCALE, value)
            first = head * (tokens + half)
            pieces[row, first : first + tokens] = value.astype(jnp.bfloat16)
            pieces[row, first + tokens : first + tokens + half] = dq_ref[head, row]
    send_pieces(pieces, outs, sem, me_ref[0])


def unpack_kernel(split, me_ref, *refs):
    sets = len(split)
    parts, (q_out, k_out, v_out) = refs[: sets * GROUP], refs[sets * GROUP : sets * GROUP + 3]
    buffers, sem = refs[sets * GROUP + 3 : -1], refs[-1]
    me = me_ref[0]
    tokens = k_out.shape[0]
    half = tokens // 2
    per = sum(split)
    copies = []
    for at in range(sets):
        for slot in range(GROUP):
            source = jnp.bitwise_xor(me, slot)
            copies.append(
                pltpu.make_async_copy(
                    parts[at * GROUP + slot], buffers[at].at[source], sem.at[at, slot]
                )
            )
    for copy in copies:
        copy.start()
    for copy in copies:
        copy.wait()
    where = [(at, index) for at, number in enumerate(split) for index in range(number)]

    def piece(head):
        group, local = divmod(head, per)
        at, index = where[local]
        first = index * (tokens + half)
        return (
            buffers[at][group, first : first + tokens],
            buffers[at][group, first + tokens : first + tokens + half],
        )

    for pair in range(GROUP * per // 2):
        columns = slice(pair * LANES, (pair + 1) * LANES)
        (a, qa), (b, qb) = piece(2 * pair), piece(2 * pair + 1)
        below = lanes_below(qa.shape)
        q_out[:half, columns] = jnp.where(below, qa, pltpu.roll(qb, HEAD, 1))
        q_out[half:, columns] = jnp.where(below, pltpu.roll(qa, HEAD, 1), qb)
        below = lanes_below(a.shape)
        k_out[:, columns] = jnp.where(below, a, pltpu.roll(b, HEAD, 1))
        v_out[:, columns] = jnp.where(below, pltpu.roll(a, HEAD, 1), b)


def weight_part(count, at, o_ref, grad_ref, send_ref, left_ref, permuted):
    block = o_ref.shape[1] // count
    bits = count.bit_length() - 1
    order = [sum((i >> b & 1) << (bits - 1 - b) for b in range(bits)) for i in range(count)]
    for at_block, owner in enumerate(order):
        columns = slice(owner * block, (owner + 1) * block)
        permuted[:, at_block * block : (at_block + 1) * block] = o_ref[:, columns]
    rows = send_ref.shape[0]
    mine = at % 2
    send_ref[...] = outer(
        permuted[:, pl.ds(pl.multiple_of((1 - mine) * rows, rows), rows)], grad_ref[...]
    ).astype(send_ref.dtype)
    left_ref[...] = permuted[:, pl.ds(pl.multiple_of(mine * rows, rows), rows)]


def outer(left, right):
    return lax.dot_general(
        left, right, (((0,), (0,)), ((), ())), preferred_element_type=jnp.float32
    )


def second_kernel(at_ref, left_ref, grad_ref, received_ref, keep_ref, send_ref):
    rows = keep_ref.shape[0]
    mine = at_ref[0] // 2 % 2
    first, second = left_ref[:, :rows], left_ref[:, rows:]
    for other, out in ((1, send_ref), (0, keep_ref)):
        part = jnp.bitwise_xor(mine, other)
        place = pl.ds(pl.multiple_of(part * rows, rows), rows)
        left = jnp.where(part == 0, first, second)
        value = outer(left, grad_ref[...]) + received_ref[place].astype(jnp.float32)
        out[...] = value.astype(out.dtype)


def fold_kernel(bit, at_ref, kept_ref, received_ref, keep_ref, send_ref):
    rows = keep_ref.shape[0]
    mine = at_ref[0] // (1 << bit) % 2
    for other, out in ((1, send_ref), (0, keep_ref)):
        place = pl.ds(pl.multiple_of(jnp.bitwise_xor(mine, other) * rows, rows), rows)
        out[...] = (kept_ref[place] + received_ref[place].astype(jnp.float32)).astype(out.dtype)


def last_kernel(kept_ref, received_ref, out_ref):
    out_ref[...] = kept_ref[...] + received_ref[...].astype(jnp.float32)


def body(queries, keys, values, outputs, grad_out, w_out, bounds):
    own_rows, cols, tile, features = queries.shape
    tokens = own_rows * cols * tile
    half = tokens // 2
    heads = features // HEAD
    per = heads // GROUP
    count = lax.axis_size("row")
    assert own_rows == 1 and count % GROUP == 0 and heads % GROUP == 0
    bf16 = jnp.bfloat16
    position = lax.axis_index("row")
    me = (position % GROUP).astype(jnp.int32)
    first_row = position - me
    me_arr = me.reshape(1)
    q2, k2, v2, o2 = [x.reshape(tokens, features) for x in (queries, keys, values, outputs)]
    g2 = grad_out.reshape(tokens, -1)

    def exchange(pieces):
        result = [pieces[0]]
        for slot in range(1, GROUP):
            result.append(
                lax.ppermute(pieces[slot], "row", [(i, i ^ slot) for i in range(count)])
            )
        return result

    def shift(value, step):
        pairs = [(i, i + step) for i in range(count) if 0 <= i + step < count]
        return lax.ppermute(value, "row", pairs)

    def after(value, *others):
        return lax.optimization_barrier((value, *others))[0]

    piece = (per, tokens, LANES)
    kv = kernel_call(
        functools.partial(pack_kv_kernel, heads),
        out_shape=[jax.ShapeDtypeStruct(piece, bf16)] * GROUP,
        in_specs=[SMEM_SPEC, VMEM_SPEC, VMEM_SPEC],
        out_specs=[ANY_SPEC] * GROUP,
        scratch_shapes=[pltpu.VMEM((GROUP,) + piece, bf16), pltpu.SemaphoreType.DMA((GROUP,))],
        compiler_params=PARAMS,
        name="pack_kv",
            micros=MICROS["pack_kv"],
    )(me_arr, k2, v2)
    kv = exchange(kv)

    bits = count.bit_length() - 1
    halving = count == 1 << bits and features // count % 16 == 0
    shape = jax.ShapeDtypeStruct
    width = g2.shape[1]
    at_arr = position.astype(jnp.int32).reshape(1)

    def hop(sent, bit):
        return lax.ppermute(sent, "row", [(i, i ^ (1 << bit)) for i in range(count)])

    def halves(kernel, rows, bit, operands):
        return kernel_call(
            kernel,
            out_shape=[shape((rows, width), jnp.float32), shape((rows, width), bf16)],
            in_specs=[SMEM_SPEC] + [VMEM_SPEC] * (len(operands) - 1),
            out_specs=[VMEM_SPEC] * 2,
            compiler_params=PARAMS,
            name="fold",
            micros=MICROS["fold"],
        )(*operands)

    def fold(bit, kept, sent, other):
        operands = (after(at_arr, other), kept, hop(sent, bit))
        return halves(functools.partial(fold_kernel, bit + 1), kept.shape[0] // 2, bit, operands)

    qd_rows = per * tokens + 16 * (-(-tokens // LANES))
    rows = features // 2
    made = kernel_call(
        functools.partial(pack_qd_kernel, heads, count if halving else 0),
        out_shape=[shape((qd_rows, LANES), bf16)] * GROUP
        + [shape((rows, width), bf16), shape((tokens, rows), bf16)] * halving,
        in_specs=[SMEM_SPEC] + [VMEM_SPEC] * 4,
        out_specs=[ANY_SPEC] * GROUP + [VMEM_SPEC] * (2 * halving),
        scratch_shapes=[
            pltpu.VMEM((GROUP, qd_rows, LANES), bf16),
            pltpu.SemaphoreType.DMA((GROUP,)),
            pltpu.VMEM((tokens, features), bf16),
        ]
        + [pltpu.VMEM((tokens, features), bf16)] * halving,
        compiler_params=PARAMS,
        name="pack_qd",
        micros=MICROS["pack_qd"],
    )(after(jnp.concatenate([me_arr, at_arr]), kv[1]), q2, g2, w_out, o2)
    qd = made[:GROUP]
    if halving:
        sent, left = made[GROUP:]
    qd_sent = qd[1]
    qd = exchange(qd)

    groups = [number for number in (per - 1, 1) if number]
    window = (REACH, tokens, LANES)
    borders = kernel_call(
        halo_kernel,
        out_shape=[shape((per,) + window, bf16)] * 2,
        in_specs=[SMEM_SPEC] + [VMEM_SPEC] * GROUP,
        out_specs=[VMEM_SPEC] * 2,
        compiler_params=PARAMS,
        name="halo",
        micros=MICROS["halo"],
    )(after(me_arr, qd_sent), *kv)

    if halving:
        kept, sent = halves(
            second_kernel, features // 4, 0, (after(at_arr, borders[0]), left, g2, hop(after(sent, borders[0]), 0))
        )
    folds = 1
    limits = lax.dynamic_slice_in_dim(bounds, first_row, GROUP, 0).reshape(-1)
    scalars = jnp.concatenate([me_arr, first_row.reshape(1), limits])
    rows_all = GROUP + 2 * REACH
    chunks = GROUP * tokens // CHUNK
    delta_rows = qd_rows - per * tokens
    results = []
    head = 0
    ready = []
    above = shift(borders[0], GROUP)
    below = shift(borders[1], -GROUP)
    for number in groups:
        if halving:
            scalars = after(scalars, kept)
        here = lambda i: (i, 0, 0, 0)
        result = kernel_call(
            functools.partial(attention_kernel, per, cols, head),
            grid=(number,),
            out_shape=[
                shape((number,) + window, bf16),
                shape((number,) + window, bf16),
                shape((number, GROUP, tokens, LANES), jnp.float32),
                shape((number, GROUP, half, LANES), bf16),
            ],
            in_specs=[SMEM_SPEC]
            + [pl.BlockSpec((1, tokens, LANES), lambda i, head=head: (head + i, 0, 0))] * GROUP
            + [pl.BlockSpec((1,) + window, lambda i, head=head: (head + i, 0, 0, 0))] * 2
            + [pl.BlockSpec((tokens, LANES), lambda i, head=head: (head + i, 0))] * GROUP
            + [pl.BlockSpec((delta_rows, LANES), lambda i: (per * tokens // delta_rows, 0))]
            * GROUP,
            out_specs=[
                pl.BlockSpec((1,) + window, here),
                pl.BlockSpec((1,) + window, here),
                pl.BlockSpec((1, GROUP, tokens, LANES), here),
                pl.BlockSpec((1, GROUP, half, LANES), here),
            ],
            scratch_shapes=[pltpu.VMEM((rows_all * tokens, LANES), bf16)] * 2
            + [pltpu.VMEM((GROUP * tokens, LANES), bf16)] * 2
            + [
                pltpu.VMEM((2, WINDOW * tokens, CHUNK), jnp.float32),
                pltpu.VMEM((2, WINDOW * tokens, CHUNK), jnp.float32),
                pltpu.VMEM((2, WINDOW * tokens, 2 * CHUNK), bf16),
                pltpu.VMEM((chunks, 2 * CHUNK, LANES), bf16),
                pltpu.VMEM((rows_all * tokens, LANES), jnp.float32),
                pltpu.VMEM((chunks, LANES, CHUNK), jnp.float32),
            ],
            compiler_params=PARAMS,
            name="attention",
            micros=MICROS["attention"] * number,
        )(scalars, *kv, above, below, *qd, *qd)
        results.append(result)
        head += number
        if halving and folds < bits - 1:
            kept, sent = fold(folds, kept, sent, result[2])
            folds += 1

    if halving:
        while folds < bits - 1:
            kept, sent = fold(folds, kept, sent, results[-1][2])
            folds += 1
        ready = [kept]
    returned = []
    turn = after(me_arr, results[-1][2], *ready)
    for number, (to_above, to_below, own, dq) in zip(groups, results):
        size = (number * (tokens + half), LANES)
        pieces = kernel_call(
            sum_kernel,
            out_shape=[shape(size, bf16)] * GROUP,
            in_specs=[SMEM_SPEC] + [VMEM_SPEC] * 4,
            out_specs=[ANY_SPEC] * GROUP,
            scratch_shapes=[pltpu.VMEM((GROUP,) + size, bf16), pltpu.SemaphoreType.DMA((GROUP,))],
            compiler_params=PARAMS,
            name="sum",
            micros=MICROS["sum"],
        )(turn, own, shift(to_below, GROUP), shift(to_above, -GROUP), dq)
        returned += exchange(pieces)
        turn = after(me_arr, returned[3])

    if halving:
        grad_w_out = kernel_call(
            last_kernel,
            out_shape=shape(kept.shape, jnp.float32),
            in_specs=[VMEM_SPEC] * 2,
            out_specs=VMEM_SPEC,
            name="last",
            micros=MICROS["last"],
        )(after(kept, pieces[0]), hop(sent, bits - 1))
    else:
        grad_w_out = lax.psum_scatter(
            lax.dot_general(o2, g2, (((0,), (0,)), ((), ())), preferred_element_type=jnp.float32),
            "row",
            scatter_dimension=0,
            tiled=True,
        )

    grads = kernel_call(
        functools.partial(unpack_kernel, groups),
        out_shape=[shape((tokens, features), bf16)] * 3,
        in_specs=[SMEM_SPEC] + [ANY_SPEC] * (len(groups) * GROUP),
        out_specs=[VMEM_SPEC] * 3,
        scratch_shapes=[
            pltpu.VMEM((GROUP, number * (tokens + half), LANES), bf16) for number in groups
        ]
        + [pltpu.SemaphoreType.DMA((len(groups), GROUP))],
        compiler_params=PARAMS,
        name="unpack",
            micros=MICROS["unpack"],
    )(after(me_arr, grad_w_out), *returned)
    grads = [x.reshape(queries.shape) for x in grads]
    return (*grads, grad_w_out)


def solution(mesh):
    placed = P(("groups", "row"), None, None, None)
    return jax.shard_map(
        body,
        mesh=mesh,
        in_specs=(placed, placed, placed, placed, placed, P(), P("groups", None)),
        out_specs=(placed, placed, placed, P(("groups", "row"), None)),
        check_vma=False,
    )
```

time: 166 us -> 133 us (0.80)
  waiting for transfers between devices: 64.8 us -> 18.2 us
  starting transfers between devices: 18.4 us -> 34.5 us
  Pallas kernels: 56.9 us -> 70.9 us
  between operations: 14.3 us -> 1.12 us
  matrix products: 4.91 us -> 0 us
    ppermute x12, waiting for transfers between devices: 47.6 us -> 10.9 us  [exchange(): lax.ppermute(pieces[slot], 'row', [(i, i ^ slot) for i in range(count)])]
    pallas_call x6 -> x12, Pallas kernels: 56.9 us -> 70.9 us  [the longest x2 38.6 us: body(): kernel_call(functools.partial(attention_kernel, per, cols, head), grid=(n...]
    ppermute x4 -> x6, waiting for transfers between devices: 17.2 us -> 4.02 us  [shift(): return lax.ppermute(value, 'row', pairs)]
    ppermute x0 -> x4, starting transfers between devices: none -> 9.83 us  [hop(): return lax.ppermute(sent, 'row', [(i, i ^ 1 << bit) for i in range(count)])]
    ppermute x4 -> x6, starting transfers between devices: 10.4 us -> 15.9 us  [shift(): return lax.ppermute(value, 'row', pairs)]
    dot_general x1 -> x0, matrix products: 4.91 us -> none  [body(): lax.dot_general(o2, g2, (((0,), (0,)), ((), ())), preferred_element_type=...]
    ppermute x0 -> x4, waiting for transfers between devices: none -> 3.27 us  [hop(): return lax.ppermute(sent, 'row', [(i, i ^ 1 << bit) for i in range(count)])]
    squeeze x1 -> x0, local copies, waits for them, and re-layouts: 1.76 us -> none  [spread(): lax.dynamic_index_in_dim(rows, jnp.bitwise_xor(me, slot), 0, keepdims=False)]
  transfers between devices with their start and end apart: 17 -> 22, of which waited for: 8 -> 7; matrix products, arithmetic and copies ran while one was open for 2% -> 1% of each run, Pallas kernels for 34% -> 45%
where the time goes in v2:
time: 133 us; the launch traced here: 132 us
  Pallas kernels  70.9 us (53%)
  starting transfers between devices  34.5 us (26%)
  waiting for transfers between devices  18.2 us (14%)
  local copies, waits for them, and re-layouts  5.47 us (4%)
  other arithmetic  1.39 us (1%)
    pallas_call x2, Pallas kernels, body(): kernel_call(functools.partial(attention_kernel, per, cols, head), grid=(n...  38.6 us
    ppermute x6, starting transfers between devices, shift(): return lax.ppermute(value, 'row', pairs)  15.9 us
    ppermute x12, waiting for transfers between devices, exchange(): lax.ppermute(pieces[slot], 'row', [(i, i ^ slot) for i in range(count)])  10.9 us
    ppermute x4, starting transfers between devices, hop(): return lax.ppermute(sent, 'row', [(i, i ^ 1 << bit) for i in range(count)])  9.83 us
    pallas_call x1, Pallas kernels, body(): kernel_call(functools.partial(pack_qd_kernel, heads, count if halving els...  9.3 us
    ppermute x12, starting transfers between devices, exchange(): lax.ppermute(pieces[slot], 'row', [(i, i ^ slot) for i in range(count)])  8.84 us
    pallas_call x3, Pallas kernels, halves(): kernel_call(kernel, out_shape=[shape((rows, width), jnp.float32), shape((...  7.98 us
    unnamed x54, local copies, waits for them, and re-layouts  5.22 us
  transfers between devices with their start and end apart: 22, of which 7 were waited for; matrix products, arithmetic and copies ran while one was open for 1% of the time, Pallas kernels for 45%

profile of v2, /device:TPU:0, one launch (start us, length us, event | category | flops | bytes accessed | tf_op | source)
XLA Modules:
  0.0 131.6 jit_solution(7073547037461367316)
XLA Ops:
  0.7 2.5 %pack_kv.1 = (bf16[3,320,128]{2,1,0:T(8,128)(2,1)}, bf16[3,320,128]{2,1,0:T(8,128)(2,1)}, bf16[3,320,128]{2,1,0:T(8,128)(2,1)}, bf16[3,320,128]{2,1,0:T(8,128)(2,1)}) custom-call(s32[1]{0:T(128)} %bitcast.me_ref, bf16[320,768]{1,0:T(8,128)(2,1)} %bitcast.13, bf16[320,768]{1,0:T(8,128)(2,1)} %bitcast.14), custom_call_target="tpu_custom_call" | custom-call | flops 2750000128 | tf_op jit(solution)/shard_map/pack_kv/pallas_call | solution.py:376
  3.7 2.6 %collective-permute-start.1 = (bf16[3,320,128]{2,1,0:T(8,128)(2,1)}, bf16[3,320,128]{2,1,0:T(8,128)(2,1)S(1)}, u32[]{:S(2)}, u32[]{:S(2)}) collective-permute-start(bf16[3,320,128]{2,1,0:T(8,128)(2,1)} %get-tuple-element.58), channel_id=1, source_target_pairs={{0,2},{1,3},{2,0},{3,1},{4,6},{5,7},{6,4},{7,5},{8,10},{9,11},{10,... | collective-permute-start | bytes 737288 | tf_op jit(solution)/shard_map/ppermute | solution.py:364
  6.9 9.3 %pack_qd.1 = (bf16[1008,128]{1,0:T(8,128)(2,1)}, bf16[1008,128]{1,0:T(8,128)(2,1)}, bf16[1008,128]{1,0:T(8,128)(2,1)}, bf16[1008,128]{1,0:T(8,128)(2,1)}, bf16[3...) custom-call(s32[2]{0:T(128)} %pad_add_fusion.1.me_ref, bf16[320,768]{1,0:T(8,128)(2,1)} %bitcast.15, ...), custom_call_target="tpu_custom_call" | custom-call | flops 12099999744 | tf_op jit(solution)/shard_map/pack_qd/pallas_call | solution.py:414
  16.3 1.7 %collective-permute-done.2.refs_3_ = bf16[3,320,128]{2,1,0:T(8,128)(2,1)S(1)} collective-permute-done((bf16[3,320,128]{2,1,0:T(8,128)(2,1)}, bf16[3,320,128]{2,1,0:T(8,128)(2,1)S(1)}, u32[]{:S(2)}, u32[]{:S(2)}) %collective-permute-start.2) | collective-permute-done | bytes 245792 | tf_op jit(solution)/shard_map/ppermute | solution.py:364
  18.7 2.7 %halo.1 = (bf16[3,3,320,128]{3,2,1,0:T(8,128)(2,1)}, bf16[3,3,320,128]{3,2,1,0:T(8,128)(2,1)}) custom-call(s32[1]{0:T(128)} %bitcast.me_ref, bf16[3,320,128]{2,1,0:T(8,128)(2,1)} %get-tuple-element.57.refs_0_, bf16[3,320,128]{2,1,0:T(8,128)(2,1)} %copy-done.12, bf16[3,320,128]{2,1,0:T(8,128)(2,1)} %copy-done.13, bf16[3,320,128]{2,1,0:T(8,128)(2,1)} %copy-done.14), custom_call_target="tpu_custom_call" | custom-call | flops 2750000128 | tf_op jit(solution)/shard_map/halo/pallas_call | solution.py:438
  21.5 1.3 collective-permute-start.5
  22.8 5.5 %collective-permute-start.4 = (bf16[3,3,320,128]{3,2,1,0:T(8,128)(2,1)}, bf16[3,3,320,128]{3,2,1,0:T(8,128)(2,1)}, u32[]{:S(2)}, u32[]{:S(2)}) collective-permute-start(bf16[3,3,320,128]{3,2,1,0:T(8,128)(2,1)} %get-tuple-element.60), channel_id=1, source_target_pairs={{0,4},{1,5},{2,6},{3,7},{4,8},{5,9},{6,10},{7,11},{8,12},{9,13},{1... | collective-permute-start | bytes 2211848 | tf_op jit(solution)/shard_map/ppermute | solution.py:370
  28.5 1.8 %collective-permute-start.7 = (bf16[1008,128]{1,0:T(8,128)(2,1)}, bf16[1008,128]{1,0:T(8,128)(2,1)S(1)}, u32[]{:S(2)}, u32[]{:S(2)}) collective-permute-start(bf16[1008,128]{1,0:T(8,128)(2,1)} %get-tuple-element.69), channel_id=1, source_target_pairs={{0,2},{1,3},{2,0},{3,1},{4,6},{5,7},{6,4},{7,5},{8,10},{9,11},{10,... | collective-permute-start | bytes 774152 | tf_op jit(solution)/shard_map/ppermute | solution.py:364
  31.3 3.6 %fold.3 = (f32[192,1536]{1,0:T(8,128)}, bf16[192,1536]{1,0:T(8,128)(2,1)}) custom-call(s32[1]{0:T(128)} %bitcast.1.at_ref, bf16[320,384]{1,0:T(8,128)(2,1)} %get-tuple-element.62.left_ref, bf16[320,1536]{1,0:T(8,128)(2,1)} %bitcast.12, bf16[384,1536]{1,0:T(8,128)(2,1)} %copy-done.2), custom_call_target="tpu_custom_call" | custom-call | flops 2200000000 | tf_op jit(solution)/shard_map/fold/pallas_call | solution.py:398
  35.0 2.9 %collective-permute-done.7.refs_8_.refs_12_ = bf16[1008,128]{1,0:T(8,128)(2,1)S(1)} collective-permute-done((bf16[1008,128]{1,0:T(8,128)(2,1)}, bf16[1008,128]{1,0:T(8,128)(2,1)S(1)}, u32[]{:S(2)}, u32[]{:S(2)}) %collective-permute-start.7) | collective-permute-done | bytes 258080 | tf_op jit(solution)/shard_map/ppermute | solution.py:364
  37.8 1.7 %collective-permute-start.9 = (bf16[192,1536]{1,0:T(8,128)(2,1)}, bf16[192,1536]{1,0:T(8,128)(2,1)S(1)}, u32[]{:S(2)}, u32[]{:S(2)}) collective-permute-start(bf16[192,1536]{1,0:T(8,128)(2,1)} %get-tuple-element.73), channel_id=1, source_target_pairs={{0,2},{1,3},{2,0},{3,1},{4,6},{5,7},{6,4},{7,5},{8,10},{9,11},{10,... | collective-permute-start | bytes 1769480 | tf_op jit(solution)/shard_map/ppermute | solution.py:395
  39.5 3.2 %collective-permute-done.8.refs_9_.refs_13_ = bf16[1008,128]{1,0:T(8,128)(2,1)S(1)} collective-permute-done((bf16[1008,128]{1,0:T(8,128)(2,1)}, bf16[1008,128]{1,0:T(8,128)(2,1)S(1)}, u32[]{:S(2)}, u32[]{:S(2)}) %collective-permute-start.8) | collective-permute-done | bytes 258080 | tf_op jit(solution)/shard_map/ppermute | solution.py:364
  42.7 1.0 collective-permute-done.4.refs_4_
  43.7 25.0 %attention.2 = (bf16[2,3,320,128]{3,2,1,0:T(8,128)(2,1)}, bf16[2,3,320,128]{3,2,1,0:T(8,128)(2,1)}, f32[2,4,320,128]{3,2,1,0:T(8,128)}, bf16[2,4,160,128]{3,2,1,0:T(8,128)(2,1)}) custom-call(s32[10]{0:T(128)} %pad_add_fusion.scalars, bf16[3,320,128]{2,1,0:T(8,128)(2,1)} %get-tuple-element.57.refs_0_, bf16[3,320,128]{2,1,0:T(8,128)(2,1)} %copy-done.12, ...), custom_call_target="tpu_custom_call" | custom-call | flops 30799998976 | tf_op jit(solution)/shard_map/attention/pallas_call | solution.py:467
  68.8 4.4 %collective-permute-start.11 = (bf16[2,3,320,128]{3,2,1,0:T(8,128)(2,1)}, bf16[2,3,320,128]{3,2,1,0:T(8,128)(2,1)S(1)}, u32[]{:S(2)}, u32[]{:S(2)}) collective-permute-start(bf16[2,3,320,128]{3,2,1,0:T(8,128)(2,1)} %get-tuple-element.81), channel_id=1, source_target_pairs={{0,4},{1,5},{2,6},{3,7},{4,8},{5,9},{6,10},{7,11},{8,12},{9,13},{1... | collective-permute-start | bytes 1474568 | tf_op jit(solution)/shard_map/ppermute | solution.py:370
  73.2 1.5 %collective-permute-start.12 = (bf16[2,3,320,128]{3,2,1,0:T(8,128)(2,1)}, bf16[2,3,320,128]{3,2,1,0:T(8,128)(2,1)S(1)}, u32[]{:S(2)}, u32[]{:S(2)}) collective-permute-start(bf16[2,3,320,128]{3,2,1,0:T(8,128)(2,1)} %get-tuple-element.82), channel_id=1, source_target_pairs={{4,0},{5,1},{6,2},{7,3},{8,4},{9,5},{10,6},{11,7},{12,8},{13,9},{1... | collective-permute-start | bytes 1474568 | tf_op jit(solution)/shard_map/ppermute | solution.py:370
  74.7 0.8 copy-done.4
  75.6 2.4 %fold.4 = (f32[96,1536]{1,0:T(8,128)}, bf16[96,1536]{1,0:T(8,128)(2,1)}) custom-call(s32[1]{0:T(128)} %bitcast.1.at_ref, f32[192,1536]{1,0:T(8,128)} %get-tuple-element.65.kept_ref, bf16[192,1536]{1,0:T(8,128)(2,1)} %copy-done.4), custom_call_target="tpu_custom_call" | custom-call | flops 2200000000 | tf_op jit(solution)/shard_map/fold/pallas_call | solution.py:398
  78.0 2.6 %collective-permute-start.10 = (bf16[96,1536]{1,0:T(8,128)(2,1)}, bf16[96,1536]{1,0:T(8,128)(2,1)S(1)}, u32[]{:S(2)}, u32[]{:S(2)}) collective-permute-start(bf16[96,1536]{1,0:T(8,128)(2,1)} %get-tuple-element.78), channel_id=1, source_target_pairs={{0,4},{1,5},{2,6},{3,7},{4,0},{5,1},{6,2},{7,3},{8,12},{9,13},{10,... | collective-permute-start | bytes 884744 | tf_op jit(solution)/shard_map/ppermute | solution.py:395
  80.6 13.6 %attention.3 = (bf16[1,3,320,128]{3,2,1,0:T(8,128)(2,1)}, bf16[1,3,320,128]{3,2,1,0:T(8,128)(2,1)}, f32[1,4,320,128]{3,2,1,0:T(8,128)}, bf16[1,4,160,128]{3,2,1,0:T(8,128)(2,1)}) custom-call(s32[10]{0:T(128)} %pad_add_fusion.scalars, bf16[3,320,128]{2,1,0:T(8,128)(2,1)} %get-tuple-element.57.refs_0_, bf16[3,320,128]{2,1,0:T(8,128)(2,1)} %copy-done.12, ...), custom_call_target="tpu_custom_call" | custom-call | flops 15399999488 | tf_op jit(solution)/shard_map/attention/pallas_call | solution.py:467
  94.9 1.9 %fold.5 = (f32[48,1536]{1,0:T(8,128)}, bf16[48,1536]{1,0:T(8,128)(2,1)}) custom-call(s32[1]{0:T(128)} %bitcast.1.at_ref, f32[96,1536]{1,0:T(8,128)} %get-tuple-element.74.kept_ref, bf16[96,1536]{1,0:T(8,128)(2,1)} %copy-done.7), custom_call_target="tpu_custom_call" | custom-call | flops 2200000000 | tf_op jit(solution)/shard_map/fold/pallas_call | solution.py:398
  97.8 2.9 %sum.2 = (bf16[960,128]{1,0:T(8,128)(2,1)}, bf16[960,128]{1,0:T(8,128)(2,1)}, bf16[960,128]{1,0:T(8,128)(2,1)}, bf16[960,128]{1,0:T(8,128)(2,1)}) custom-call(s32[1]{0:T(128)} %bitcast.me_ref, f32[2,4,320,128]{3,2,1,0:T(8,128)} %get-tuple-element.71.own_ref, bf16[2,3,320,128]{3,2,1,0:T(8,128)(2,1)} %copy-done.5, bf16[2,3,320,128]{3,2,1,0:T(8,128)(2,1)} %copy-done.6, ...), custom_call_target="tpu_custom_call" | custom-call | flops 2750000128 | tf_op jit(solution)/shard_map/sum/pallas_call | solution.py:517
  100.8 1.9 %collective-permute-start.14 = (bf16[1,3,320,128]{3,2,1,0:T(8,128)(2,1)S(1)}, bf16[1,3,320,128]{3,2,1,0:T(8,128)(2,1)S(1)}, u32[]{:S(2)}, u32[]{:S(2)}) collective-permute-start(bf16[1,3,320,128]{3,2,1,0:T(8,128)(2,1)S(1)} %copy-done.18), channel_id=1, source_target_pairs={{0,4},{1,5},{2,6},{3,7},{4,8},{5,9},{6,10},{7,11},{8,12},{9,13},{1... | collective-permute-start | bytes 737288 | tf_op jit(solution)/shard_map/ppermute | solution.py:370
  102.8 1.3 collective-permute-start.15
  104.1 5.4 %collective-permute-start.16 = (bf16[48,1536]{1,0:T(8,128)(2,1)S(1)}, bf16[48,1536]{1,0:T(8,128)(2,1)S(1)}, u32[]{:S(2)}, u32[]{:S(2)}) collective-permute-start(bf16[48,1536]{1,0:T(8,128)(2,1)S(1)} %copy-done.22), channel_id=1, source_target_pairs={{0,8},{1,9},{2,10},{3,11},{4,12},{5,13},{6,14},{7,15},{8,0},{9,1},... | collective-permute-start | bytes 442376 | tf_op jit(solution)/shard_map/ppermute | solution.py:395
  111.1 3.1 %collective-permute-done.15.below_ref = bf16[1,3,320,128]{3,2,1,0:T(8,128)(2,1)S(1)} collective-permute-done((bf16[1,3,320,128]{3,2,1,0:T(8,128)(2,1)S(1)}, bf16[1,3,320,128]{3,2,1,0:T(8,128)(2,1)S(1)}, u32[]{:S(2)}, u32[]{:S(2)}) %collective-permute-start.15) | collective-permute-done | bytes 245792 | tf_op jit(solution)/shard_map/ppermute | solution.py:370
  114.8 2.2 %sum.3 = (bf16[480,128]{1,0:T(8,128)(2,1)}, bf16[480,128]{1,0:T(8,128)(2,1)}, bf16[480,128]{1,0:T(8,128)(2,1)}, bf16[480,128]{1,0:T(8,128)(2,1)}) custom-call(s32[1]{0:T(128)} %bitcast.me_ref, f32[1,4,320,128]{3,2,1,0:T(8,128)} %get-tuple-element.76.own_ref, bf16[1,3,320,128]{3,2,1,0:T(8,128)(2,1)} %copy-done.20, bf16[1,3,320,128]{3,2,1,0:T(8,128)(2,1)} %copy-done.21, ...), custom_call_target="tpu_custom_call" | custom-call | flops 2750000128 | tf_op jit(solution)/shard_map/sum/pallas_call | solution.py:517
  117.8 1.1 collective-permute-start.20
  118.9 3.3 %collective-permute-done.16.received_ref = bf16[48,1536]{1,0:T(8,128)(2,1)S(1)} collective-permute-done((bf16[48,1536]{1,0:T(8,128)(2,1)S(1)}, bf16[48,1536]{1,0:T(8,128)(2,1)S(1)}, u32[]{:S(2)}, u32[]{:S(2)}) %collective-permute-start.16) | collective-permute-done | bytes 147488 | tf_op jit(solution)/shard_map/ppermute | solution.py:395
  122.9 1.7 %last.1 = f32[48,1536]{1,0:T(8,128)} custom-call(f32[48,1536]{1,0:T(8,128)} %get-tuple-element.90.kept_ref, bf16[48,1536]{1,0:T(8,128)(2,1)} %copy-done.23), custom_call_target="tpu_custom_call" | custom-call | flops 2200000000 | tf_op jit(solution)/shard_map/last/pallas_call | solution.py:531
  124.7 3.1 %collective-permute-done.21.refs_7_ = bf16[480,128]{1,0:T(8,128)(2,1)S(1)} collective-permute-done((bf16[480,128]{1,0:T(8,128)(2,1)}, bf16[480,128]{1,0:T(8,128)(2,1)S(1)}, u32[]{:S(2)}, u32[]{:S(2)}) %collective-permute-start.21) | collective-permute-done | bytes 122912 | tf_op jit(solution)/shard_map/ppermute | solution.py:364
  128.4 3.0 %unpack.1 = (bf16[320,768]{1,0:T(8,128)(2,1)}, bf16[320,768]{1,0:T(8,128)(2,1)}, bf16[320,768]{1,0:T(8,128)(2,1)}) custom-call(s32[1]{0:T(128)} %bitcast.me_ref, bf16[960,128]{1,0:T(8,128)(2,1)} %get-tuple-element.93.refs_0_, bf16[960,128]{1,0:T(8,128)(2,1)} %copy-done.17, bf16[960,128]{1,0:T(8,128)(2,1)} %copy-done.19, bf16[960,128]{1,0:T(8,128)(2,1)} %copy-done.15, ...), custom_call_target="tpu_custom_call" | custom-call | flops 3300000000 | tf_op jit(solution)/shard_map/unpack/pallas_call | solution.py:547
  (83 shorter events, 9.6 us)
Async XLA Ops:
  0.6 27.6 %copy-start = (s32[16,2]{0,1:T(2,128)S(1)}, s32[16,2]{0,1:T(2,128)}, u32[]{:S(2)}) copy-start(s32[16,2]{0,1:T(2,128)} %param.13) | copy-start | bytes 388
  3.1 3.8 %collective-permute-start = (bf16[3,320,128]{2,1,0:T(8,128)(2,1)}, bf16[3,320,128]{2,1,0:T(8,128)(2,1)S(1)}, u32[]{:S(2)}, u32[]{:S(2)}) collective-permute-start(bf16[3,320,128]{2,1,0:T(8,128)(2,1)} %get-tuple-element.53), channel_id=1, source_target_pairs={{0,1},{1,0},{2,3},{3,2},{4,5},{5,4},{6,7},{7,6},{8,9},{9,8},{10,11... | collective-permute-start | bytes 737288 | tf_op jit(solution)/shard_map/ppermute | solution.py:364
  3.7 12.6 %collective-permute-start.1 = (bf16[3,320,128]{2,1,0:T(8,128)(2,1)}, bf16[3,320,128]{2,1,0:T(8,128)(2,1)S(1)}, u32[]{:S(2)}, u32[]{:S(2)}) collective-permute-start(bf16[3,320,128]{2,1,0:T(8,128)(2,1)} %get-tuple-element.58), channel_id=1, source_target_pairs={{0,2},{1,3},{2,0},{3,1},{4,6},{5,7},{6,4},{7,5},{8,10},{9,11},{10,... | collective-permute-start | bytes 737288 | tf_op jit(solution)/shard_map/ppermute | solution.py:364
  6.2 11.8 %collective-permute-start.2 = (bf16[3,320,128]{2,1,0:T(8,128)(2,1)}, bf16[3,320,128]{2,1,0:T(8,128)(2,1)S(1)}, u32[]{:S(2)}, u32[]{:S(2)}) collective-permute-start(bf16[3,320,128]{2,1,0:T(8,128)(2,1)} %get-tuple-element.59), channel_id=1, source_target_pairs={{0,3},{1,2},{2,1},{3,0},{4,7},{5,6},{6,5},{7,4},{8,11},{9,10},{10,... | collective-permute-start | bytes 737288 | tf_op jit(solution)/shard_map/ppermute | solution.py:364
  6.9 9.3 %copy-start.12 = (bf16[3,320,128]{2,1,0:T(8,128)(2,1)}, bf16[3,320,128]{2,1,0:T(8,128)(2,1)S(1)}, u32[]{:S(2)}) copy-start(bf16[3,320,128]{2,1,0:T(8,128)(2,1)S(1)} %collective-permute-done.refs_1_) | copy-start | bytes 737284
  18.7 9.8 %copy-start.10 = (bf16[1008,128]{1,0:T(8,128)(2,1)S(1)}, bf16[1008,128]{1,0:T(8,128)(2,1)}, u32[]{:S(2)}) copy-start(bf16[1008,128]{1,0:T(8,128)(2,1)} %get-tuple-element.55) | copy-start | bytes 774148
  21.4 8.9 %collective-permute-start.3 = (bf16[384,1536]{1,0:T(8,128)(2,1)S(1)}, bf16[384,1536]{1,0:T(8,128)(2,1)S(1)}, u32[]{:S(2)}, u32[]{:S(2)}) collective-permute-start(bf16[384,1536]{1,0:T(8,128)(2,1)S(1)} %copy-done.1), channel_id=1, source_target_pairs={{0,1},{1,0},{2,3},{3,2},{4,5},{5,4},{6,7},{7,6},{8,9},{9,8},{10,11... | collective-permute-start | bytes 3538952 | tf_op jit(solution)/shard_map/ppermute | solution.py:395
  21.5 21.2 %collective-permute-start.5 = (bf16[3,3,320,128]{3,2,1,0:T(8,128)(2,1)}, bf16[3,3,320,128]{3,2,1,0:T(8,128)(2,1)S(1)}, u32[]{:S(2)}, u32[]{:S(2)}) collective-permute-start(bf16[3,3,320,128]{3,2,1,0:T(8,128)(2,1)} %get-tuple-element.67), channel_id=1, source_target_pairs={{4,0},{5,1},{6,2},{7,3},{8,4},{9,5},{10,6},{11,7},{12,8},{13,9},{1... | collective-permute-start | bytes 2211848 | tf_op jit(solution)/shard_map/ppermute | solution.py:370
  22.8 20.9 %collective-permute-start.4 = (bf16[3,3,320,128]{3,2,1,0:T(8,128)(2,1)}, bf16[3,3,320,128]{3,2,1,0:T(8,128)(2,1)}, u32[]{:S(2)}, u32[]{:S(2)}) collective-permute-start(bf16[3,3,320,128]{3,2,1,0:T(8,128)(2,1)} %get-tuple-element.60), channel_id=1, source_target_pairs={{0,4},{1,5},{2,6},{3,7},{4,8},{5,9},{6,10},{7,11},{8,12},{9,13},{1... | collective-permute-start | bytes 2211848 | tf_op jit(solution)/shard_map/ppermute | solution.py:370
  28.5 14.2 %collective-permute-start.6 = (bf16[1008,128]{1,0:T(8,128)(2,1)S(1)}, bf16[1008,128]{1,0:T(8,128)(2,1)S(1)}, u32[]{:S(2)}, u32[]{:S(2)}) collective-permute-start(bf16[1008,128]{1,0:T(8,128)(2,1)S(1)} %copy-done.10), channel_id=1, source_target_pairs={{0,1},{1,0},{2,3},{3,2},{4,5},{5,4},{6,7},{7,6},{8,9},{9,8},{10,11... | collective-permute-start | bytes 774152 | tf_op jit(solution)/shard_map/ppermute | solution.py:364
  28.5 9.3 %collective-permute-start.7 = (bf16[1008,128]{1,0:T(8,128)(2,1)}, bf16[1008,128]{1,0:T(8,128)(2,1)S(1)}, u32[]{:S(2)}, u32[]{:S(2)}) collective-permute-start(bf16[1008,128]{1,0:T(8,128)(2,1)} %get-tuple-element.69), channel_id=1, source_target_pairs={{0,2},{1,3},{2,0},{3,1},{4,6},{5,7},{6,4},{7,5},{8,10},{9,11},{10,... | collective-permute-start | bytes 774152 | tf_op jit(solution)/shard_map/ppermute | solution.py:364
  30.3 12.4 %collective-permute-start.8 = (bf16[1008,128]{1,0:T(8,128)(2,1)}, bf16[1008,128]{1,0:T(8,128)(2,1)S(1)}, u32[]{:S(2)}, u32[]{:S(2)}) collective-permute-start(bf16[1008,128]{1,0:T(8,128)(2,1)} %get-tuple-element.70), channel_id=1, source_target_pairs={{0,3},{1,2},{2,1},{3,0},{4,7},{5,6},{6,5},{7,4},{8,11},{9,10},{10,... | collective-permute-start | bytes 774152 | tf_op jit(solution)/shard_map/ppermute | solution.py:364
  37.8 5.8 %copy-start.9 = (bf16[1008,128]{1,0:T(8,128)(2,1)}, bf16[1008,128]{1,0:T(8,128)(2,1)S(1)}, u32[]{:S(2)}) copy-start(bf16[1008,128]{1,0:T(8,128)(2,1)S(1)} %collective-permute-done.7.refs_8_.refs_12_) | copy-start | bytes 774148
  37.8 36.9 %collective-permute-start.9 = (bf16[192,1536]{1,0:T(8,128)(2,1)}, bf16[192,1536]{1,0:T(8,128)(2,1)S(1)}, u32[]{:S(2)}, u32[]{:S(2)}) collective-permute-start(bf16[192,1536]{1,0:T(8,128)(2,1)} %get-tuple-element.73), channel_id=1, source_target_pairs={{0,2},{1,3},{2,0},{3,1},{4,6},{5,7},{6,4},{7,5},{8,10},{9,11},{10,... | collective-permute-start | bytes 1769480 | tf_op jit(solution)/shard_map/ppermute | solution.py:395
  68.8 28.1 %collective-permute-start.11 = (bf16[2,3,320,128]{3,2,1,0:T(8,128)(2,1)}, bf16[2,3,320,128]{3,2,1,0:T(8,128)(2,1)S(1)}, u32[]{:S(2)}, u32[]{:S(2)}) collective-permute-start(bf16[2,3,320,128]{3,2,1,0:T(8,128)(2,1)} %get-tuple-element.81), channel_id=1, source_target_pairs={{0,4},{1,5},{2,6},{3,7},{4,8},{5,9},{6,10},{7,11},{8,12},{9,13},{1... | collective-permute-start | bytes 1474568 | tf_op jit(solution)/shard_map/ppermute | solution.py:370
  73.2 23.7 %collective-permute-start.12 = (bf16[2,3,320,128]{3,2,1,0:T(8,128)(2,1)}, bf16[2,3,320,128]{3,2,1,0:T(8,128)(2,1)S(1)}, u32[]{:S(2)}, u32[]{:S(2)}) collective-permute-start(bf16[2,3,320,128]{3,2,1,0:T(8,128)(2,1)} %get-tuple-element.82), channel_id=1, source_target_pairs={{4,0},{5,1},{6,2},{7,3},{8,4},{9,5},{10,6},{11,7},{12,8},{13,9},{1... | collective-permute-start | bytes 1474568 | tf_op jit(solution)/shard_map/ppermute | solution.py:370
  78.0 16.2 %collective-permute-start.10 = (bf16[96,1536]{1,0:T(8,128)(2,1)}, bf16[96,1536]{1,0:T(8,128)(2,1)S(1)}, u32[]{:S(2)}, u32[]{:S(2)}) collective-permute-start(bf16[96,1536]{1,0:T(8,128)(2,1)} %get-tuple-element.78), channel_id=1, source_target_pairs={{0,4},{1,5},{2,6},{3,7},{4,0},{5,1},{6,2},{7,3},{8,12},{9,13},{10,... | collective-permute-start | bytes 884744 | tf_op jit(solution)/shard_map/ppermute | solution.py:395
  97.8 5.0 %copy-start.16 = (bf16[1,3,320,128]{3,2,1,0:T(8,128)(2,1)S(1)}, bf16[1,3,320,128]{3,2,1,0:T(8,128)(2,1)}, u32[]{:S(2)}) copy-start(bf16[1,3,320,128]{3,2,1,0:T(8,128)(2,1)} %get-tuple-element.87) | copy-start | bytes 737284
  97.8 6.3 %copy-start.22 = (bf16[48,1536]{1,0:T(8,128)(2,1)S(1)}, bf16[48,1536]{1,0:T(8,128)(2,1)}, u32[]{:S(2)}) copy-start(bf16[48,1536]{1,0:T(8,128)(2,1)} %get-tuple-element.91) | copy-start | bytes 442372
  100.7 9.5 %collective-permute-start.13 = (bf16[960,128]{1,0:T(8,128)(2,1)}, bf16[960,128]{1,0:T(8,128)(2,1)S(1)}, u32[]{:S(2)}, u32[]{:S(2)}) collective-permute-start(bf16[960,128]{1,0:T(8,128)(2,1)} %get-tuple-element.84), channel_id=1, source_target_pairs={{0,3},{1,2},{2,1},{3,0},{4,7},{5,6},{6,5},{7,4},{8,11},{9,10},{10,... | collective-permute-start | bytes 737288 | tf_op jit(solution)/shard_map/ppermute | solution.py:364
  100.8 10.2 %collective-permute-start.14 = (bf16[1,3,320,128]{3,2,1,0:T(8,128)(2,1)S(1)}, bf16[1,3,320,128]{3,2,1,0:T(8,128)(2,1)S(1)}, u32[]{:S(2)}, u32[]{:S(2)}) collective-permute-start(bf16[1,3,320,128]{3,2,1,0:T(8,128)(2,1)S(1)} %copy-done.18), channel_id=1, source_target_pairs={{0,4},{1,5},{2,6},{3,7},{4,8},{5,9},{6,10},{7,11},{8,12},{9,13},{1... | collective-permute-start | bytes 737288 | tf_op jit(solution)/shard_map/ppermute | solution.py:370
  102.8 11.3 %collective-permute-start.15 = (bf16[1,3,320,128]{3,2,1,0:T(8,128)(2,1)S(1)}, bf16[1,3,320,128]{3,2,1,0:T(8,128)(2,1)S(1)}, u32[]{:S(2)}, u32[]{:S(2)}) collective-permute-start(bf16[1,3,320,128]{3,2,1,0:T(8,128)(2,1)S(1)} %copy-done.16), channel_id=1, source_target_pairs={{4,0},{5,1},{6,2},{7,3},{8,4},{9,5},{10,6},{11,7},{12,8},{13,9},{1... | collective-permute-start | bytes 737288 | tf_op jit(solution)/shard_map/ppermute | solution.py:370
  104.1 18.1 %collective-permute-start.16 = (bf16[48,1536]{1,0:T(8,128)(2,1)S(1)}, bf16[48,1536]{1,0:T(8,128)(2,1)S(1)}, u32[]{:S(2)}, u32[]{:S(2)}) collective-permute-start(bf16[48,1536]{1,0:T(8,128)(2,1)S(1)} %copy-done.22), channel_id=1, source_target_pairs={{0,8},{1,9},{2,10},{3,11},{4,12},{5,13},{6,14},{7,15},{8,0},{9,1},... | collective-permute-start | bytes 442376 | tf_op jit(solution)/shard_map/ppermute | solution.py:395
  109.5 15.2 %collective-permute-start.17 = (bf16[960,128]{1,0:T(8,128)(2,1)}, bf16[960,128]{1,0:T(8,128)(2,1)S(1)}, u32[]{:S(2)}, u32[]{:S(2)}) collective-permute-start(bf16[960,128]{1,0:T(8,128)(2,1)} %get-tuple-element.94), channel_id=1, source_target_pairs={{0,1},{1,0},{2,3},{3,2},{4,5},{5,4},{6,7},{7,6},{8,9},{9,8},{10,11... | collective-permute-start | bytes 737288 | tf_op jit(solution)/shard_map/ppermute | solution.py:364
  110.2 6.8 %copy-start.15 = (bf16[960,128]{1,0:T(8,128)(2,1)}, bf16[960,128]{1,0:T(8,128)(2,1)S(1)}, u32[]{:S(2)}) copy-start(bf16[960,128]{1,0:T(8,128)(2,1)S(1)} %collective-permute-done.13.refs_3_) | copy-start | bytes 737284
  110.2 14.4 %collective-permute-start.18 = (bf16[960,128]{1,0:T(8,128)(2,1)}, bf16[960,128]{1,0:T(8,128)(2,1)S(1)}, u32[]{:S(2)}, u32[]{:S(2)}) collective-permute-start(bf16[960,128]{1,0:T(8,128)(2,1)} %get-tuple-element.95), channel_id=1, source_target_pairs={{0,2},{1,3},{2,0},{3,1},{4,6},{5,7},{6,4},{7,5},{8,10},{9,11},{10,... | collective-permute-start | bytes 737288 | tf_op jit(solution)/shard_map/ppermute | solution.py:364
  117.1 7.6 %collective-permute-start.19 = (bf16[480,128]{1,0:T(8,128)(2,1)}, bf16[480,128]{1,0:T(8,128)(2,1)S(1)}, u32[]{:S(2)}, u32[]{:S(2)}) collective-permute-start(bf16[480,128]{1,0:T(8,128)(2,1)} %get-tuple-element.96), channel_id=1, source_target_pairs={{0,1},{1,0},{2,3},{3,2},{4,5},{5,4},{6,7},{7,6},{8,9},{9,8},{10,11... | collective-permute-start | bytes 368648 | tf_op jit(solution)/shard_map/ppermute | solution.py:364
  117.8 6.8 %collective-permute-start.20 = (bf16[480,128]{1,0:T(8,128)(2,1)}, bf16[480,128]{1,0:T(8,128)(2,1)S(1)}, u32[]{:S(2)}, u32[]{:S(2)}) collective-permute-start(bf16[480,128]{1,0:T(8,128)(2,1)} %get-tuple-element.97), channel_id=1, source_target_pairs={{0,2},{1,3},{2,0},{3,1},{4,6},{5,7},{6,4},{7,5},{8,10},{9,11},{10,... | collective-permute-start | bytes 368648 | tf_op jit(solution)/shard_map/ppermute | solution.py:364
  122.2 5.5 %collective-permute-start.21 = (bf16[480,128]{1,0:T(8,128)(2,1)}, bf16[480,128]{1,0:T(8,128)(2,1)S(1)}, u32[]{:S(2)}, u32[]{:S(2)}) collective-permute-start(bf16[480,128]{1,0:T(8,128)(2,1)} %get-tuple-element.98), channel_id=1, source_target_pairs={{0,3},{1,2},{2,1},{3,0},{4,7},{5,6},{6,5},{7,4},{8,11},{9,10},{10,... | collective-permute-start | bytes 368648 | tf_op jit(solution)/shard_map/ppermute | solution.py:364
  124.6 3.1 %copy-start.17 = (bf16[960,128]{1,0:T(8,128)(2,1)}, bf16[960,128]{1,0:T(8,128)(2,1)S(1)}, u32[]{:S(2)}) copy-start(bf16[960,128]{1,0:T(8,128)(2,1)S(1)} %collective-permute-done.17.refs_1_) | copy-start | bytes 737284
  124.6 3.1 %copy-start.19 = (bf16[960,128]{1,0:T(8,128)(2,1)}, bf16[960,128]{1,0:T(8,128)(2,1)S(1)}, u32[]{:S(2)}) copy-start(bf16[960,128]{1,0:T(8,128)(2,1)S(1)} %collective-permute-done.18.refs_2_) | copy-start | bytes 737284
  124.6 3.1 %copy-start.24 = (bf16[480,128]{1,0:T(8,128)(2,1)}, bf16[480,128]{1,0:T(8,128)(2,1)S(1)}, u32[]{:S(2)}) copy-start(bf16[480,128]{1,0:T(8,128)(2,1)S(1)} %collective-permute-done.19.refs_5_) | copy-start | bytes 368644
  (17 other events, 23.7 us)

commit v3 on v2

--- a/solution.py
+++ b/solution.py
@@ -20,7 +20,7 @@
 VMEM_SPEC = pl.BlockSpec(memory_space=pltpu.VMEM)
 SMEM_SPEC = pl.BlockSpec(memory_space=pltpu.SMEM)
 ANY_SPEC = pl.BlockSpec(memory_space=pl.ANY)
-PARAMS = pltpu.CompilerParams(vmem_limit_bytes=56 * 1024 * 1024)
+PARAMS = pltpu.CompilerParams(vmem_limit_bytes=40 * 1024 * 1024)
 
 
 MICROS = {
@@ -38,6 +38,10 @@
 def kernel_call(*args, micros, **options):
     cost = pl.CostEstimate(flops=int(micros * 1.1e9), bytes_accessed=0, transcendentals=0)
     return pl.pallas_call(*args, cost_estimate=cost, **options)
+
+
+def near(value):
+    return pltpu.with_memory_space_constraint(value, pltpu.VMEM)
 
 
 def lanes_below(shape):
@@ -126,9 +130,8 @@
     kv_refs = refs[:GROUP]
     above_ref, below_ref = refs[GROUP : GROUP + 2]
     qd_refs = refs[GROUP + 2 : 2 * GROUP + 2]
-    delta_refs = refs[2 * GROUP + 2 : 3 * GROUP + 2]
-    to_above, to_below, own_ref, dq_ref = refs[3 * GROUP + 2 : 3 * GROUP + 6]
-    k_buf, v_buf, q_buf, d_buf, s_buf, dp_buf, wds_buf, zq_buf, acc, dq_buf = refs[3 * GROUP + 6 :]
+    to_above, to_below, own_ref, dq_ref = refs[2 * GROUP + 2 : 2 * GROUP + 6]
+    k_buf, v_buf, q_buf, d_buf, s_buf, dp_buf, wds_buf, zq_buf, acc, dq_buf = refs[2 * GROUP + 6 :]
     me, first_row = scalars[0], scalars[1]
     head = first_head + pl.program_id(0)
     tokens = above_ref.shape[2]
@@ -157,25 +160,26 @@
 
     for slot in range(GROUP):
         row = jnp.bitwise_xor(me, slot)
-        put_kv(row + REACH, kv_refs[slot][0])
+        put_kv(row + REACH, kv_refs[slot][head])
         here = first_row + row
         base = first_row - REACH
         low = jnp.maximum(scalars[2 + 2 * row], here - REACH) - base
         high = jnp.minimum(scalars[3 + 2 * row], here + REACH) - base
         bias = col_bias | ((at >= 0) & (at < rows_all) & ((at < low) | (at > high)))
-        qd = qd_refs[slot][...]
+        qd = qd_refs[slot][pl.ds(pl.multiple_of(head * tokens, tokens), tokens)]
         place = pl.ds(pl.multiple_of(row * tokens, tokens), tokens)
         q_buf[place] = jnp.where(low_half, qd, jnp.where(bias, NEGATIVE, 0.0).astype(bf16))
         blocks = -(-tokens // LANES)
-        lines = [delta_refs[slot][16 * b : 16 * (b + 1)] for b in range(blocks)]
+        ends = [per * tokens + 16 * b for b in range(blocks)]
+        lines = [qd_refs[slot][end : end + 16] for end in ends]
         lines = jnp.concatenate(lines, axis=1).astype(f32)
         lines = jnp.concatenate(
             [lines, jnp.zeros((LANES - 16, blocks * LANES), f32)], axis=0
         )
         d_buf[place] = jnp.where(low_half, jnp.transpose(lines)[:tokens].astype(bf16), qd)
     for row in range(REACH):
-        put_kv(row, above_ref[0, row])
-        put_kv(GROUP + REACH + row, below_ref[0, row])
+        put_kv(row, above_ref[head, row])
+        put_kv(GROUP + REACH + row, below_ref[head, row])
     chunk_low = lax.broadcasted_iota(jnp.int32, (CHUNK, LANES), 1) < HEAD
     for chunk in range(chunks):
         place = slice(chunk * CHUNK, (chunk + 1) * CHUNK)
@@ -256,24 +260,14 @@
 def unpack_kernel(split, me_ref, *refs):
     sets = len(split)
     parts, (q_out, k_out, v_out) = refs[: sets * GROUP], refs[sets * GROUP : sets * GROUP + 3]
-    buffers, sem = refs[sets * GROUP + 3 : -1], refs[-1]
+    buffers = refs[sets * GROUP + 3 :]
     me = me_ref[0]
     tokens = k_out.shape[0]
     half = tokens // 2
     per = sum(split)
-    copies = []
     for at in range(sets):
         for slot in range(GROUP):
-            source = jnp.bitwise_xor(me, slot)
-            copies.append(
-                pltpu.make_async_copy(
-                    parts[at * GROUP + slot], buffers[at].at[source], sem.at[at, slot]
-                )
-            )
-    for copy in copies:
-        copy.start()
-    for copy in copies:
-        copy.wait()
+            buffers[at][jnp.bitwise_xor(me, slot)] = parts[at * GROUP + slot][...]
     where = [(at, index) for at, number in enumerate(split) for index in range(number)]
 
     def piece(head):
@@ -360,14 +354,13 @@
     def exchange(pieces):
         result = [pieces[0]]
         for slot in range(1, GROUP):
-            result.append(
-                lax.ppermute(pieces[slot], "row", [(i, i ^ slot) for i in range(count)])
-            )
+            pairs = [(i, i ^ slot) for i in range(count)]
+            result.append(near(lax.ppermute(pieces[slot], "row", pairs)))
         return result
 
     def shift(value, step):
         pairs = [(i, i + step) for i in range(count) if 0 <= i + step < count]
-        return lax.ppermute(value, "row", pairs)
+        return near(lax.ppermute(value, "row", pairs))
 
     def after(value, *others):
         return lax.optimization_barrier((value, *others))[0]
@@ -392,7 +385,7 @@
     at_arr = position.astype(jnp.int32).reshape(1)
 
     def hop(sent, bit):
-        return lax.ppermute(sent, "row", [(i, i ^ (1 << bit)) for i in range(count)])
+        return near(lax.ppermute(sent, "row", [(i, i ^ (1 << bit)) for i in range(count)]))
 
     def halves(kernel, rows, bit, operands):
         return kernel_call(
@@ -454,7 +447,6 @@
     scalars = jnp.concatenate([me_arr, first_row.reshape(1), limits])
     rows_all = GROUP + 2 * REACH
     chunks = GROUP * tokens // CHUNK
-    delta_rows = qd_rows - per * tokens
     results = []
     head = 0
     ready = []
@@ -473,12 +465,7 @@
                 shape((number, GROUP, tokens, LANES), jnp.float32),
                 shape((number, GROUP, half, LANES), bf16),
             ],
-            in_specs=[SMEM_SPEC]
-            + [pl.BlockSpec((1, tokens, LANES), lambda i, head=head: (head + i, 0, 0))] * GROUP
-            + [pl.BlockSpec((1,) + window, lambda i, head=head: (head + i, 0, 0, 0))] * 2
-            + [pl.BlockSpec((tokens, LANES), lambda i, head=head: (head + i, 0))] * GROUP
-            + [pl.BlockSpec((delta_rows, LANES), lambda i: (per * tokens // delta_rows, 0))]
-            * GROUP,
+            in_specs=[SMEM_SPEC] + [VMEM_SPEC] * (2 * GROUP + 2),
             out_specs=[
                 pl.BlockSpec((1,) + window, here),
                 pl.BlockSpec((1,) + window, here),
@@ -498,7 +485,7 @@
             compiler_params=PARAMS,
             name="attention",
             micros=MICROS["attention"] * number,
-        )(scalars, *kv, above, below, *qd, *qd)
+        )(scalars, *kv, above, below, *qd)
         results.append(result)
         head += number
         if halving and folds < bits - 1:
@@ -547,16 +534,15 @@
     grads = kernel_call(
         functools.partial(unpack_kernel, groups),
         out_shape=[shape((tokens, features), bf16)] * 3,
-        in_specs=[SMEM_SPEC] + [ANY_SPEC] * (len(groups) * GROUP),
+        in_specs=[SMEM_SPEC] + [VMEM_SPEC] * (len(groups) * GROUP),
         out_specs=[VMEM_SPEC] * 3,
         scratch_shapes=[
             pltpu.VMEM((GROUP, number * (tokens + half), LANES), bf16) for number in groups
-        ]
-        + [pltpu.SemaphoreType.DMA((len(groups), GROUP))],
+        ],
         compiler_params=PARAMS,
         name="unpack",
             micros=MICROS["unpack"],
-    )(after(me_arr, grad_w_out), *returned)
+    )(after(me_arr, grad_w_out), *[near(x) for x in returned])
     grads = [x.reshape(queries.shape) for x in grads]
     return (*grads, grad_w_out)
 

time: 133 us -> 123 us (0.925); the launches traced: 132 us -> 123 us
  Pallas kernels: 70.9 us -> 53.6 us
  waiting for transfers between devices: 18.2 us -> 28.9 us
  local copies, waits for them, and re-layouts: 5.47 us -> 4.05 us
    ppermute x22, waiting for transfers between devices: 18.2 us -> 28.9 us  [the longest x12 16.2 us: exchange(): result.append(near(lax.ppermute(pieces[slot], 'row', pairs)))]
    pallas_call x3, Pallas kernels: 7.98 us -> 1.11 us  [halves(): kernel_call(kernel, out_shape=[shape((rows, width), jnp.float32), shape((...]
    pallas_call x2, Pallas kernels: 5.17 us -> 2.51 us  [body(): kernel_call(sum_kernel, out_shape=[shape(size, bf16)] * GROUP, in_specs=[...]
    pallas_call x1, Pallas kernels: 9.3 us -> 6.91 us  [body(): kernel_call(functools.partial(pack_qd_kernel, heads, count if halving els...]
    pallas_call x2, Pallas kernels: 38.6 us -> 36.8 us  [body(): kernel_call(functools.partial(attention_kernel, per, cols, head), grid=(n...]
    pallas_call x1, Pallas kernels: 3.02 us -> 1.58 us  [body(): kernel_call(functools.partial(unpack_kernel, groups), out_shape=[shape((t...]
    unnamed x54 -> x46, local copies, waits for them, and re-layouts: 5.22 us -> 3.8 us
    pallas_call x1, Pallas kernels: 2.66 us -> 1.27 us  [body(): kernel_call(halo_kernel, out_shape=[shape((per,) + window, bf16)] * 2, in...]
  transfers between devices with their start and end apart: 22 -> 22, of which waited for: 7 -> 8; matrix products, arithmetic and copies ran while one was open for 1% -> 0% of each run, Pallas kernels for 45% -> 39%
where the time goes in v3:
time: 123 us
  Pallas kernels  53.6 us (44%)
  starting transfers between devices  35.3 us (29%)
  waiting for transfers between devices  28.9 us (23%)
  local copies, waits for them, and re-layouts  4.05 us (3%)
    pallas_call x2, Pallas kernels, body(): kernel_call(functools.partial(attention_kernel, per, cols, head), grid=(n...  36.8 us
    ppermute x12, waiting for transfers between devices, exchange(): result.append(near(lax.ppermute(pieces[slot], 'row', pairs)))  16.2 us
    ppermute x6, starting transfers between devices, shift(): return near(lax.ppermute(value, 'row', pairs))  15.4 us
    ppermute x4, starting transfers between devices, hop(): lax.ppermute(sent, 'row', [(i, i ^ 1 << bit) for i in range(count)])  11.1 us
    ppermute x12, starting transfers between devices, exchange(): result.append(near(lax.ppermute(pieces[slot], 'row', pairs)))  8.81 us
    ppermute x4, waiting for transfers between devices, hop(): lax.ppermute(sent, 'row', [(i, i ^ 1 << bit) for i in range(count)])  8.54 us
    pallas_call x1, Pallas kernels, body(): kernel_call(functools.partial(pack_qd_kernel, heads, count if halving els...  6.91 us
    ppermute x6, waiting for transfers between devices, shift(): return near(lax.ppermute(value, 'row', pairs))  4.2 us
  transfers between devices with their start and end apart: 22, of which 8 were waited for; matrix products, arithmetic and copies ran while one was open for 0% of the time, Pallas kernels for 39%

profile of v3, /device:TPU:0, one launch (start us, length us, event | category | flops | bytes accessed | tf_op | source)
XLA Modules:
  0.0 123.1 jit_solution(13632225040243589223)
XLA Ops:
  0.7 1.0 copy-done.3
  1.7 1.0 copy-done.4
  2.7 1.7 %pack_kv.1 = (bf16[3,320,128]{2,1,0:T(8,128)(2,1)S(1)}, bf16[3,320,128]{2,1,0:T(8,128)(2,1)S(1)}, bf16[3,320,128]{2,1,0:T(8,128)(2,1)S(1)}, bf16[3,320,128]{2,1,0:T(8,128)(2,1)S(1)}) custom-call(s32[1]{0:T(128)} %bitcast.me_ref, bf16[320,768]{1,0:T(8,128)(2,1)S(1)} %bitcast.13, bf16[320,768]{1,0:T(8,128)(2,1)S(1)} %bitcast.14), custom_call_target="tpu_custom_call" | custom-call | flops 2750000128 | tf_op jit(solution)/shard_map/pack_kv/pallas_call | solution.py:369
  5.0 2.6 %collective-permute-start.1 = (bf16[3,320,128]{2,1,0:T(8,128)(2,1)S(1)}, bf16[3,320,128]{2,1,0:T(8,128)(2,1)S(1)}, u32[]{:S(2)}, u32[]{:S(2)}) collective-permute-start(bf16[3,320,128]{2,1,0:T(8,128)(2,1)S(1)} %get-tuple-element.58), channel_id=1, source_target_pairs={{0,2},{1,3},{2,0},{3,1},{4,6},{5,7},{6,4},{7,5},{8,10},{9,11},{10,... | collective-permute-start | bytes 737288 | tf_op jit(solution)/shard_map/ppermute | solution.py:358
  7.7 6.9 %pack_qd.1 = (bf16[1008,128]{1,0:T(8,128)(2,1)S(1)}, bf16[1008,128]{1,0:T(8,128)(2,1)S(1)}, bf16[1008,128]{1,0:T(8,128)(2,1)S(1)}, bf16[1008,128]{1,0:T(8,128)(2...) custom-call(s32[2]{0:T(128)S(1)} %pad_add_fusion.1.me_ref, bf16[320,768]{1,0:T(8,128)(2,1)S(1)} %bitcast.15, ...), custom_call_target="tpu_custom_call" | custom-call | flops 12099999744 | tf_op jit(solution)/shard_map/pack_qd/pallas_call | solution.py:407
  14.7 4.4 %collective-permute-done.2.refs_3_ = bf16[3,320,128]{2,1,0:T(8,128)(2,1)S(1)} collective-permute-done((bf16[3,320,128]{2,1,0:T(8,128)(2,1)S(1)}, bf16[3,320,128]{2,1,0:T(8,128)(2,1)S(1)}, u32[]{:S(2)}, u32[]{:S(2)}) %collective-permute-start.2) | collective-permute-done | bytes 245792 | tf_op jit(solution)/shard_map/ppermute | solution.py:358
  19.1 1.3 %halo.1 = (bf16[3,3,320,128]{3,2,1,0:T(8,128)(2,1)}, bf16[3,3,320,128]{3,2,1,0:T(8,128)(2,1)}) custom-call(s32[1]{0:T(128)} %bitcast.me_ref, bf16[3,320,128]{2,1,0:T(8,128)(2,1)S(1)} %get-tuple-element.57.refs_0_, bf16[3,320,128]{2,1,0:T(8,128)(2,1)S(1)} %collective-permute-done.refs_1_, bf16[3,320,128]{2,1,0:T(8,128)(2,1)S(1)} %collective-permute-done.1.refs_2_, ...), custom_call_target="tpu_custom_call" | custom-call | flops 2750000128 | tf_op jit(solution)/shard_map/halo/pallas_call | solution.py:431
  20.6 1.3 %collective-permute-start.5 = (bf16[3,3,320,128]{3,2,1,0:T(8,128)(2,1)}, bf16[3,3,320,128]{3,2,1,0:T(8,128)(2,1)}, u32[]{:S(2)}, u32[]{:S(2)}) collective-permute-start(bf16[3,3,320,128]{3,2,1,0:T(8,128)(2,1)} %get-tuple-element.67), channel_id=1, source_target_pairs={{4,0},{5,1},{6,2},{7,3},{8,4},{9,5},{10,6},{11,7},{12,8},{13,9},{1... | collective-permute-start | bytes 2211848 | tf_op jit(solution)/shard_map/ppermute | solution.py:363
  21.9 5.5 %collective-permute-start.4 = (bf16[3,3,320,128]{3,2,1,0:T(8,128)(2,1)}, bf16[3,3,320,128]{3,2,1,0:T(8,128)(2,1)}, u32[]{:S(2)}, u32[]{:S(2)}) collective-permute-start(bf16[3,3,320,128]{3,2,1,0:T(8,128)(2,1)} %get-tuple-element.60), channel_id=1, source_target_pairs={{0,4},{1,5},{2,6},{3,7},{4,8},{5,9},{6,10},{7,11},{8,12},{9,13},{1... | collective-permute-start | bytes 2211848 | tf_op jit(solution)/shard_map/ppermute | solution.py:363
  27.7 1.8 %collective-permute-start.7 = (bf16[1008,128]{1,0:T(8,128)(2,1)}, bf16[1008,128]{1,0:T(8,128)(2,1)S(1)}, u32[]{:S(2)}, u32[]{:S(2)}) collective-permute-start(bf16[1008,128]{1,0:T(8,128)(2,1)} %copy-done.9), channel_id=1, source_target_pairs={{0,2},{1,3},{2,0},{3,1},{4,6},{5,7},{6,4},{7,5},{8,10},{9,11},{10,... | collective-permute-start | bytes 774152 | tf_op jit(solution)/shard_map/ppermute | solution.py:358
  29.6 0.9 copy-done.17
  30.6 0.9 fold.3
  31.5 5.4 %collective-permute-done.7.refs_8_ = bf16[1008,128]{1,0:T(8,128)(2,1)S(1)} collective-permute-done((bf16[1008,128]{1,0:T(8,128)(2,1)}, bf16[1008,128]{1,0:T(8,128)(2,1)S(1)}, u32[]{:S(2)}, u32[]{:S(2)}) %collective-permute-start.7) | collective-permute-done | bytes 258080 | tf_op jit(solution)/shard_map/ppermute | solution.py:358
  36.9 1.7 %collective-permute-start.9 = (bf16[192,1536]{1,0:T(8,128)(2,1)S(1)}, bf16[192,1536]{1,0:T(8,128)(2,1)S(1)}, u32[]{:S(2)}, u32[]{:S(2)}) collective-permute-start(bf16[192,1536]{1,0:T(8,128)(2,1)S(1)} %get-tuple-element.73), channel_id=1, source_target_pairs={{0,2},{1,3},{2,0},{3,1},{4,6},{5,7},{6,4},{7,5},{8,10},{9,11},{10,... | collective-permute-start | bytes 1769480 | tf_op jit(solution)/shard_map/ppermute | solution.py:388
  38.6 3.2 %collective-permute-done.8.refs_9_ = bf16[1008,128]{1,0:T(8,128)(2,1)S(1)} collective-permute-done((bf16[1008,128]{1,0:T(8,128)(2,1)}, bf16[1008,128]{1,0:T(8,128)(2,1)S(1)}, u32[]{:S(2)}, u32[]{:S(2)}) %collective-permute-start.8) | collective-permute-done | bytes 258080 | tf_op jit(solution)/shard_map/ppermute | solution.py:358
  41.8 1.0 collective-permute-done.4.refs_4_
  42.8 24.2 %attention.2 = (bf16[2,3,320,128]{3,2,1,0:T(8,128)(2,1)S(1)}, bf16[2,3,320,128]{3,2,1,0:T(8,128)(2,1)S(1)}, f32[2,4,320,128]{3,2,1,0:T(8,128)S(1)}, bf16[2,4,160,128]{3,2,1,0:T(8,128)(2,1)S(1)}) custom-call(s32[10]{0:T(128)S(1)} %pad_add_fusion.scalars, bf16[3,320,128]{2,1,0:T(8,128)(2,1)S(1)} %copy-done.20, bf16[3,320,128]{2,1,0:T(8,128)(2,1)S(1)} %copy-done.11, ...), custom_call_target="tpu_custom_call" | custom-call | flops 30799998976 | tf_op jit(solution)/shard_map/attention/pallas_call | solution.py:459
  67.0 4.4 %collective-permute-start.11 = (bf16[2,3,320,128]{3,2,1,0:T(8,128)(2,1)S(1)}, bf16[2,3,320,128]{3,2,1,0:T(8,128)(2,1)S(1)}, u32[]{:S(2)}, u32[]{:S(2)}) collective-permute-start(bf16[2,3,320,128]{3,2,1,0:T(8,128)(2,1)S(1)} %get-tuple-element.81), channel_id=1, source_target_pairs={{0,4},{1,5},{2,6},{3,7},{4,8},{5,9},{6,10},{7,11},{8,12},{9,13},{1... | collective-permute-start | bytes 1474568 | tf_op jit(solution)/shard_map/ppermute | solution.py:363
  71.5 1.5 %collective-permute-start.12 = (bf16[2,3,320,128]{3,2,1,0:T(8,128)(2,1)S(1)}, bf16[2,3,320,128]{3,2,1,0:T(8,128)(2,1)S(1)}, u32[]{:S(2)}, u32[]{:S(2)}) collective-permute-start(bf16[2,3,320,128]{3,2,1,0:T(8,128)(2,1)S(1)} %get-tuple-element.82), channel_id=1, source_target_pairs={{4,0},{5,1},{6,2},{7,3},{8,4},{9,5},{10,6},{11,7},{12,8},{13,9},{1... | collective-permute-start | bytes 1474568 | tf_op jit(solution)/shard_map/ppermute | solution.py:363
  73.1 2.7 %collective-permute-start.10 = (bf16[96,1536]{1,0:T(8,128)(2,1)S(1)}, bf16[96,1536]{1,0:T(8,128)(2,1)S(1)}, u32[]{:S(2)}, u32[]{:S(2)}) collective-permute-start(bf16[96,1536]{1,0:T(8,128)(2,1)S(1)} %get-tuple-element.78), channel_id=1, source_target_pairs={{0,4},{1,5},{2,6},{3,7},{4,0},{5,1},{6,2},{7,3},{8,12},{9,13},{10,... | collective-permute-start | bytes 884744 | tf_op jit(solution)/shard_map/ppermute | solution.py:388
  75.8 12.6 %attention.3 = (bf16[1,3,320,128]{3,2,1,0:T(8,128)(2,1)S(1)}, bf16[1,3,320,128]{3,2,1,0:T(8,128)(2,1)S(1)}, f32[1,4,320,128]{3,2,1,0:T(8,128)S(1)}, bf16[1,4,160,128]{3,2,1,0:T(8,128)(2,1)S(1)}) custom-call(s32[10]{0:T(128)S(1)} %pad_add_fusion.scalars, bf16[3,320,128]{2,1,0:T(8,128)(2,1)S(1)} %copy-done.20, bf16[3,320,128]{2,1,0:T(8,128)(2,1)S(1)} %copy-done.11, ...), custom_call_target="tpu_custom_call" | custom-call | flops 15399999488 | tf_op jit(solution)/shard_map/attention/pallas_call | solution.py:459
  88.5 3.3 %collective-permute-done.10.received_ref = bf16[96,1536]{1,0:T(8,128)(2,1)S(1)} collective-permute-done((bf16[96,1536]{1,0:T(8,128)(2,1)S(1)}, bf16[96,1536]{1,0:T(8,128)(2,1)S(1)}, u32[]{:S(2)}, u32[]{:S(2)}) %collective-permute-start.10) | collective-permute-done | bytes 294944 | tf_op jit(solution)/shard_map/ppermute | solution.py:388
  92.5 1.6 %sum.2 = (bf16[960,128]{1,0:T(8,128)(2,1)S(1)}, bf16[960,128]{1,0:T(8,128)(2,1)S(1)}, bf16[960,128]{1,0:T(8,128)(2,1)S(1)}, bf16[960,128]{1,0:T(8,128)(2,1)S(1)}) custom-call(s32[1]{0:T(128)} %bitcast.me_ref, f32[2,4,320,128]{3,2,1,0:T(8,128)S(1)} %get-tuple-element.71.own_ref, bf16[2,3,320,128]{3,2,1,0:T(8,128)(2,1)S(1)} %collective-permute-done.11.above_ref, ...), custom_call_target="tpu_custom_call" | custom-call | flops 2750000128 | tf_op jit(solution)/shard_map/sum/pallas_call | solution.py:504
  94.2 1.5 %collective-permute-start.14 = (bf16[1,3,320,128]{3,2,1,0:T(8,128)(2,1)S(1)}, bf16[1,3,320,128]{3,2,1,0:T(8,128)(2,1)S(1)}, u32[]{:S(2)}, u32[]{:S(2)}) collective-permute-start(bf16[1,3,320,128]{3,2,1,0:T(8,128)(2,1)S(1)} %get-tuple-element.86), channel_id=1, source_target_pairs={{0,4},{1,5},{2,6},{3,7},{4,8},{5,9},{6,10},{7,11},{8,12},{9,13},{1... | collective-permute-start | bytes 737288 | tf_op jit(solution)/shard_map/ppermute | solution.py:363
  95.7 1.3 %collective-permute-start.15 = (bf16[1,3,320,128]{3,2,1,0:T(8,128)(2,1)S(1)}, bf16[1,3,320,128]{3,2,1,0:T(8,128)(2,1)S(1)}, u32[]{:S(2)}, u32[]{:S(2)}) collective-permute-start(bf16[1,3,320,128]{3,2,1,0:T(8,128)(2,1)S(1)} %get-tuple-element.87), channel_id=1, source_target_pairs={{4,0},{5,1},{6,2},{7,3},{8,4},{9,5},{10,6},{11,7},{12,8},{13,9},{1... | collective-permute-start | bytes 737288 | tf_op jit(solution)/shard_map/ppermute | solution.py:363
  97.0 6.5 %collective-permute-start.16 = (bf16[48,1536]{1,0:T(8,128)(2,1)S(1)}, bf16[48,1536]{1,0:T(8,128)(2,1)S(1)}, u32[]{:S(2)}, u32[]{:S(2)}) collective-permute-start(bf16[48,1536]{1,0:T(8,128)(2,1)S(1)} %get-tuple-element.91), channel_id=1, source_target_pairs={{0,8},{1,9},{2,10},{3,11},{4,12},{5,13},{6,14},{7,15},{8,0},{9,1},... | collective-permute-start | bytes 442376 | tf_op jit(solution)/shard_map/ppermute | solution.py:388
  105.0 3.2 %collective-permute-done.15.below_ref = bf16[1,3,320,128]{3,2,1,0:T(8,128)(2,1)S(1)} collective-permute-done((bf16[1,3,320,128]{3,2,1,0:T(8,128)(2,1)S(1)}, bf16[1,3,320,128]{3,2,1,0:T(8,128)(2,1)S(1)}, u32[]{:S(2)}, u32[]{:S(2)}) %collective-permute-start.15) | collective-permute-done | bytes 245792 | tf_op jit(solution)/shard_map/ppermute | solution.py:363
  109.8 1.1 collective-permute-start.20
  111.0 5.2 %collective-permute-done.16.received_ref = bf16[48,1536]{1,0:T(8,128)(2,1)S(1)} collective-permute-done((bf16[48,1536]{1,0:T(8,128)(2,1)S(1)}, bf16[48,1536]{1,0:T(8,128)(2,1)S(1)}, u32[]{:S(2)}, u32[]{:S(2)}) %collective-permute-start.16) | collective-permute-done | bytes 147488 | tf_op jit(solution)/shard_map/ppermute | solution.py:388
  116.5 1.7 %last.1 = f32[48,1536]{1,0:T(8,128)} custom-call(f32[48,1536]{1,0:T(8,128)} %copy-done.18, bf16[48,1536]{1,0:T(8,128)(2,1)S(1)} %collective-permute-done.16.received_ref), custom_call_target="tpu_custom_call" | custom-call | flops 2200000000 | tf_op jit(solution)/shard_map/last/pallas_call | solution.py:518
  118.3 3.2 %collective-permute-done.21.refs_7_ = bf16[480,128]{1,0:T(8,128)(2,1)S(1)} collective-permute-done((bf16[480,128]{1,0:T(8,128)(2,1)S(1)}, bf16[480,128]{1,0:T(8,128)(2,1)S(1)}, u32[]{:S(2)}, u32[]{:S(2)}) %collective-permute-start.21) | collective-permute-done | bytes 122912 | tf_op jit(solution)/shard_map/ppermute | solution.py:358
  121.5 1.6 %unpack.1 = (bf16[320,768]{1,0:T(8,128)(2,1)}, bf16[320,768]{1,0:T(8,128)(2,1)}, bf16[320,768]{1,0:T(8,128)(2,1)}) custom-call(s32[1]{0:T(128)} %bitcast.me_ref, bf16[960,128]{1,0:T(8,128)(2,1)S(1)} %get-tuple-element.93.refs_0_, bf16[960,128]{1,0:T(8,128)(2,1)S(1)} %collective-permute-done.17.refs_1_, bf16[960,128]{1,0:T(8,128)(2,1)S(1)} %collective-permute-done.18.refs_2_, ...), custom_call_target="tpu_custom_call" | custom-call | flops 3300000000 | tf_op jit(solution)/shard_map/unpack/pallas_call | solution.py:534
  (75 shorter events, 5.8 us)
Async XLA Ops:
  0.6 26.8 %copy-start = (s32[16,2]{0,1:T(2,128)S(1)}, s32[16,2]{0,1:T(2,128)}, u32[]{:S(2)}) copy-start(s32[16,2]{0,1:T(2,128)} %param.13) | copy-start | bytes 388
  4.5 14.7 %copy-start.19 = (bf16[3,320,128]{2,1,0:T(8,128)(2,1)}, bf16[3,320,128]{2,1,0:T(8,128)(2,1)S(1)}, u32[]{:S(2)}) copy-start(bf16[3,320,128]{2,1,0:T(8,128)(2,1)S(1)} %get-tuple-element.57.refs_0_) | copy-start | bytes 737284
  4.5 3.3 %collective-permute-start = (bf16[3,320,128]{2,1,0:T(8,128)(2,1)S(1)}, bf16[3,320,128]{2,1,0:T(8,128)(2,1)S(1)}, u32[]{:S(2)}, u32[]{:S(2)}) collective-permute-start(bf16[3,320,128]{2,1,0:T(8,128)(2,1)S(1)} %get-tuple-element.53), channel_id=1, source_target_pairs={{0,1},{1,0},{2,3},{3,2},{4,5},{5,4},{6,7},{7,6},{8,9},{9,8},{10,11... | collective-permute-start | bytes 737288 | tf_op jit(solution)/shard_map/ppermute | solution.py:358
  5.0 9.8 %collective-permute-start.1 = (bf16[3,320,128]{2,1,0:T(8,128)(2,1)S(1)}, bf16[3,320,128]{2,1,0:T(8,128)(2,1)S(1)}, u32[]{:S(2)}, u32[]{:S(2)}) collective-permute-start(bf16[3,320,128]{2,1,0:T(8,128)(2,1)S(1)} %get-tuple-element.58), channel_id=1, source_target_pairs={{0,2},{1,3},{2,0},{3,1},{4,6},{5,7},{6,4},{7,5},{8,10},{9,11},{10,... | collective-permute-start | bytes 737288 | tf_op jit(solution)/shard_map/ppermute | solution.py:358
  7.6 11.6 %collective-permute-start.2 = (bf16[3,320,128]{2,1,0:T(8,128)(2,1)S(1)}, bf16[3,320,128]{2,1,0:T(8,128)(2,1)S(1)}, u32[]{:S(2)}, u32[]{:S(2)}) collective-permute-start(bf16[3,320,128]{2,1,0:T(8,128)(2,1)S(1)} %get-tuple-element.59), channel_id=1, source_target_pairs={{0,3},{1,2},{2,1},{3,0},{4,7},{5,6},{6,5},{7,4},{8,11},{9,10},{10,... | collective-permute-start | bytes 737288 | tf_op jit(solution)/shard_map/ppermute | solution.py:358
  7.7 11.4 %copy-start.10 = (bf16[3,320,128]{2,1,0:T(8,128)(2,1)}, bf16[3,320,128]{2,1,0:T(8,128)(2,1)S(1)}, u32[]{:S(2)}) copy-start(bf16[3,320,128]{2,1,0:T(8,128)(2,1)S(1)} %collective-permute-done.refs_1_) | copy-start | bytes 737284
  14.7 5.7 %copy-start.7 = (bf16[1008,128]{1,0:T(8,128)(2,1)}, bf16[1008,128]{1,0:T(8,128)(2,1)S(1)}, u32[]{:S(2)}) copy-start(bf16[1008,128]{1,0:T(8,128)(2,1)S(1)} %get-tuple-element.55) | copy-start | bytes 774148
  14.7 5.7 %copy-start.8 = (bf16[1008,128]{1,0:T(8,128)(2,1)}, bf16[1008,128]{1,0:T(8,128)(2,1)S(1)}, u32[]{:S(2)}) copy-start(bf16[1008,128]{1,0:T(8,128)(2,1)S(1)} %get-tuple-element.70) | copy-start | bytes 774148
  20.5 9.0 %collective-permute-start.3 = (bf16[384,1536]{1,0:T(8,128)(2,1)S(1)}, bf16[384,1536]{1,0:T(8,128)(2,1)S(1)}, u32[]{:S(2)}, u32[]{:S(2)}) collective-permute-start(bf16[384,1536]{1,0:T(8,128)(2,1)S(1)} %get-tuple-element.64), channel_id=1, source_target_pairs={{0,1},{1,0},{2,3},{3,2},{4,5},{5,4},{6,7},{7,6},{8,9},{9,8},{10,11... | collective-permute-start | bytes 3538952 | tf_op jit(solution)/shard_map/ppermute | solution.py:388
  20.6 21.2 %collective-permute-start.5 = (bf16[3,3,320,128]{3,2,1,0:T(8,128)(2,1)}, bf16[3,3,320,128]{3,2,1,0:T(8,128)(2,1)}, u32[]{:S(2)}, u32[]{:S(2)}) collective-permute-start(bf16[3,3,320,128]{3,2,1,0:T(8,128)(2,1)} %get-tuple-element.67), channel_id=1, source_target_pairs={{4,0},{5,1},{6,2},{7,3},{8,4},{9,5},{10,6},{11,7},{12,8},{13,9},{1... | collective-permute-start | bytes 2211848 | tf_op jit(solution)/shard_map/ppermute | solution.py:363
  21.9 20.9 %collective-permute-start.4 = (bf16[3,3,320,128]{3,2,1,0:T(8,128)(2,1)}, bf16[3,3,320,128]{3,2,1,0:T(8,128)(2,1)}, u32[]{:S(2)}, u32[]{:S(2)}) collective-permute-start(bf16[3,3,320,128]{3,2,1,0:T(8,128)(2,1)} %get-tuple-element.60), channel_id=1, source_target_pairs={{0,4},{1,5},{2,6},{3,7},{4,8},{5,9},{6,10},{7,11},{8,12},{9,13},{1... | collective-permute-start | bytes 2211848 | tf_op jit(solution)/shard_map/ppermute | solution.py:363
  27.7 14.1 %collective-permute-start.6 = (bf16[1008,128]{1,0:T(8,128)(2,1)}, bf16[1008,128]{1,0:T(8,128)(2,1)S(1)}, u32[]{:S(2)}, u32[]{:S(2)}) collective-permute-start(bf16[1008,128]{1,0:T(8,128)(2,1)} %copy-done.7), channel_id=1, source_target_pairs={{0,1},{1,0},{2,3},{3,2},{4,5},{5,4},{6,7},{7,6},{8,9},{9,8},{10,11... | collective-permute-start | bytes 774152 | tf_op jit(solution)/shard_map/ppermute | solution.py:358
  27.7 9.3 %collective-permute-start.7 = (bf16[1008,128]{1,0:T(8,128)(2,1)}, bf16[1008,128]{1,0:T(8,128)(2,1)S(1)}, u32[]{:S(2)}, u32[]{:S(2)}) collective-permute-start(bf16[1008,128]{1,0:T(8,128)(2,1)} %copy-done.9), channel_id=1, source_target_pairs={{0,2},{1,3},{2,0},{3,1},{4,6},{5,7},{6,4},{7,5},{8,10},{9,11},{10,... | collective-permute-start | bytes 774152 | tf_op jit(solution)/shard_map/ppermute | solution.py:358
  29.4 12.4 %collective-permute-start.8 = (bf16[1008,128]{1,0:T(8,128)(2,1)}, bf16[1008,128]{1,0:T(8,128)(2,1)S(1)}, u32[]{:S(2)}, u32[]{:S(2)}) collective-permute-start(bf16[1008,128]{1,0:T(8,128)(2,1)} %copy-done.8), channel_id=1, source_target_pairs={{0,3},{1,2},{2,1},{3,0},{4,7},{5,6},{6,5},{7,4},{8,11},{9,10},{10,... | collective-permute-start | bytes 774152 | tf_op jit(solution)/shard_map/ppermute | solution.py:358
  30.5 12.3 %copy-start.11 = (bf16[3,320,128]{2,1,0:T(8,128)(2,1)S(1)}, bf16[3,320,128]{2,1,0:T(8,128)(2,1)}, u32[]{:S(2)}) copy-start(bf16[3,320,128]{2,1,0:T(8,128)(2,1)} %copy-done.10) | copy-start | bytes 737284
  30.5 12.3 %copy-start.13 = (bf16[3,320,128]{2,1,0:T(8,128)(2,1)S(1)}, bf16[3,320,128]{2,1,0:T(8,128)(2,1)}, u32[]{:S(2)}) copy-start(bf16[3,320,128]{2,1,0:T(8,128)(2,1)} %copy-done.12) | copy-start | bytes 737284
  30.5 12.3 %copy-start.15 = (bf16[3,320,128]{2,1,0:T(8,128)(2,1)S(1)}, bf16[3,320,128]{2,1,0:T(8,128)(2,1)}, u32[]{:S(2)}) copy-start(bf16[3,320,128]{2,1,0:T(8,128)(2,1)} %copy-done.14) | copy-start | bytes 737284
  30.5 12.3 %copy-start.20 = (bf16[3,320,128]{2,1,0:T(8,128)(2,1)S(1)}, bf16[3,320,128]{2,1,0:T(8,128)(2,1)}, u32[]{:S(2)}) copy-start(bf16[3,320,128]{2,1,0:T(8,128)(2,1)} %copy-done.19) | copy-start | bytes 737284
  30.6 12.3 %copy-start.22 = (bf16[1008,128]{1,0:T(8,128)(2,1)S(1)}, bf16[1008,128]{1,0:T(8,128)(2,1)}, u32[]{:S(2)}) copy-start(bf16[1008,128]{1,0:T(8,128)(2,1)} %copy-done.21) | copy-start | bytes 774148
  36.9 36.0 %collective-permute-start.9 = (bf16[192,1536]{1,0:T(8,128)(2,1)S(1)}, bf16[192,1536]{1,0:T(8,128)(2,1)S(1)}, u32[]{:S(2)}, u32[]{:S(2)}) collective-permute-start(bf16[192,1536]{1,0:T(8,128)(2,1)S(1)} %get-tuple-element.73), channel_id=1, source_target_pairs={{0,2},{1,3},{2,0},{3,1},{4,6},{5,7},{6,4},{7,5},{8,10},{9,11},{10,... | collective-permute-start | bytes 1769480 | tf_op jit(solution)/shard_map/ppermute | solution.py:388
  67.0 25.5 %collective-permute-start.11 = (bf16[2,3,320,128]{3,2,1,0:T(8,128)(2,1)S(1)}, bf16[2,3,320,128]{3,2,1,0:T(8,128)(2,1)S(1)}, u32[]{:S(2)}, u32[]{:S(2)}) collective-permute-start(bf16[2,3,320,128]{3,2,1,0:T(8,128)(2,1)S(1)} %get-tuple-element.81), channel_id=1, source_target_pairs={{0,4},{1,5},{2,6},{3,7},{4,8},{5,9},{6,10},{7,11},{8,12},{9,13},{1... | collective-permute-start | bytes 1474568 | tf_op jit(solution)/shard_map/ppermute | solution.py:363
  71.5 21.1 %collective-permute-start.12 = (bf16[2,3,320,128]{3,2,1,0:T(8,128)(2,1)S(1)}, bf16[2,3,320,128]{3,2,1,0:T(8,128)(2,1)S(1)}, u32[]{:S(2)}, u32[]{:S(2)}) collective-permute-start(bf16[2,3,320,128]{3,2,1,0:T(8,128)(2,1)S(1)} %get-tuple-element.82), channel_id=1, source_target_pairs={{4,0},{5,1},{6,2},{7,3},{8,4},{9,5},{10,6},{11,7},{12,8},{13,9},{1... | collective-permute-start | bytes 1474568 | tf_op jit(solution)/shard_map/ppermute | solution.py:363
  73.1 18.6 %collective-permute-start.10 = (bf16[96,1536]{1,0:T(8,128)(2,1)S(1)}, bf16[96,1536]{1,0:T(8,128)(2,1)S(1)}, u32[]{:S(2)}, u32[]{:S(2)}) collective-permute-start(bf16[96,1536]{1,0:T(8,128)(2,1)S(1)} %get-tuple-element.78), channel_id=1, source_target_pairs={{0,4},{1,5},{2,6},{3,7},{4,0},{5,1},{6,2},{7,3},{8,12},{9,13},{10,... | collective-permute-start | bytes 884744 | tf_op jit(solution)/shard_map/ppermute | solution.py:388
  94.2 10.1 %collective-permute-start.13 = (bf16[960,128]{1,0:T(8,128)(2,1)S(1)}, bf16[960,128]{1,0:T(8,128)(2,1)S(1)}, u32[]{:S(2)}, u32[]{:S(2)}) collective-permute-start(bf16[960,128]{1,0:T(8,128)(2,1)S(1)} %get-tuple-element.84), channel_id=1, source_target_pairs={{0,3},{1,2},{2,1},{3,0},{4,7},{5,6},{6,5},{7,4},{8,11},{9,10},{10,... | collective-permute-start | bytes 737288 | tf_op jit(solution)/shard_map/ppermute | solution.py:358
  94.2 10.8 %collective-permute-start.14 = (bf16[1,3,320,128]{3,2,1,0:T(8,128)(2,1)S(1)}, bf16[1,3,320,128]{3,2,1,0:T(8,128)(2,1)S(1)}, u32[]{:S(2)}, u32[]{:S(2)}) collective-permute-start(bf16[1,3,320,128]{3,2,1,0:T(8,128)(2,1)S(1)} %get-tuple-element.86), channel_id=1, source_target_pairs={{0,4},{1,5},{2,6},{3,7},{4,8},{5,9},{6,10},{7,11},{8,12},{9,13},{1... | collective-permute-start | bytes 737288 | tf_op jit(solution)/shard_map/ppermute | solution.py:363
  95.7 12.5 %collective-permute-start.15 = (bf16[1,3,320,128]{3,2,1,0:T(8,128)(2,1)S(1)}, bf16[1,3,320,128]{3,2,1,0:T(8,128)(2,1)S(1)}, u32[]{:S(2)}, u32[]{:S(2)}) collective-permute-start(bf16[1,3,320,128]{3,2,1,0:T(8,128)(2,1)S(1)} %get-tuple-element.87), channel_id=1, source_target_pairs={{4,0},{5,1},{6,2},{7,3},{8,4},{9,5},{10,6},{11,7},{12,8},{13,9},{1... | collective-permute-start | bytes 737288 | tf_op jit(solution)/shard_map/ppermute | solution.py:363
  97.0 19.2 %collective-permute-start.16 = (bf16[48,1536]{1,0:T(8,128)(2,1)S(1)}, bf16[48,1536]{1,0:T(8,128)(2,1)S(1)}, u32[]{:S(2)}, u32[]{:S(2)}) collective-permute-start(bf16[48,1536]{1,0:T(8,128)(2,1)S(1)} %get-tuple-element.91), channel_id=1, source_target_pairs={{0,8},{1,9},{2,10},{3,11},{4,12},{5,13},{6,14},{7,15},{8,0},{9,1},... | collective-permute-start | bytes 442376 | tf_op jit(solution)/shard_map/ppermute | solution.py:388
  103.5 14.7 %collective-permute-start.17 = (bf16[960,128]{1,0:T(8,128)(2,1)S(1)}, bf16[960,128]{1,0:T(8,128)(2,1)S(1)}, u32[]{:S(2)}, u32[]{:S(2)}) collective-permute-start(bf16[960,128]{1,0:T(8,128)(2,1)S(1)} %get-tuple-element.94), channel_id=1, source_target_pairs={{0,1},{1,0},{2,3},{3,2},{4,5},{5,4},{6,7},{7,6},{8,9},{9,8},{10,11... | collective-permute-start | bytes 737288 | tf_op jit(solution)/shard_map/ppermute | solution.py:358
  104.3 14.0 %collective-permute-start.18 = (bf16[960,128]{1,0:T(8,128)(2,1)S(1)}, bf16[960,128]{1,0:T(8,128)(2,1)S(1)}, u32[]{:S(2)}, u32[]{:S(2)}) collective-permute-start(bf16[960,128]{1,0:T(8,128)(2,1)S(1)} %get-tuple-element.95), channel_id=1, source_target_pairs={{0,2},{1,3},{2,0},{3,1},{4,6},{5,7},{6,4},{7,5},{8,10},{9,11},{10,... | collective-permute-start | bytes 737288 | tf_op jit(solution)/shard_map/ppermute | solution.py:358
  109.1 9.2 %collective-permute-start.19 = (bf16[480,128]{1,0:T(8,128)(2,1)S(1)}, bf16[480,128]{1,0:T(8,128)(2,1)S(1)}, u32[]{:S(2)}, u32[]{:S(2)}) collective-permute-start(bf16[480,128]{1,0:T(8,128)(2,1)S(1)} %get-tuple-element.96), channel_id=1, source_target_pairs={{0,1},{1,0},{2,3},{3,2},{4,5},{5,4},{6,7},{7,6},{8,9},{9,8},{10,11... | collective-permute-start | bytes 368648 | tf_op jit(solution)/shard_map/ppermute | solution.py:358
  109.8 8.4 %collective-permute-start.20 = (bf16[480,128]{1,0:T(8,128)(2,1)S(1)}, bf16[480,128]{1,0:T(8,128)(2,1)S(1)}, u32[]{:S(2)}, u32[]{:S(2)}) collective-permute-start(bf16[480,128]{1,0:T(8,128)(2,1)S(1)} %get-tuple-element.97), channel_id=1, source_target_pairs={{0,2},{1,3},{2,0},{3,1},{4,6},{5,7},{6,4},{7,5},{8,10},{9,11},{10,... | collective-permute-start | bytes 368648 | tf_op jit(solution)/shard_map/ppermute | solution.py:358
  116.2 5.3 %collective-permute-start.21 = (bf16[480,128]{1,0:T(8,128)(2,1)S(1)}, bf16[480,128]{1,0:T(8,128)(2,1)S(1)}, u32[]{:S(2)}, u32[]{:S(2)}) collective-permute-start(bf16[480,128]{1,0:T(8,128)(2,1)S(1)} %get-tuple-element.98), channel_id=1, source_target_pairs={{0,3},{1,2},{2,1},{3,0},{4,7},{5,6},{6,5},{7,4},{8,11},{9,10},{10,... | collective-permute-start | bytes 368648 | tf_op jit(solution)/shard_map/ppermute | solution.py:358
  (13 other events, 47.9 us)

commit v4 on v3

--- a/solution.py
+++ b/solution.py
@@ -20,7 +20,7 @@
 VMEM_SPEC = pl.BlockSpec(memory_space=pltpu.VMEM)
 SMEM_SPEC = pl.BlockSpec(memory_space=pltpu.SMEM)
 ANY_SPEC = pl.BlockSpec(memory_space=pl.ANY)
-PARAMS = pltpu.CompilerParams(vmem_limit_bytes=40 * 1024 * 1024)
+PARAMS = pltpu.CompilerParams(vmem_limit_bytes=28 * 1024 * 1024)
 
 
 MICROS = {
@@ -449,7 +449,6 @@
     chunks = GROUP * tokens // CHUNK
     results = []
     head = 0
-    ready = []
     above = shift(borders[0], GROUP)
     below = shift(borders[1], -GROUP)
     for number in groups:
@@ -492,13 +491,8 @@
             kept, sent = fold(folds, kept, sent, result[2])
             folds += 1
 
-    if halving:
-        while folds < bits - 1:
-            kept, sent = fold(folds, kept, sent, results[-1][2])
-            folds += 1
-        ready = [kept]
     returned = []
-    turn = after(me_arr, results[-1][2], *ready)
+    turn = after(me_arr, results[-1][2])
     for number, (to_above, to_below, own, dq) in zip(groups, results):
         size = (number * (tokens + half), LANES)
         pieces = kernel_call(
@@ -512,7 +506,10 @@
             micros=MICROS["sum"],
         )(turn, own, shift(to_below, GROUP), shift(to_above, -GROUP), dq)
         returned += exchange(pieces)
-        turn = after(me_arr, returned[3])
+        while halving and folds < bits - 1:
+            kept, sent = fold(folds, kept, sent, pieces[0])
+            folds += 1
+        turn = after(me_arr, returned[3], *([kept] if halving else []))
 
     if halving:
         grad_w_out = kernel_call(
@@ -522,7 +519,7 @@
             out_specs=VMEM_SPEC,
             name="last",
             micros=MICROS["last"],
-        )(after(kept, pieces[0]), hop(sent, bits - 1))
+        )(kept, hop(sent, bits - 1))
     else:
         grad_w_out = lax.psum_scatter(
             lax.dot_general(o2, g2, (((0,), (0,)), ((), ())), preferred_element_type=jnp.float32),
@@ -542,7 +539,7 @@
         compiler_params=PARAMS,
         name="unpack",
             micros=MICROS["unpack"],
-    )(after(me_arr, grad_w_out), *[near(x) for x in returned])
+    )(me_arr, *[near(x) for x in returned])
     grads = [x.reshape(queries.shape) for x in grads]
     return (*grads, grad_w_out)
 

time: 123 us -> 120 us (0.976)
  starting transfers between devices: 35.3 us -> 31.6 us
    ppermute x4, waiting for transfers between devices: 8.54 us -> 3.15 us  [hop(): lax.ppermute(sent, 'row', [(i, i ^ 1 << bit) for i in range(count)])]
    ppermute x4, starting transfers between devices: 11.1 us -> 6.29 us  [hop(): lax.ppermute(sent, 'row', [(i, i ^ 1 << bit) for i in range(count)])]
    ppermute x12, waiting for transfers between devices: 16.2 us -> 19.5 us  [exchange(): result.append(near(lax.ppermute(pieces[slot], 'row', pairs)))]
    ppermute x6, waiting for transfers between devices: 4.2 us -> 7.01 us  [shift(): return near(lax.ppermute(value, 'row', pairs))]
  transfers between devices with their start and end apart: 22 -> 22, of which waited for: 8 -> 10; matrix products, arithmetic and copies ran while one was open for 0% -> 0% of each run, Pallas kernels for 39% -> 41%
where the time goes in v4:
time: 120 us; the launch traced here: 119 us
  Pallas kernels  53.6 us (45%)
  starting transfers between devices  31.6 us (26%)
  waiting for transfers between devices  29.6 us (25%)
  local copies, waits for them, and re-layouts  3.35 us (3%)
    pallas_call x2, Pallas kernels, body(): kernel_call(functools.partial(attention_kernel, per, cols, head), grid=(n...  36.8 us
    ppermute x12, waiting for transfers between devices, exchange(): result.append(near(lax.ppermute(pieces[slot], 'row', pairs)))  19.5 us
    ppermute x6, starting transfers between devices, shift(): return near(lax.ppermute(value, 'row', pairs))  15.9 us
    ppermute x12, starting transfers between devices, exchange(): result.append(near(lax.ppermute(pieces[slot], 'row', pairs)))  9.33 us
    ppermute x6, waiting for transfers between devices, shift(): return near(lax.ppermute(value, 'row', pairs))  7.01 us
    pallas_call x1, Pallas kernels, body(): kernel_call(functools.partial(pack_qd_kernel, heads, count if halving els...  6.91 us
    ppermute x4, starting transfers between devices, hop(): lax.ppermute(sent, 'row', [(i, i ^ 1 << bit) for i in range(count)])  6.29 us
    ppermute x4, waiting for transfers between devices, hop(): lax.ppermute(sent, 'row', [(i, i ^ 1 << bit) for i in range(count)])  3.15 us
  transfers between devices with their start and end apart: 22, of which 10 were waited for; matrix products, arithmetic and copies ran while one was open for 0% of the time, Pallas kernels for 41%

profile of v4, /device:TPU:0, one launch (start us, length us, event | category | flops | bytes accessed | tf_op | source)
XLA Modules:
  0.0 119.3 jit_solution(12130599425996055884)
XLA Ops:
  0.7 1.0 copy-done.3
  1.7 1.0 copy-done.4
  2.7 1.7 %pack_kv.1 = (bf16[3,320,128]{2,1,0:T(8,128)(2,1)S(1)}, bf16[3,320,128]{2,1,0:T(8,128)(2,1)S(1)}, bf16[3,320,128]{2,1,0:T(8,128)(2,1)S(1)}, bf16[3,320,128]{2,1,0:T(8,128)(2,1)S(1)}) custom-call(s32[1]{0:T(128)} %bitcast.me_ref, bf16[320,768]{1,0:T(8,128)(2,1)S(1)} %bitcast.13, bf16[320,768]{1,0:T(8,128)(2,1)S(1)} %bitcast.14), custom_call_target="tpu_custom_call" | custom-call | flops 2750000128 | tf_op jit(solution)/shard_map/pack_kv/pallas_call | solution.py:369
  5.0 2.6 %collective-permute-start.1 = (bf16[3,320,128]{2,1,0:T(8,128)(2,1)S(1)}, bf16[3,320,128]{2,1,0:T(8,128)(2,1)S(1)}, u32[]{:S(2)}, u32[]{:S(2)}) collective-permute-start(bf16[3,320,128]{2,1,0:T(8,128)(2,1)S(1)} %get-tuple-element.56), channel_id=1, source_target_pairs={{0,2},{1,3},{2,0},{3,1},{4,6},{5,7},{6,4},{7,5},{8,10},{9,11},{10,... | collective-permute-start | bytes 737288 | tf_op jit(solution)/shard_map/ppermute | solution.py:358
  7.7 6.9 %pack_qd.1 = (bf16[1008,128]{1,0:T(8,128)(2,1)S(1)}, bf16[1008,128]{1,0:T(8,128)(2,1)S(1)}, bf16[1008,128]{1,0:T(8,128)(2,1)S(1)}, bf16[1008,128]{1,0:T(8,128)(2...) custom-call(s32[2]{0:T(128)S(1)} %pad_add_fusion.1.me_ref, bf16[320,768]{1,0:T(8,128)(2,1)S(1)} %bitcast.15, ...), custom_call_target="tpu_custom_call" | custom-call | flops 12099999744 | tf_op jit(solution)/shard_map/pack_qd/pallas_call | solution.py:407
  14.7 4.4 %collective-permute-done.2.refs_3_ = bf16[3,320,128]{2,1,0:T(8,128)(2,1)S(1)} collective-permute-done((bf16[3,320,128]{2,1,0:T(8,128)(2,1)S(1)}, bf16[3,320,128]{2,1,0:T(8,128)(2,1)S(1)}, u32[]{:S(2)}, u32[]{:S(2)}) %collective-permute-start.2) | collective-permute-done | bytes 245792 | tf_op jit(solution)/shard_map/ppermute | solution.py:358
  19.1 1.3 %halo.1 = (bf16[3,3,320,128]{3,2,1,0:T(8,128)(2,1)}, bf16[3,3,320,128]{3,2,1,0:T(8,128)(2,1)}) custom-call(s32[1]{0:T(128)} %bitcast.me_ref, bf16[3,320,128]{2,1,0:T(8,128)(2,1)S(1)} %get-tuple-element.55.refs_0_, bf16[3,320,128]{2,1,0:T(8,128)(2,1)S(1)} %collective-permute-done.refs_1_, bf16[3,320,128]{2,1,0:T(8,128)(2,1)S(1)} %collective-permute-done.1.refs_2_, ...), custom_call_target="tpu_custom_call" | custom-call | flops 2750000128 | tf_op jit(solution)/shard_map/halo/pallas_call | solution.py:431
  20.6 1.3 %collective-permute-start.5 = (bf16[3,3,320,128]{3,2,1,0:T(8,128)(2,1)}, bf16[3,3,320,128]{3,2,1,0:T(8,128)(2,1)}, u32[]{:S(2)}, u32[]{:S(2)}) collective-permute-start(bf16[3,3,320,128]{3,2,1,0:T(8,128)(2,1)} %get-tuple-element.65), channel_id=1, source_target_pairs={{4,0},{5,1},{6,2},{7,3},{8,4},{9,5},{10,6},{11,7},{12,8},{13,9},{1... | collective-permute-start | bytes 2211848 | tf_op jit(solution)/shard_map/ppermute | solution.py:363
  21.9 5.5 %collective-permute-start.4 = (bf16[3,3,320,128]{3,2,1,0:T(8,128)(2,1)}, bf16[3,3,320,128]{3,2,1,0:T(8,128)(2,1)}, u32[]{:S(2)}, u32[]{:S(2)}) collective-permute-start(bf16[3,3,320,128]{3,2,1,0:T(8,128)(2,1)} %get-tuple-element.58), channel_id=1, source_target_pairs={{0,4},{1,5},{2,6},{3,7},{4,8},{5,9},{6,10},{7,11},{8,12},{9,13},{1... | collective-permute-start | bytes 2211848 | tf_op jit(solution)/shard_map/ppermute | solution.py:363
  27.7 1.8 %collective-permute-start.7 = (bf16[1008,128]{1,0:T(8,128)(2,1)}, bf16[1008,128]{1,0:T(8,128)(2,1)S(1)}, u32[]{:S(2)}, u32[]{:S(2)}) collective-permute-start(bf16[1008,128]{1,0:T(8,128)(2,1)} %copy-done.9), channel_id=1, source_target_pairs={{0,2},{1,3},{2,0},{3,1},{4,6},{5,7},{6,4},{7,5},{8,10},{9,11},{10,... | collective-permute-start | bytes 774152 | tf_op jit(solution)/shard_map/ppermute | solution.py:358
  31.5 5.4 %collective-permute-done.7.refs_8_ = bf16[1008,128]{1,0:T(8,128)(2,1)S(1)} collective-permute-done((bf16[1008,128]{1,0:T(8,128)(2,1)}, bf16[1008,128]{1,0:T(8,128)(2,1)S(1)}, u32[]{:S(2)}, u32[]{:S(2)}) %collective-permute-start.7) | collective-permute-done | bytes 258080 | tf_op jit(solution)/shard_map/ppermute | solution.py:358
  36.9 1.7 %collective-permute-start.9 = (bf16[192,1536]{1,0:T(8,128)(2,1)S(1)}, bf16[192,1536]{1,0:T(8,128)(2,1)S(1)}, u32[]{:S(2)}, u32[]{:S(2)}) collective-permute-start(bf16[192,1536]{1,0:T(8,128)(2,1)S(1)} %get-tuple-element.71), channel_id=1, source_target_pairs={{0,2},{1,3},{2,0},{3,1},{4,6},{5,7},{6,4},{7,5},{8,10},{9,11},{10,... | collective-permute-start | bytes 1769480 | tf_op jit(solution)/shard_map/ppermute | solution.py:388
  38.6 3.2 %collective-permute-done.8.refs_9_ = bf16[1008,128]{1,0:T(8,128)(2,1)S(1)} collective-permute-done((bf16[1008,128]{1,0:T(8,128)(2,1)}, bf16[1008,128]{1,0:T(8,128)(2,1)S(1)}, u32[]{:S(2)}, u32[]{:S(2)}) %collective-permute-start.8) | collective-permute-done | bytes 258080 | tf_op jit(solution)/shard_map/ppermute | solution.py:358
  41.8 1.0 collective-permute-done.4.refs_4_
  42.8 24.2 %attention.2 = (bf16[2,3,320,128]{3,2,1,0:T(8,128)(2,1)S(1)}, bf16[2,3,320,128]{3,2,1,0:T(8,128)(2,1)S(1)}, f32[2,4,320,128]{3,2,1,0:T(8,128)S(1)}, bf16[2,4,160,128]{3,2,1,0:T(8,128)(2,1)S(1)}) custom-call(s32[10]{0:T(128)S(1)} %pad_add_fusion.scalars, bf16[3,320,128]{2,1,0:T(8,128)(2,1)S(1)} %copy-done.20, bf16[3,320,128]{2,1,0:T(8,128)(2,1)S(1)} %copy-done.11, ...), custom_call_target="tpu_custom_call" | custom-call | flops 30799998976 | tf_op jit(solution)/shard_map/attention/pallas_call | solution.py:458
  67.0 4.4 %collective-permute-start.10 = (bf16[2,3,320,128]{3,2,1,0:T(8,128)(2,1)S(1)}, bf16[2,3,320,128]{3,2,1,0:T(8,128)(2,1)S(1)}, u32[]{:S(2)}, u32[]{:S(2)}) collective-permute-start(bf16[2,3,320,128]{3,2,1,0:T(8,128)(2,1)S(1)} %get-tuple-element.76), channel_id=1, source_target_pairs={{0,4},{1,5},{2,6},{3,7},{4,8},{5,9},{6,10},{7,11},{8,12},{9,13},{1... | collective-permute-start | bytes 1474568 | tf_op jit(solution)/shard_map/ppermute | solution.py:363
  71.5 1.5 %collective-permute-start.11 = (bf16[2,3,320,128]{3,2,1,0:T(8,128)(2,1)S(1)}, bf16[2,3,320,128]{3,2,1,0:T(8,128)(2,1)S(1)}, u32[]{:S(2)}, u32[]{:S(2)}) collective-permute-start(bf16[2,3,320,128]{3,2,1,0:T(8,128)(2,1)S(1)} %get-tuple-element.77), channel_id=1, source_target_pairs={{4,0},{5,1},{6,2},{7,3},{8,4},{9,5},{10,6},{11,7},{12,8},{13,9},{1... | collective-permute-start | bytes 1474568 | tf_op jit(solution)/shard_map/ppermute | solution.py:363
  73.1 12.6 %attention.3 = (bf16[1,3,320,128]{3,2,1,0:T(8,128)(2,1)S(1)}, bf16[1,3,320,128]{3,2,1,0:T(8,128)(2,1)S(1)}, f32[1,4,320,128]{3,2,1,0:T(8,128)S(1)}, bf16[1,4,160,128]{3,2,1,0:T(8,128)(2,1)S(1)}) custom-call(s32[10]{0:T(128)S(1)} %pad_add_fusion.scalars, bf16[3,320,128]{2,1,0:T(8,128)(2,1)S(1)} %copy-done.20, bf16[3,320,128]{2,1,0:T(8,128)(2,1)S(1)} %copy-done.11, ...), custom_call_target="tpu_custom_call" | custom-call | flops 15399999488 | tf_op jit(solution)/shard_map/attention/pallas_call | solution.py:458
  85.8 2.7 %collective-permute-start.15 = (bf16[96,1536]{1,0:T(8,128)(2,1)S(1)}, bf16[96,1536]{1,0:T(8,128)(2,1)S(1)}, u32[]{:S(2)}, u32[]{:S(2)}) collective-permute-start(bf16[96,1536]{1,0:T(8,128)(2,1)S(1)} %get-tuple-element.84), channel_id=1, source_target_pairs={{0,4},{1,5},{2,6},{3,7},{4,0},{5,1},{6,2},{7,3},{8,12},{9,13},{10,... | collective-permute-start | bytes 884744 | tf_op jit(solution)/shard_map/ppermute | solution.py:388
  88.5 1.6 %sum.2 = (bf16[960,128]{1,0:T(8,128)(2,1)S(1)}, bf16[960,128]{1,0:T(8,128)(2,1)S(1)}, bf16[960,128]{1,0:T(8,128)(2,1)S(1)}, bf16[960,128]{1,0:T(8,128)(2,1)S(1)}) custom-call(s32[1]{0:T(128)} %bitcast.me_ref, f32[2,4,320,128]{3,2,1,0:T(8,128)S(1)} %get-tuple-element.69.own_ref, bf16[2,3,320,128]{3,2,1,0:T(8,128)(2,1)S(1)} %collective-permute-done.10.above_ref, ...), custom_call_target="tpu_custom_call" | custom-call | flops 2750000128 | tf_op jit(solution)/shard_map/sum/pallas_call | solution.py:498
  90.2 2.0 %collective-permute-start.16 = (bf16[1,3,320,128]{3,2,1,0:T(8,128)(2,1)S(1)}, bf16[1,3,320,128]{3,2,1,0:T(8,128)(2,1)S(1)}, u32[]{:S(2)}, u32[]{:S(2)}) collective-permute-start(bf16[1,3,320,128]{3,2,1,0:T(8,128)(2,1)S(1)} %get-tuple-element.87), channel_id=1, source_target_pairs={{0,4},{1,5},{2,6},{3,7},{4,8},{5,9},{6,10},{7,11},{8,12},{9,13},{1... | collective-permute-start | bytes 737288 | tf_op jit(solution)/shard_map/ppermute | solution.py:363
  92.1 1.3 %collective-permute-start.17 = (bf16[1,3,320,128]{3,2,1,0:T(8,128)(2,1)S(1)}, bf16[1,3,320,128]{3,2,1,0:T(8,128)(2,1)S(1)}, u32[]{:S(2)}, u32[]{:S(2)}) collective-permute-start(bf16[1,3,320,128]{3,2,1,0:T(8,128)(2,1)S(1)} %get-tuple-element.88), channel_id=1, source_target_pairs={{4,0},{5,1},{6,2},{7,3},{8,4},{9,5},{10,6},{11,7},{12,8},{13,9},{1... | collective-permute-start | bytes 737288 | tf_op jit(solution)/shard_map/ppermute | solution.py:363
  93.4 1.4 %collective-permute-start.12 = (bf16[960,128]{1,0:T(8,128)(2,1)S(1)}, bf16[960,128]{1,0:T(8,128)(2,1)S(1)}, u32[]{:S(2)}, u32[]{:S(2)}) collective-permute-start(bf16[960,128]{1,0:T(8,128)(2,1)S(1)} %get-tuple-element.80), channel_id=1, source_target_pairs={{0,1},{1,0},{2,3},{3,2},{4,5},{5,4},{6,7},{7,6},{8,9},{9,8},{10,11... | collective-permute-start | bytes 737288 | tf_op jit(solution)/shard_map/ppermute | solution.py:358
  95.8 2.5 %collective-permute-done.14.refs_3_ = bf16[960,128]{1,0:T(8,128)(2,1)S(1)} collective-permute-done((bf16[960,128]{1,0:T(8,128)(2,1)S(1)}, bf16[960,128]{1,0:T(8,128)(2,1)S(1)}, u32[]{:S(2)}, u32[]{:S(2)}) %collective-permute-start.14) | collective-permute-done | bytes 245792 | tf_op jit(solution)/shard_map/ppermute | solution.py:358
  98.5 5.8 %collective-permute-done.17.below_ref = bf16[1,3,320,128]{3,2,1,0:T(8,128)(2,1)S(1)} collective-permute-done((bf16[1,3,320,128]{3,2,1,0:T(8,128)(2,1)S(1)}, bf16[1,3,320,128]{3,2,1,0:T(8,128)(2,1)S(1)}, u32[]{:S(2)}, u32[]{:S(2)}) %collective-permute-start.17) | collective-permute-done | bytes 245792 | tf_op jit(solution)/shard_map/ppermute | solution.py:363
  105.7 1.4 %collective-permute-start.19 = (bf16[480,128]{1,0:T(8,128)(2,1)S(1)}, bf16[480,128]{1,0:T(8,128)(2,1)S(1)}, u32[]{:S(2)}, u32[]{:S(2)}) collective-permute-start(bf16[480,128]{1,0:T(8,128)(2,1)S(1)} %get-tuple-element.92), channel_id=1, source_target_pairs={{0,2},{1,3},{2,0},{3,1},{4,6},{5,7},{6,4},{7,5},{8,10},{9,11},{10,... | collective-permute-start | bytes 368648 | tf_op jit(solution)/shard_map/ppermute | solution.py:358
  107.2 1.7 %collective-permute-start.21 = (bf16[48,1536]{1,0:T(8,128)(2,1)S(1)}, bf16[48,1536]{1,0:T(8,128)(2,1)S(1)}, u32[]{:S(2)}, u32[]{:S(2)}) collective-permute-start(bf16[48,1536]{1,0:T(8,128)(2,1)S(1)} %get-tuple-element.97), channel_id=1, source_target_pairs={{0,8},{1,9},{2,10},{3,11},{4,12},{5,13},{6,14},{7,15},{8,0},{9,1},... | collective-permute-start | bytes 442376 | tf_op jit(solution)/shard_map/ppermute | solution.py:388
  108.9 3.0 %collective-permute-done.19.refs_6_ = bf16[480,128]{1,0:T(8,128)(2,1)S(1)} collective-permute-done((bf16[480,128]{1,0:T(8,128)(2,1)S(1)}, bf16[480,128]{1,0:T(8,128)(2,1)S(1)}, u32[]{:S(2)}, u32[]{:S(2)}) %collective-permute-start.19) | collective-permute-done | bytes 122912 | tf_op jit(solution)/shard_map/ppermute | solution.py:358
  111.8 1.1 collective-permute-done.20.refs_7_
  112.9 1.6 %unpack.1 = (bf16[320,768]{1,0:T(8,128)(2,1)}, bf16[320,768]{1,0:T(8,128)(2,1)}, bf16[320,768]{1,0:T(8,128)(2,1)}) custom-call(s32[1]{0:T(128)} %bitcast.me_ref, bf16[960,128]{1,0:T(8,128)(2,1)S(1)} %get-tuple-element.79.refs_0_, bf16[960,128]{1,0:T(8,128)(2,1)S(1)} %collective-permute-done.12.refs_1_, bf16[960,128]{1,0:T(8,128)(2,1)S(1)} %collective-permute-done.13.refs_2_, ...), custom_call_target="tpu_custom_call" | custom-call | flops 3300000000 | tf_op jit(solution)/shard_map/unpack/pallas_call | solution.py:531
  114.5 3.1 %collective-permute-done.21.received_ref = bf16[48,1536]{1,0:T(8,128)(2,1)S(1)} collective-permute-done((bf16[48,1536]{1,0:T(8,128)(2,1)S(1)}, bf16[48,1536]{1,0:T(8,128)(2,1)S(1)}, u32[]{:S(2)}, u32[]{:S(2)}) %collective-permute-start.21) | collective-permute-done | bytes 147488 | tf_op jit(solution)/shard_map/ppermute | solution.py:388
  117.6 1.7 %last.1 = f32[48,1536]{1,0:T(8,128)} custom-call(f32[48,1536]{1,0:T(8,128)} %copy-done.18, bf16[48,1536]{1,0:T(8,128)(2,1)S(1)} %collective-permute-done.21.received_ref), custom_call_target="tpu_custom_call" | custom-call | flops 2200000000 | tf_op jit(solution)/shard_map/last/pallas_call | solution.py:515
  (75 shorter events, 6.0 us)
Async XLA Ops:
  0.6 26.8 %copy-start = (s32[16,2]{0,1:T(2,128)S(1)}, s32[16,2]{0,1:T(2,128)}, u32[]{:S(2)}) copy-start(s32[16,2]{0,1:T(2,128)} %param.13) | copy-start | bytes 388
  4.5 14.7 %copy-start.19 = (bf16[3,320,128]{2,1,0:T(8,128)(2,1)}, bf16[3,320,128]{2,1,0:T(8,128)(2,1)S(1)}, u32[]{:S(2)}) copy-start(bf16[3,320,128]{2,1,0:T(8,128)(2,1)S(1)} %get-tuple-element.55.refs_0_) | copy-start | bytes 737284
  4.5 3.3 %collective-permute-start = (bf16[3,320,128]{2,1,0:T(8,128)(2,1)S(1)}, bf16[3,320,128]{2,1,0:T(8,128)(2,1)S(1)}, u32[]{:S(2)}, u32[]{:S(2)}) collective-permute-start(bf16[3,320,128]{2,1,0:T(8,128)(2,1)S(1)} %get-tuple-element.51), channel_id=1, source_target_pairs={{0,1},{1,0},{2,3},{3,2},{4,5},{5,4},{6,7},{7,6},{8,9},{9,8},{10,11... | collective-permute-start | bytes 737288 | tf_op jit(solution)/shard_map/ppermute | solution.py:358
  5.0 9.8 %collective-permute-start.1 = (bf16[3,320,128]{2,1,0:T(8,128)(2,1)S(1)}, bf16[3,320,128]{2,1,0:T(8,128)(2,1)S(1)}, u32[]{:S(2)}, u32[]{:S(2)}) collective-permute-start(bf16[3,320,128]{2,1,0:T(8,128)(2,1)S(1)} %get-tuple-element.56), channel_id=1, source_target_pairs={{0,2},{1,3},{2,0},{3,1},{4,6},{5,7},{6,4},{7,5},{8,10},{9,11},{10,... | collective-permute-start | bytes 737288 | tf_op jit(solution)/shard_map/ppermute | solution.py:358
  7.6 11.6 %collective-permute-start.2 = (bf16[3,320,128]{2,1,0:T(8,128)(2,1)S(1)}, bf16[3,320,128]{2,1,0:T(8,128)(2,1)S(1)}, u32[]{:S(2)}, u32[]{:S(2)}) collective-permute-start(bf16[3,320,128]{2,1,0:T(8,128)(2,1)S(1)} %get-tuple-element.57), channel_id=1, source_target_pairs={{0,3},{1,2},{2,1},{3,0},{4,7},{5,6},{6,5},{7,4},{8,11},{9,10},{10,... | collective-permute-start | bytes 737288 | tf_op jit(solution)/shard_map/ppermute | solution.py:358
  7.7 11.4 %copy-start.10 = (bf16[3,320,128]{2,1,0:T(8,128)(2,1)}, bf16[3,320,128]{2,1,0:T(8,128)(2,1)S(1)}, u32[]{:S(2)}) copy-start(bf16[3,320,128]{2,1,0:T(8,128)(2,1)S(1)} %collective-permute-done.refs_1_) | copy-start | bytes 737284
  14.7 5.7 %copy-start.7 = (bf16[1008,128]{1,0:T(8,128)(2,1)}, bf16[1008,128]{1,0:T(8,128)(2,1)S(1)}, u32[]{:S(2)}) copy-start(bf16[1008,128]{1,0:T(8,128)(2,1)S(1)} %get-tuple-element.53) | copy-start | bytes 774148
  20.5 9.0 %collective-permute-start.3 = (bf16[384,1536]{1,0:T(8,128)(2,1)S(1)}, bf16[384,1536]{1,0:T(8,128)(2,1)S(1)}, u32[]{:S(2)}, u32[]{:S(2)}) collective-permute-start(bf16[384,1536]{1,0:T(8,128)(2,1)S(1)} %get-tuple-element.62), channel_id=1, source_target_pairs={{0,1},{1,0},{2,3},{3,2},{4,5},{5,4},{6,7},{7,6},{8,9},{9,8},{10,11... | collective-permute-start | bytes 3538952 | tf_op jit(solution)/shard_map/ppermute | solution.py:388
  20.6 21.2 %collective-permute-start.5 = (bf16[3,3,320,128]{3,2,1,0:T(8,128)(2,1)}, bf16[3,3,320,128]{3,2,1,0:T(8,128)(2,1)}, u32[]{:S(2)}, u32[]{:S(2)}) collective-permute-start(bf16[3,3,320,128]{3,2,1,0:T(8,128)(2,1)} %get-tuple-element.65), channel_id=1, source_target_pairs={{4,0},{5,1},{6,2},{7,3},{8,4},{9,5},{10,6},{11,7},{12,8},{13,9},{1... | collective-permute-start | bytes 2211848 | tf_op jit(solution)/shard_map/ppermute | solution.py:363
  21.9 20.9 %collective-permute-start.4 = (bf16[3,3,320,128]{3,2,1,0:T(8,128)(2,1)}, bf16[3,3,320,128]{3,2,1,0:T(8,128)(2,1)}, u32[]{:S(2)}, u32[]{:S(2)}) collective-permute-start(bf16[3,3,320,128]{3,2,1,0:T(8,128)(2,1)} %get-tuple-element.58), channel_id=1, source_target_pairs={{0,4},{1,5},{2,6},{3,7},{4,8},{5,9},{6,10},{7,11},{8,12},{9,13},{1... | collective-permute-start | bytes 2211848 | tf_op jit(solution)/shard_map/ppermute | solution.py:363
  27.7 14.1 %collective-permute-start.6 = (bf16[1008,128]{1,0:T(8,128)(2,1)}, bf16[1008,128]{1,0:T(8,128)(2,1)S(1)}, u32[]{:S(2)}, u32[]{:S(2)}) collective-permute-start(bf16[1008,128]{1,0:T(8,128)(2,1)} %copy-done.7), channel_id=1, source_target_pairs={{0,1},{1,0},{2,3},{3,2},{4,5},{5,4},{6,7},{7,6},{8,9},{9,8},{10,11... | collective-permute-start | bytes 774152 | tf_op jit(solution)/shard_map/ppermute | solution.py:358
  27.7 9.3 %collective-permute-start.7 = (bf16[1008,128]{1,0:T(8,128)(2,1)}, bf16[1008,128]{1,0:T(8,128)(2,1)S(1)}, u32[]{:S(2)}, u32[]{:S(2)}) collective-permute-start(bf16[1008,128]{1,0:T(8,128)(2,1)} %copy-done.9), channel_id=1, source_target_pairs={{0,2},{1,3},{2,0},{3,1},{4,6},{5,7},{6,4},{7,5},{8,10},{9,11},{10,... | collective-permute-start | bytes 774152 | tf_op jit(solution)/shard_map/ppermute | solution.py:358
  29.4 12.4 %collective-permute-start.8 = (bf16[1008,128]{1,0:T(8,128)(2,1)}, bf16[1008,128]{1,0:T(8,128)(2,1)S(1)}, u32[]{:S(2)}, u32[]{:S(2)}) collective-permute-start(bf16[1008,128]{1,0:T(8,128)(2,1)} %copy-done.8), channel_id=1, source_target_pairs={{0,3},{1,2},{2,1},{3,0},{4,7},{5,6},{6,5},{7,4},{8,11},{9,10},{10,... | collective-permute-start | bytes 774152 | tf_op jit(solution)/shard_map/ppermute | solution.py:358
  30.5 12.3 %copy-start.11 = (bf16[3,320,128]{2,1,0:T(8,128)(2,1)S(1)}, bf16[3,320,128]{2,1,0:T(8,128)(2,1)}, u32[]{:S(2)}) copy-start(bf16[3,320,128]{2,1,0:T(8,128)(2,1)} %copy-done.10) | copy-start | bytes 737284
  30.5 12.3 %copy-start.13 = (bf16[3,320,128]{2,1,0:T(8,128)(2,1)S(1)}, bf16[3,320,128]{2,1,0:T(8,128)(2,1)}, u32[]{:S(2)}) copy-start(bf16[3,320,128]{2,1,0:T(8,128)(2,1)} %copy-done.12) | copy-start | bytes 737284
  30.5 12.3 %copy-start.15 = (bf16[3,320,128]{2,1,0:T(8,128)(2,1)S(1)}, bf16[3,320,128]{2,1,0:T(8,128)(2,1)}, u32[]{:S(2)}) copy-start(bf16[3,320,128]{2,1,0:T(8,128)(2,1)} %copy-done.14) | copy-start | bytes 737284
  30.5 12.3 %copy-start.20 = (bf16[3,320,128]{2,1,0:T(8,128)(2,1)S(1)}, bf16[3,320,128]{2,1,0:T(8,128)(2,1)}, u32[]{:S(2)}) copy-start(bf16[3,320,128]{2,1,0:T(8,128)(2,1)} %copy-done.19) | copy-start | bytes 737284
  30.6 12.3 %copy-start.22 = (bf16[1008,128]{1,0:T(8,128)(2,1)S(1)}, bf16[1008,128]{1,0:T(8,128)(2,1)}, u32[]{:S(2)}) copy-start(bf16[1008,128]{1,0:T(8,128)(2,1)} %copy-done.21) | copy-start | bytes 774148
  36.9 36.0 %collective-permute-start.9 = (bf16[192,1536]{1,0:T(8,128)(2,1)S(1)}, bf16[192,1536]{1,0:T(8,128)(2,1)S(1)}, u32[]{:S(2)}, u32[]{:S(2)}) collective-permute-start(bf16[192,1536]{1,0:T(8,128)(2,1)S(1)} %get-tuple-element.71), channel_id=1, source_target_pairs={{0,2},{1,3},{2,0},{3,1},{4,6},{5,7},{6,4},{7,5},{8,10},{9,11},{10,... | collective-permute-start | bytes 1769480 | tf_op jit(solution)/shard_map/ppermute | solution.py:388
  67.0 21.4 %collective-permute-start.10 = (bf16[2,3,320,128]{3,2,1,0:T(8,128)(2,1)S(1)}, bf16[2,3,320,128]{3,2,1,0:T(8,128)(2,1)S(1)}, u32[]{:S(2)}, u32[]{:S(2)}) collective-permute-start(bf16[2,3,320,128]{3,2,1,0:T(8,128)(2,1)S(1)} %get-tuple-element.76), channel_id=1, source_target_pairs={{0,4},{1,5},{2,6},{3,7},{4,8},{5,9},{6,10},{7,11},{8,12},{9,13},{1... | collective-permute-start | bytes 1474568 | tf_op jit(solution)/shard_map/ppermute | solution.py:363
  71.5 17.0 %collective-permute-start.11 = (bf16[2,3,320,128]{3,2,1,0:T(8,128)(2,1)S(1)}, bf16[2,3,320,128]{3,2,1,0:T(8,128)(2,1)S(1)}, u32[]{:S(2)}, u32[]{:S(2)}) collective-permute-start(bf16[2,3,320,128]{3,2,1,0:T(8,128)(2,1)S(1)} %get-tuple-element.77), channel_id=1, source_target_pairs={{4,0},{5,1},{6,2},{7,3},{8,4},{9,5},{10,6},{11,7},{12,8},{13,9},{1... | collective-permute-start | bytes 1474568 | tf_op jit(solution)/shard_map/ppermute | solution.py:363
  85.8 9.1 %collective-permute-start.15 = (bf16[96,1536]{1,0:T(8,128)(2,1)S(1)}, bf16[96,1536]{1,0:T(8,128)(2,1)S(1)}, u32[]{:S(2)}, u32[]{:S(2)}) collective-permute-start(bf16[96,1536]{1,0:T(8,128)(2,1)S(1)} %get-tuple-element.84), channel_id=1, source_target_pairs={{0,4},{1,5},{2,6},{3,7},{4,0},{5,1},{6,2},{7,3},{8,12},{9,13},{10,... | collective-permute-start | bytes 884744 | tf_op jit(solution)/shard_map/ppermute | solution.py:388
  90.1 8.2 %collective-permute-start.14 = (bf16[960,128]{1,0:T(8,128)(2,1)S(1)}, bf16[960,128]{1,0:T(8,128)(2,1)S(1)}, u32[]{:S(2)}, u32[]{:S(2)}) collective-permute-start(bf16[960,128]{1,0:T(8,128)(2,1)S(1)} %get-tuple-element.82), channel_id=1, source_target_pairs={{0,3},{1,2},{2,1},{3,0},{4,7},{5,6},{6,5},{7,4},{8,11},{9,10},{10,... | collective-permute-start | bytes 737288 | tf_op jit(solution)/shard_map/ppermute | solution.py:358
  90.2 8.3 %collective-permute-start.16 = (bf16[1,3,320,128]{3,2,1,0:T(8,128)(2,1)S(1)}, bf16[1,3,320,128]{3,2,1,0:T(8,128)(2,1)S(1)}, u32[]{:S(2)}, u32[]{:S(2)}) collective-permute-start(bf16[1,3,320,128]{3,2,1,0:T(8,128)(2,1)S(1)} %get-tuple-element.87), channel_id=1, source_target_pairs={{0,4},{1,5},{2,6},{3,7},{4,8},{5,9},{6,10},{7,11},{8,12},{9,13},{1... | collective-permute-start | bytes 737288 | tf_op jit(solution)/shard_map/ppermute | solution.py:363
  92.1 12.2 %collective-permute-start.17 = (bf16[1,3,320,128]{3,2,1,0:T(8,128)(2,1)S(1)}, bf16[1,3,320,128]{3,2,1,0:T(8,128)(2,1)S(1)}, u32[]{:S(2)}, u32[]{:S(2)}) collective-permute-start(bf16[1,3,320,128]{3,2,1,0:T(8,128)(2,1)S(1)} %get-tuple-element.88), channel_id=1, source_target_pairs={{4,0},{5,1},{6,2},{7,3},{8,4},{9,5},{10,6},{11,7},{12,8},{13,9},{1... | collective-permute-start | bytes 737288 | tf_op jit(solution)/shard_map/ppermute | solution.py:363
  93.4 13.7 %collective-permute-start.12 = (bf16[960,128]{1,0:T(8,128)(2,1)S(1)}, bf16[960,128]{1,0:T(8,128)(2,1)S(1)}, u32[]{:S(2)}, u32[]{:S(2)}) collective-permute-start(bf16[960,128]{1,0:T(8,128)(2,1)S(1)} %get-tuple-element.80), channel_id=1, source_target_pairs={{0,1},{1,0},{2,3},{3,2},{4,5},{5,4},{6,7},{7,6},{8,9},{9,8},{10,11... | collective-permute-start | bytes 737288 | tf_op jit(solution)/shard_map/ppermute | solution.py:358
  94.9 14.0 %collective-permute-start.13 = (bf16[960,128]{1,0:T(8,128)(2,1)S(1)}, bf16[960,128]{1,0:T(8,128)(2,1)S(1)}, u32[]{:S(2)}, u32[]{:S(2)}) collective-permute-start(bf16[960,128]{1,0:T(8,128)(2,1)S(1)} %get-tuple-element.81), channel_id=1, source_target_pairs={{0,2},{1,3},{2,0},{3,1},{4,6},{5,7},{6,4},{7,5},{8,10},{9,11},{10,... | collective-permute-start | bytes 737288 | tf_op jit(solution)/shard_map/ppermute | solution.py:358
  95.8 9.4 %copy-start.18 = (f32[48,1536]{1,0:T(8,128)}, f32[48,1536]{1,0:T(8,128)S(1)}, u32[]{:S(2)}) copy-start(f32[48,1536]{1,0:T(8,128)S(1)} %get-tuple-element.85.kept_ref) | copy-start | bytes 884740
  105.2 3.7 %collective-permute-start.18 = (bf16[480,128]{1,0:T(8,128)(2,1)S(1)}, bf16[480,128]{1,0:T(8,128)(2,1)S(1)}, u32[]{:S(2)}, u32[]{:S(2)}) collective-permute-start(bf16[480,128]{1,0:T(8,128)(2,1)S(1)} %get-tuple-element.91), channel_id=1, source_target_pairs={{0,1},{1,0},{2,3},{3,2},{4,5},{5,4},{6,7},{7,6},{8,9},{9,8},{10,11... | collective-permute-start | bytes 368648 | tf_op jit(solution)/shard_map/ppermute | solution.py:358
  105.7 6.2 %collective-permute-start.19 = (bf16[480,128]{1,0:T(8,128)(2,1)S(1)}, bf16[480,128]{1,0:T(8,128)(2,1)S(1)}, u32[]{:S(2)}, u32[]{:S(2)}) collective-permute-start(bf16[480,128]{1,0:T(8,128)(2,1)S(1)} %get-tuple-element.92), channel_id=1, source_target_pairs={{0,2},{1,3},{2,0},{3,1},{4,6},{5,7},{6,4},{7,5},{8,10},{9,11},{10,... | collective-permute-start | bytes 368648 | tf_op jit(solution)/shard_map/ppermute | solution.py:358
  107.1 5.8 %collective-permute-start.20 = (bf16[480,128]{1,0:T(8,128)(2,1)S(1)}, bf16[480,128]{1,0:T(8,128)(2,1)S(1)}, u32[]{:S(2)}, u32[]{:S(2)}) collective-permute-start(bf16[480,128]{1,0:T(8,128)(2,1)S(1)} %get-tuple-element.93), channel_id=1, source_target_pairs={{0,3},{1,2},{2,1},{3,0},{4,7},{5,6},{6,5},{7,4},{8,11},{9,10},{10,... | collective-permute-start | bytes 368648 | tf_op jit(solution)/shard_map/ppermute | solution.py:358
  107.2 10.5 %collective-permute-start.21 = (bf16[48,1536]{1,0:T(8,128)(2,1)S(1)}, bf16[48,1536]{1,0:T(8,128)(2,1)S(1)}, u32[]{:S(2)}, u32[]{:S(2)}) collective-permute-start(bf16[48,1536]{1,0:T(8,128)(2,1)S(1)} %get-tuple-element.97), channel_id=1, source_target_pairs={{0,8},{1,9},{2,10},{3,11},{4,12},{5,13},{6,14},{7,15},{8,0},{9,1},... | collective-permute-start | bytes 442376 | tf_op jit(solution)/shard_map/ppermute | solution.py:388
  (13 other events, 52.9 us)
